TPU v7x, 32 devices: a whole 2x2x4 slice. The times are simulated.
32 devices in a mesh: section: 2 (over x), batch: 16 (over z, y, core).
Axes of the slice: x: 2, y: 2, z: 4, core: 2. Of those that a mesh axis runs over, the one named last changes fastest.
Arguments:
- clips: bfloat16 [32, 512, 768], P('batch'), may hold values from -30 to 30
- mask_flags: int32 [32, 512], P('batch'), may hold values from 0 to 1, as said below
- mask_embed: float32 [768], replicated, may hold values from -4 to 4
- pos_embed: float32 [512, 768], replicated, may hold values from -2.5 to 2.5
- first_gain: float32 [2, 768], P('section'), may hold values from 0.25 to 1.75
- first_shift: float32 [2, 768], P('section'), may hold values from -1.5 to 1.5
- joint_weight: bfloat16 [2, 768, 2304], P('section'), may hold values from -0.21875 to 0.21875
- query_bias: float32 [2, 768], P('section'), may hold values from -2.5 to 2.5
- value_bias: float32 [2, 768], P('section'), may hold values from -2.5 to 2.5
- mixer_weight: bfloat16 [2, 768, 768], P('section'), may hold values from -2.5 to 2.5
- mixer_bias: float32 [2, 768], P('section'), may hold values from -1.5 to 1.5
- second_gain: float32 [2, 768], P('section'), may hold values from 0.25 to 1.75
- second_shift: float32 [2, 768], P('section'), may hold values from -1.5 to 1.5
- up_weight: bfloat16 [2, 768, 3072], P('section'), may hold values from -0.21875 to 0.21875
- up_bias: float32 [2, 3072], P('section'), may hold values from -2.5 to 2.5
- down_weight: bfloat16 [2, 3072, 768], P('section'), may hold values from -0.109375 to 0.109375
- down_bias: float32 [2, 768], P('section'), may hold values from -1.5 to 1.5
- out_grad: bfloat16 [32, 512, 768], P('batch'), may hold values from -6 to 6
Outputs:
- layer_outputs: bfloat16 [2, 32, 512, 768], P('section', 'batch')
- input_grads: bfloat16 [2, 32, 512, 768], P('section', 'batch')
- grad_first_gain: float32 [2, 768], P('section', 'batch')
- grad_first_shift: float32 [2, 768], P('section', 'batch')
- grad_joint_weight: float32 [2, 768, 2304], P('section', 'batch')
- grad_query_bias: float32 [2, 768], P('section', 'batch')
- grad_value_bias: float32 [2, 768], P('section', 'batch')
- grad_mixer_weight: float32 [2, 768, 768], P('section', 'batch')
- grad_mixer_bias: float32 [2, 768], P('section', 'batch')
- grad_second_gain: float32 [2, 768], P('section', 'batch')
- grad_second_shift: float32 [2, 768], P('section', 'batch')
- grad_up_weight: float32 [2, 768, 3072], P('section', 'batch')
- grad_up_bias: float32 [2, 3072], P('section', 'batch')
- grad_down_weight: float32 [2, 3072, 768], P('section', 'batch')
- grad_down_bias: float32 [2, 768], P('section', 'batch')
- grad_mask_embed: float32 [768], P('section')
- grad_pos_embed: float32 [512, 768], P('section')
Inputs may be any that keep to these rules, and one draw needn't show every extreme that they name: `mask_flags`: every clip has exactly 400 patches set to 1.
All inputs are finite; a program needn't handle non-finite values.
Results may differ from a plain program's by a relative error of at most 0.012.
Values may be sent and summed in bfloat16 or wider, within the bound.
No kernel may reach another device: no remote copies, remote signals or barrier semaphores. Data moves between devices by JAX's collectives and lax.ppermute only.
A program may use at most 448 MiB of HBM per device.

v0:
```python
from functools import reduce

import jax
import jax.numpy as jnp
from jax import lax
from jax.sharding import PartitionSpec as P

D = 768
HEADS = 12
HD = 64
FF = 3072
L = 512
MB = 2
CLIP_MB = 1


def passed_along(block, axis, distance):
    devices = range(lax.axis_size(axis))
    route = [(i - distance, i) for i in devices if i - distance in devices]
    return lax.ppermute(block, axis, route)


def norm_rows(value, gain, shift):
    average = jnp.mean(value, axis=-1, keepdims=True)
    centered = value - average
    variance = jnp.mean(centered * centered, axis=-1, keepdims=True)
    return centered * lax.rsqrt(variance + 1e-06) * gain + shift


def gelu_exact(value):
    return jax.nn.gelu(value, approximate=False)


def contract_rows(left, right):
    return lax.dot_general(
        left, right, (((0,), (0,)), ((), ())), preferred_element_type=jnp.float32
    )


def contract_cols(left, right):
    return lax.dot_general(
        left, right, (((1,), (1,)), ((), ())), preferred_element_type=jnp.float32
    )


def column_sums(values):
    return jnp.sum(values, axis=0, dtype=jnp.float32)


def split_heads(values):
    return values.reshape(values.shape[0], HEADS, HD)


def add_tuples(left, right):
    return tuple((first_item + second_item for first_item, second_item in zip(left, right)))


def clip_scores(query, keys):
    raw = jnp.einsum(
        "qhc,khc->hqk", split_heads(query), split_heads(keys), preferred_element_type=jnp.float32
    )
    return raw * HD ** (-0.5)


def attend_clip(parts):
    query, keys, values = parts
    scores = clip_scores(query, keys)
    highest_score = jnp.max(scores, axis=-1, keepdims=True)
    log_total = highest_score + jnp.log(
        jnp.sum(jnp.exp(scores - highest_score), axis=-1, keepdims=True)
    )
    weights = jnp.exp(scores - log_total).astype(jnp.bfloat16)
    mixed = jnp.einsum(
        "hqk,khc->qhc", weights, split_heads(values), preferred_element_type=jnp.float32
    )
    return (mixed.reshape(query.shape[0], D).astype(jnp.bfloat16), log_total[..., 0])


def attend_clip_back(parts):
    query, keys, values, log_total, grad_mixed = parts
    weights = jnp.exp(clip_scores(query, keys) - log_total[..., None])
    grad_weights = jnp.einsum(
        "qhc,khc->hqk",
        split_heads(grad_mixed),
        split_heads(values),
        preferred_element_type=jnp.float32,
    )
    inner = jnp.sum(weights * grad_weights, axis=-1, keepdims=True)
    grad_scores = (weights * (grad_weights - inner)).astype(jnp.bfloat16)
    scale = HD ** (-0.5)
    grad_query = (
        jnp.einsum(
            "hqk,khc->qhc", grad_scores, split_heads(keys), preferred_element_type=jnp.float32
        )
        * scale
    )
    grad_keys = (
        jnp.einsum(
            "hqk,qhc->khc", grad_scores, split_heads(query), preferred_element_type=jnp.float32
        )
        * scale
    )
    grad_values = jnp.einsum(
        "hqk,qhc->khc",
        weights.astype(jnp.bfloat16),
        split_heads(grad_mixed),
        preferred_element_type=jnp.float32,
    )
    count = query.shape[0]
    joined = jnp.concatenate(
        [grad_query.reshape(count, D), grad_keys.reshape(count, D), grad_values.reshape(count, D)],
        axis=1,
    )
    return joined.astype(jnp.bfloat16)


def layer_forward(hidden, params):
    (
        first_gain,
        first_shift,
        joint_weight,
        query_bias,
        value_bias,
        mixer_weight,
        mixer_bias,
        second_gain,
        second_shift,
        up_weight,
        up_bias,
        down_weight,
        down_bias,
    ) = params
    clip_count = hidden.shape[0]
    shaped = (clip_count, L, D)
    rows = hidden.reshape(-1, D)
    normed = norm_rows(rows, first_gain, first_shift).astype(jnp.bfloat16)
    joint = jnp.dot(normed, joint_weight, preferred_element_type=jnp.float32)
    query = (joint[:, :D] + query_bias).astype(jnp.bfloat16)
    keys = joint[:, D : 2 * D].astype(jnp.bfloat16)
    values = (joint[:, 2 * D :] + value_bias).astype(jnp.bfloat16)
    mixed, log_total = lax.map(
        attend_clip, (query.reshape(shaped), keys.reshape(shaped), values.reshape(shaped))
    )
    mixed = mixed.reshape(-1, D)
    after = rows + (jnp.dot(mixed, mixer_weight, preferred_element_type=jnp.float32) + mixer_bias)
    normed_second = norm_rows(after, second_gain, second_shift).astype(jnp.bfloat16)
    lifted = jnp.dot(normed_second, up_weight, preferred_element_type=jnp.float32) + up_bias
    active = gelu_exact(lifted).astype(jnp.bfloat16)
    output = after + (jnp.dot(active, down_weight, preferred_element_type=jnp.float32) + down_bias)
    saved = (rows, query, keys, values, log_total, mixed, after, lifted)
    return (output.reshape(shaped).astype(jnp.bfloat16), saved)


def blank_forward(clip_count):
    count = clip_count * L
    zeros_float = jnp.zeros((count, D), jnp.float32)
    zeros_low = jnp.zeros((count, D), jnp.bfloat16)
    saved = (
        zeros_float,
        zeros_low,
        zeros_low,
        zeros_low,
        jnp.zeros((clip_count, HEADS, L), jnp.float32),
        zeros_low,
        zeros_float,
        jnp.zeros((count, FF), jnp.float32),
    )
    return (jnp.zeros((clip_count, L, D), jnp.bfloat16), saved)


def layer_backward(saved, grad_output, params):
    (
        first_gain,
        first_shift,
        joint_weight,
        query_bias,
        value_bias,
        mixer_weight,
        mixer_bias,
        second_gain,
        second_shift,
        up_weight,
        up_bias,
        down_weight,
        down_bias,
    ) = params
    rows, query, keys, values, log_total, mixed, after, lifted = saved
    clip_count = log_total.shape[0]
    shaped = (clip_count, L, D)
    grad_branch_two = grad_output.astype(jnp.bfloat16)
    active_full, gelu_pull = jax.vjp(gelu_exact, lifted)
    active = active_full.astype(jnp.bfloat16)
    grad_active = contract_cols(grad_branch_two, down_weight)
    grad_lifted = gelu_pull(grad_active)[0].astype(jnp.bfloat16)
    normed_full, second_pull = jax.vjp(norm_rows, after, second_gain, second_shift)
    normed_second = normed_full.astype(jnp.bfloat16)
    grad_after_part, grad_second_gain, grad_second_shift = second_pull(
        contract_cols(grad_lifted, up_weight)
    )
    grad_after = grad_output + grad_after_part
    grad_branch = grad_after.astype(jnp.bfloat16)
    grad_mixed = contract_cols(grad_branch, mixer_weight).astype(jnp.bfloat16)
    grad_joint = lax.map(
        attend_clip_back,
        (
            query.reshape(shaped),
            keys.reshape(shaped),
            values.reshape(shaped),
            log_total,
            grad_mixed.reshape(shaped),
        ),
    )
    grad_joint = grad_joint.reshape(-1, 3 * D)
    normed_first, first_pull = jax.vjp(norm_rows, rows, first_gain, first_shift)
    normed_low = normed_first.astype(jnp.bfloat16)
    grad_rows_part, grad_first_gain, grad_first_shift = first_pull(
        contract_cols(grad_joint, joint_weight)
    )
    grad_input = grad_after + grad_rows_part
    attention_part = (grad_first_gain, grad_first_shift, normed_low, grad_joint, mixed, grad_branch)
    feed_part = (
        grad_second_gain,
        grad_second_shift,
        normed_second,
        grad_lifted,
        active,
        grad_branch_two,
    )
    return (grad_input.reshape(shaped), attention_part, feed_part)


def attention_weights(part):
    grad_gain, grad_shift, normed_low, grad_joint, mixed, grad_branch = part
    return (
        grad_gain,
        grad_shift,
        contract_rows(normed_low, grad_joint),
        column_sums(grad_joint[:, :D]),
        column_sums(grad_joint[:, 2 * D :]),
        contract_rows(mixed, grad_branch),
        column_sums(grad_branch),
    )


def feed_weights(part):
    grad_gain, grad_shift, normed_second, grad_lifted, active, grad_branch_two = part
    return (
        grad_gain,
        grad_shift,
        contract_rows(normed_second, grad_lifted),
        column_sums(grad_lifted),
        contract_rows(active, grad_branch_two),
        column_sums(grad_branch_two),
    )


def run_backward(saved, grad_output, params):
    grad_input, attention_part, feed_part = layer_backward(saved, grad_output, params)
    return (grad_input, attention_weights(attention_part), feed_weights(feed_part))


def blank_backward(clip_count):
    grad_input = jnp.zeros((clip_count, L, D), jnp.float32)
    vector = jnp.zeros((D,), jnp.float32)
    attention_part = (
        vector,
        vector,
        jnp.zeros((D, 3 * D), jnp.float32),
        vector,
        vector,
        jnp.zeros((D, D), jnp.float32),
        vector,
    )
    feed_part = (
        vector,
        vector,
        jnp.zeros((D, FF), jnp.float32),
        jnp.zeros((FF,), jnp.float32),
        jnp.zeros((FF, D), jnp.float32),
        vector,
    )
    return (grad_input, attention_part, feed_part)


def shards(
    clips,
    mask_flags,
    mask_embed,
    pos_embed,
    first_gain,
    first_shift,
    joint_weight,
    query_bias,
    value_bias,
    mixer_weight,
    mixer_bias,
    second_gain,
    second_shift,
    up_weight,
    up_bias,
    down_weight,
    down_bias,
    out_grad,
):
    params = tuple(
        (
            weight[0]
            for weight in (
                first_gain,
                first_shift,
                joint_weight,
                query_bias,
                value_bias,
                mixer_weight,
                mixer_bias,
                second_gain,
                second_shift,
                up_weight,
                up_bias,
                down_weight,
                down_bias,
            )
        )
    )
    first_section = lax.axis_index("section") == 0
    keep = mask_flags.astype(jnp.float32)[..., None]
    blended = clips.astype(jnp.float32) * (1.0 - keep) + keep * mask_embed + pos_embed
    width = CLIP_MB
    forward_outputs = []
    forward_saved = []
    arriving = None
    for tick in range(MB + 1):

        def lead_forward():
            if tick < MB:
                return layer_forward(blended[tick * width : (tick + 1) * width], params)
            return blank_forward(width)

        def tail_forward():
            if tick >= 1:
                return layer_forward(arriving.astype(jnp.float32), params)
            return blank_forward(width)

        output, saved = lax.cond(first_section, lead_forward, tail_forward)
        forward_outputs.append(output)
        forward_saved.append(saved)
        if tick < MB:
            arriving = passed_along(output, "section", 1)
    returned = []
    attention_list = []
    feed_list = []
    leaving = None
    for tick in range(MB + 1):

        def lead_backward():
            if tick >= 1:
                incoming = leaving.astype(jnp.float32).reshape(-1, D)
                return run_backward(forward_saved[tick - 1], incoming, params)
            return blank_backward(width)

        def tail_backward():
            if tick < MB:
                incoming = (
                    out_grad[tick * width : (tick + 1) * width].astype(jnp.float32).reshape(-1, D)
                )
                return run_backward(forward_saved[tick + 1], incoming, params)
            return blank_backward(width)

        grad_input, attention_part, feed_part = lax.cond(
            first_section, lead_backward, tail_backward
        )
        returned.append(grad_input)
        attention_list.append(attention_part)
        feed_list.append(feed_part)
        if tick < MB:
            leaving = passed_along(grad_input.astype(jnp.bfloat16), "section", -1)
    feed_total = reduce(add_tuples, feed_list)
    feed_gain, feed_shift, feed_up, feed_up_bias, feed_down, feed_down_bias = feed_total
    attention_total = reduce(add_tuples, attention_list)
    attn_gain, attn_shift, attn_joint, attn_query, attn_value, attn_mixer, attn_mixer_bias = (
        attention_total
    )
    (
        attn_gain,
        attn_shift,
        attn_joint,
        attn_query,
        attn_value,
        attn_mixer,
        attn_mixer_bias,
        feed_gain,
        feed_shift,
        feed_up,
        feed_up_bias,
        feed_down,
        feed_down_bias,
    ) = (
        lax.psum_scatter(attn_gain, "batch", scatter_dimension=0, tiled=True),
        lax.psum_scatter(attn_shift, "batch", scatter_dimension=0, tiled=True),
        lax.psum_scatter(attn_joint, "batch", scatter_dimension=0, tiled=True),
        lax.psum_scatter(attn_query, "batch", scatter_dimension=0, tiled=True),
        lax.psum_scatter(attn_value, "batch", scatter_dimension=0, tiled=True),
        lax.psum_scatter(attn_mixer, "batch", scatter_dimension=0, tiled=True),
        lax.psum_scatter(attn_mixer_bias, "batch", scatter_dimension=0, tiled=True),
        lax.psum_scatter(feed_gain, "batch", scatter_dimension=0, tiled=True),
        lax.psum_scatter(feed_shift, "batch", scatter_dimension=0, tiled=True),
        lax.psum_scatter(feed_up, "batch", scatter_dimension=0, tiled=True),
        lax.psum_scatter(feed_up_bias, "batch", scatter_dimension=0, tiled=True),
        lax.psum_scatter(feed_down, "batch", scatter_dimension=0, tiled=True),
        lax.psum_scatter(feed_down_bias, "batch", scatter_dimension=0, tiled=True),
    )
    lead_outputs = jnp.concatenate(forward_outputs[:MB], axis=0)
    tail_outputs = jnp.concatenate(forward_outputs[1:], axis=0)
    layer_outputs = jnp.where(first_section, lead_outputs, tail_outputs)[None]
    lead_grads = jnp.concatenate(returned[1:], axis=0)
    tail_grads = jnp.concatenate(returned[:MB], axis=0)
    input_grads = jnp.where(first_section, lead_grads * (1.0 - keep), tail_grads).astype(
        jnp.bfloat16
    )[None]
    section_weight = jnp.where(first_section, 1.0, 0.0).astype(jnp.float32)
    mask_term = jnp.sum(lead_grads * keep, axis=(0, 1)) * section_weight
    position_term = jnp.sum(lead_grads, axis=0) * section_weight
    mask_half, position_half = (
        lax.psum_scatter(
            mask_term.astype(jnp.bfloat16), "section", scatter_dimension=0, tiled=True
        ).astype(jnp.float32),
        lax.psum_scatter(
            position_term.astype(jnp.bfloat16), "section", scatter_dimension=0, tiled=True
        ).astype(jnp.float32),
    )
    grad_mask_embed, grad_pos_embed = lax.psum((mask_half, position_half), "batch")
    return (
        layer_outputs,
        input_grads,
        attn_gain[None],
        attn_shift[None],
        attn_joint[None],
        attn_query[None],
        attn_value[None],
        attn_mixer[None],
        attn_mixer_bias[None],
        feed_gain[None],
        feed_shift[None],
        feed_up[None],
        feed_up_bias[None],
        feed_down[None],
        feed_down_bias[None],
        grad_mask_embed,
        grad_pos_embed,
    )


def solution(mesh):
    in_specs = (
        P("batch", None, None),
        P("batch", None),
        P(),
        P(),
        P("section", None),
        P("section", None),
        P("section", None, None),
        P("section", None),
        P("section", None),
        P("section", None, None),
        P("section", None),
        P("section", None),
        P("section", None),
        P("section", None, None),
        P("section", None),
        P("section", None, None),
        P("section", None),
        P("batch", None, None),
    )
    out_specs = (
        P("section", "batch", None, None),
        P("section", "batch", None, None),
        P("section", "batch"),
        P("section", "batch"),
        P("section", "batch", None),
        P("section", "batch"),
        P("section", "batch"),
        P("section", "batch", None),
        P("section", "batch"),
        P("section", "batch"),
        P("section", "batch"),
        P("section", "batch", None),
        P("section", "batch"),
        P("section", "batch", None),
        P("section", "batch"),
        P("section"),
        P("section", None),
    )
    return jax.shard_map(shards, mesh=mesh, in_specs=in_specs, out_specs=out_specs, check_vma=False)
```

profile of v0, /device:TPU:0, one launch (start us, length us, event | category | flops | bytes accessed | tf_op | source)
XLA Modules:
  0.0 1071.4 jit_solution(10581030471167765894)
XLA Ops:
  8.7 2.5 add_add_fusion.16
  11.3 73.3 %conditional.8 = (bf16[1,512,768]{2,1,0:T(8,128)(2,1)}, f32[512,768]{1,0:T(8,128)}, bf16[512,768]{1,0:T(8,128)(2,1)}, bf16[512,768]{1,0:T(8,128)(2,1)}, bf16[512...) conditional(s32[]{:T(128)} %convert_element_type.385, () %tuple.92, ...), branch_computations={%region_0.0_spmd, %region_1.8_spmd} | conditional | flops 8193043456 | bytes 151388304 | solution.py:344
  12.9 6.7 fusion.20
  19.6 3.3 fusion.15
  29.9 3.2 multiply_reduce_fusion
  35.2 2.4 copy-done
  40.0 8.0 fusion.19
  48.0 4.0 fusion.417
  53.7 8.4 convolution_add_fusion
  62.1 20.0 %add_convert_fusion = bf16[512,768]{1,0:T(8,128)(2,1)} fusion(f32[512,768]{1,0:T(8,128)} %get-tuple-element.1160, bf16[3072,768]{1,0:T(8,128)(2,1)} %get-tuple-element.427, f32[512,3072]{1,0:T(8,128)} %convolution_add_fusion, f32[768]{0:T(1024)S(1)} %reduce.13), kind=kOutput, calls=%fused_computation.32 | convolution fusion | flops 2519334912 | bytes 13372416 | tf_op jit(solution)/shard_map/cond/branch_1_fun/dot_general | solution.py:149
  85.9 18.0 %collective-permute-done = bf16[1,512,768]{2,1,0:T(8,128)(2,1)S(1)} collective-permute-done((bf16[1,512,768]{2,1,0:T(8,128)(2,1)}, bf16[1,512,768]{2,1,0:T(8,128)(2,1)S(1)}, u32[]{:S(2)}, u32[]{:S(2)}) %collective-permute-start) | collective-permute-done | bytes 786464 | tf_op jit(solution)/shard_map/ppermute | solution.py:20
  103.9 76.5 %conditional.27 = (bf16[1,512,768]{2,1,0:T(8,128)(2,1)}, f32[512,768]{1,0:T(8,128)}, f32[1,12,512]{2,1,0:T(8,128)}, f32[512,768]{1,0:T(8,128)}, f32[512,3072]{1,...) conditional(s32[]{:T(128)} %convert_element_type.385, ...), branch_computations={%region_8.15_spmd, %region_15.22_spmd} | conditional | flops 8193829888 | bytes 156008608
  114.1 6.8 fusion.136
  120.9 3.9 fusion.420
  136.0 7.8 fusion.135
  143.8 3.7 fusion.421
  149.3 8.5 convolution_add_fusion.2
  157.8 20.1 %add_convert_fusion.10 = bf16[512,768]{1,0:T(8,128)(2,1)} fusion(f32[512,768]{1,0:T(8,128)} %get-tuple-element.1176, bf16[3072,768]{1,0:T(8,128)(2,1)} %get-tuple-element.479, f32[512,3072]{1,0:T(8,128)} %convolution_add_fusion.2, f32[768]{0:T(1024)S(1)} %reduce.29), kind=kOutput, calls=%fused_computation.198 | convolution fusion | flops 2519334912 | bytes 13372416 | tf_op jit(solution)/shard_map/cond/branch_1_fun/dot_general | solution.py:149
  180.4 6.3 collective-permute-start.1
  186.7 22.0 %conditional.11 = (bf16[1,512,768]{2,1,0:T(8,128)(2,1)}, f32[768]{0:T(1024)S(1)}, f32[768]{0:T(1024)S(1)}, f32[768,2304]{1,0:T(8,128)}, f32[768]{0:T(1024)S(1)},...) conditional(s32[]{:T(128)} %convert_element_type.385, ...), branch_computations={%region_30.49_spmd, %region_49.50_spmd} | conditional | flops 16715996160 | bytes 395090624 | solution.py:369
  198.4 4.2 broadcast.1252
  202.6 3.4 broadcast.1248
  212.3 16.3 %conditional.10 = (f32[512,768]{1,0:T(8,128)S(1)}, bf16[512,768]{1,0:T(8,128)(2,1)}, bf16[512,768]{1,0:T(8,128)(2,1)}, bf16[512,768]{1,0:T(8,128)(2,1)}, f32[1,1...) conditional(s32[]{:T(128)} %convert_element_type.385, ...), branch_computations={%region_22.29_spmd, %region_29.30_spmd} | conditional | flops 8193829888 | bytes 154435776 | solution.py:344
  221.1 3.4 broadcast.1209
  228.6 100.7 %collective-permute-done.2 = bf16[1,512,768]{2,1,0:T(8,128)(2,1)} collective-permute-done((bf16[1,512,768]{2,1,0:T(8,128)(2,1)}, bf16[1,512,768]{2,1,0:T(8,128)(2,1)}, u32[]{:S(2)}, u32[]{:S(2)}) %collective-permute-start.2) | collective-permute-done | bytes 786464 | tf_op jit(solution)/shard_map/ppermute | solution.py:20
  329.3 131.9 %conditional.12 = (f32[1,512,768]{2,1,0:T(8,128)}, f32[768]{0:T(1024)S(1)}, f32[768]{0:T(1024)S(1)}, f32[768,2304]{1,0:T(8,128)}, f32[768]{0:T(1024)S(1)}, /*ind...) conditional(s32[]{:T(128)} %convert_element_type.385, ...), branch_computations={%region_50.69_spmd, %region_69.88_spmd} | conditional | flops 16715603968 | bytes 414751488 | solution.py:369
  340.9 14.1 %fusion.324 = f32[512,3072]{1,0:T(8,128)S(1)} fusion(f32[512,3072]{1,0:T(8,128)} %get-tuple-element.530), kind=kLoop, calls=%fused_computation.505 | loop fusion | flops 97517568 | bytes 12582912 | tf_op jit(solution)/shard_map/cond/branch_1_fun/jvp()/erfc | solution.py:31
  355.1 9.0 convert_reduce_fusion.12
  364.1 6.9 multiply_reduce_fusion.27
  383.8 7.5 fusion.425
  393.7 11.0 %multiply_reduce_fusion.26 = (f32[12,512]{1,0:T(8,128)S(1)}, f32[12,512,512]{1,2,0:T(8,128)}) fusion(f32[12,512,512]{1,2,0:T(8,128)} %fusion.425, f32[12,512]{1,0:T(8,128)S(1)} %bitcast.405, bf16[512,12,64]{0,2,1:T(8,128)(2,1)S(1)} %bitcast.354, bf16[512,12,64]{0,2,1:T(8,128)(2,1)} %bitcast.368), kind=kOutput, calls=%fused_computation.500 | convolution fusion | flops 415229952 | bytes 26787840 | tf_op jit(solution)/shard_map/cond/branch_1_fun/while/body/eval_jaxpr/qhc,khc->hqk/dot_general | solution.py:82
  406.6 6.9 multiply_convert_fusion.10
  415.5 2.9 multiply_convert_fusion.13
  418.4 3.1 fusion.334
  421.6 7.1 fusion.338
  428.7 3.9 multiply_reduce_fusion.28
  434.8 2.7 convert_reduce_fusion.13
  442.2 9.0 fusion.340
  451.2 9.6 fusion.332
  464.0 60.5 %collective-permute-done.3 = bf16[1,512,768]{2,1,0:T(8,128)(2,1)S(1)} collective-permute-done((bf16[1,512,768]{2,1,0:T(8,128)(2,1)S(1)}, bf16[1,512,768]{2,1,0:T(8,128)(2,1)S(1)}, u32[]{:S(2)}, u32[]{:S(2)}) %collective-permute-start.3) | collective-permute-done | bytes 786464 | tf_op jit(solution)/shard_map/ppermute | solution.py:20
  524.5 125.0 %conditional.26 = (f32[1,512,768]{2,1,0:T(8,128)}, f32[768]{0:T(1024)S(1)}, f32[768]{0:T(1024)S(1)}, f32[768,2304]{1,0:T(8,128)}, f32[768]{0:T(1024)S(1)}, /*ind...) conditional(s32[]{:T(128)} %convert_element_type.385, ...), branch_computations={%region_88.89_spmd, %region_89.108_spmd} | conditional | flops 16715603968 | bytes 381721184 | solution.py:369
  528.4 14.1 %fusion.363 = f32[512,3072]{1,0:T(8,128)S(1)} fusion(f32[512,3072]{1,0:T(8,128)} %get-tuple-element.547), kind=kLoop, calls=%fused_computation.583 | loop fusion | flops 97517568 | bytes 12582912 | tf_op jit(solution)/shard_map/cond/branch_1_fun/jvp()/erfc | solution.py:31
  542.6 10.0 convert_reduce_fusion.17
  552.5 6.7 multiply_reduce_fusion.34
  571.8 7.5 fusion.426
  581.5 11.0 %multiply_reduce_fusion.33 = (f32[12,512]{1,0:T(8,128)S(1)}, f32[12,512,512]{1,2,0:T(8,128)}) fusion(f32[12,512,512]{1,2,0:T(8,128)} %fusion.426, f32[12,512]{1,0:T(8,128)} %bitcast.91, bf16[512,12,64]{0,2,1:T(8,128)(2,1)S(1)} %bitcast.356, bf16[512,12,64]{0,2,1:T(8,128)(2,1)} %bitcast.369), kind=kOutput, calls=%fused_computation.578 | convolution fusion | flops 415229952 | bytes 26787840 | tf_op jit(solution)/shard_map/cond/branch_1_fun/while/body/eval_jaxpr/qhc,khc->hqk/dot_general | solution.py:82
  594.4 6.9 multiply_convert_fusion.15
  603.3 2.9 multiply_convert_fusion.18
  606.2 4.2 fusion.373
  610.5 7.2 fusion.377
  617.8 4.2 multiply_reduce_fusion.35
  631.0 9.0 fusion.379
  640.0 9.4 fusion.371
  649.5 3.1 fusion.404
  652.7 4.3 add_add_fusion.17
  657.1 11.4 %add_add_fusion.15 = f32[768,2304]{1,0:T(8,128)} fusion(f32[768,2304]{1,0:T(8,128)} %get-tuple-element.691, f32[768,2304]{1,0:T(8,128)} %get-tuple-element.689, f32[768,2304]{1,0:T(8,128)} %get-tuple-element.690), kind=kLoop, calls=%fused_computation.659 | loop fusion | flops 3538944 | bytes 28311552 | tf_op jit(solution)/shard_map/add | solution.py:55
  668.6 13.9 %add_add_fusion.13 = f32[3072,768]{1,0:T(8,128)} fusion(f32[3072,768]{1,0:T(8,128)} %get-tuple-element.718, f32[3072,768]{1,0:T(8,128)} %get-tuple-element.716, f32[3072,768]{1,0:T(8,128)} %get-tuple-element.717), kind=kLoop, calls=%fused_computation.657 | loop fusion | flops 4718592 | bytes 37748736 | tf_op jit(solution)/shard_map/add | solution.py:55
  682.6 15.7 %add_add_fusion.14 = f32[768,3072]{1,0:T(8,128)} fusion(f32[768,3072]{1,0:T(8,128)} %get-tuple-element.712, f32[768,3072]{1,0:T(8,128)} %copy-done.18, f32[768,3072]{1,0:T(8,128)} %get-tuple-element.711), kind=kLoop, calls=%fused_computation.658 | loop fusion | flops 4718592 | bytes 37748736 | tf_op jit(solution)/shard_map/add | solution.py:55
  704.0 4.9 all-reduce.9
  709.2 4.4 fusion.402
  713.6 72.7 %all-reduce.12 = (f32[768]{0:T(1024)S(1)}, f32[768]{0:T(1024)S(1)}, f32[768]{0:T(1024)S(1)}, f32[768]{0:T(1024)S(1)}, f32[768]{0:T(1024)S(1)}, /*index=5*/f32[76...) all-reduce(f32[768]{0:T(1024)S(1)} %get-tuple-element.1142, ...), channel_id=2, replica_groups=mesh['section'=2,'batch'=16] {'batch'}, use_global_device_ids=true, to_apply=%region_108.109.clone | all-reduce | flops 206208 | bytes 1256448
  791.6 42.3 %reduce-scatter.6.cloned.1.call-done = f32[48,2304]{1,0:T(8,128)} async-done(((f32[768,2304]{1,0:T(8,128)}), f32[48,2304]{1,0:T(8,128)}) %reduce-scatter.6.cloned.1.call-update) | async-done | bytes 442384 | tf_op jit(solution)/shard_map/reduce_scatter | solution.py:400
  833.8 115.4 %reduce-scatter.12.cloned.1.call-done = f32[192,768]{1,0:T(8,128)} async-done(((f32[3072,768]{1,0:T(8,128)}), f32[192,768]{1,0:T(8,128)}) %reduce-scatter.12.cloned.1.call-update) | async-done | bytes 589840 | tf_op jit(solution)/shard_map/reduce_scatter | solution.py:409
  949.3 115.4 %reduce-scatter.10.cloned.1.call-done = f32[48,3072]{1,0:T(8,128)} async-done(((f32[768,3072]{1,0:T(8,128)}), f32[48,3072]{1,0:T(8,128)}) %reduce-scatter.10.cloned.1.call-update) | async-done | bytes 589840 | tf_op jit(solution)/shard_map/reduce_scatter | solution.py:407
  (314 shorter events, 120.2 us)
Async XLA Ops:
  7.2 4.0 copy-start.50
  7.2 4.0 copy-start.51
  7.2 4.0 copy-start.55
  7.2 4.0 copy-start.54
  7.2 4.0 copy-start.56
  7.2 4.0 copy-start.52
  7.3 4.0 copy-start.53
  7.3 4.0 copy-start.86
  7.3 4.0 copy-start.57
  7.3 706.3 %reduce-scatter.14.cloned.1.call-start = ((), (), s32[]{:S(2)}) async-start(), calls=%async_computation.9 | async-start | bytes 1179648 | tf_op jit(solution)/shard_map/reduce_scatter | solution.py:427
  33.1 4.6 copy-start
  37.7 10.3 copy-start.46
  84.6 19.3 %collective-permute-start = (bf16[1,512,768]{2,1,0:T(8,128)(2,1)}, bf16[1,512,768]{2,1,0:T(8,128)(2,1)S(1)}, u32[]{:S(2)}, u32[]{:S(2)}) collective-permute-start(bf16[1,512,768]{2,1,0:T(8,128)(2,1)} %get-tuple-element.652), channel_id=1, source_target_pairs={{0,16},{1,17},{2,18},{3,19},{4,20},{5,21},{6,22},{7,23},{8,24},{9,... | collective-permute-start | bytes 2359304 | tf_op jit(solution)/shard_map/ppermute | solution.py:20
  129.4 4.5 copy-start.2
  135.9 7.9 copy-start.85
  180.4 29.7 %collective-permute-start.1 = (bf16[1,512,768]{2,1,0:T(8,128)(2,1)}, bf16[1,512,768]{2,1,0:T(8,128)(2,1)}, u32[]{:S(2)}, u32[]{:S(2)}) collective-permute-start(bf16[1,512,768]{2,1,0:T(8,128)(2,1)} %get-tuple-element.654), channel_id=1, source_target_pairs={{0,16},{1,17},{2,18},{3,19},{4,20},{5,21},{6,22},{7,23},{8,24},{9,... | collective-permute-start | bytes 2359304 | tf_op jit(solution)/shard_map/ppermute | solution.py:20
  208.8 120.5 %collective-permute-start.2 = (bf16[1,512,768]{2,1,0:T(8,128)(2,1)}, bf16[1,512,768]{2,1,0:T(8,128)(2,1)}, u32[]{:S(2)}, u32[]{:S(2)}) collective-permute-start(bf16[1,512,768]{2,1,0:T(8,128)(2,1)} %get-tuple-element.672), channel_id=1, source_target_pairs={{16,0},{17,1},{18,2},{19,3},{20,4},{21,5},{22,6},{23,7},{24,8},{25... | collective-permute-start | bytes 2359304 | tf_op jit(solution)/shard_map/ppermute | solution.py:20
  210.1 119.2 %copy-start.47 = (f32[1,12,512]{2,1,0:T(8,128)S(1)}, f32[1,12,512]{2,1,0:T(8,128)}, u32[]{:S(2)}) copy-start(f32[1,12,512]{2,1,0:T(8,128)} %get-tuple-element.677) | copy-start | bytes 73732
  228.6 100.7 %copy-start.48 = (bf16[1,1,512,768]{3,2,1,0:T(8,128)(2,1)}, bf16[1,1,512,768]{3,2,1,0:T(8,128)(2,1)S(1)}, u32[]{:S(2)}) copy-start(bf16[1,1,512,768]{3,2,1,0:T(8,128)(2,1)S(1)} %get-tuple-element.655) | copy-start | bytes 2359300
  339.0 16.0 %slice-start.24 = ((s8[4718592]{0:T(1024)(128)(4,1)}), s8[4194304]{0:T(1024)(128)(4,1)S(1)}, s32[]{:S(2)}) async-start(s8[4718592]{0:T(1024)(128)(4,1)} %bitcast.429), calls=%async_computation.34 | async-start | bytes 8388608 | tf_op jit(solution)/shard_map/cond
  340.9 14.2 %slice-start.25 = ((s8[4718592]{0:T(1024)(128)(4,1)}), s8[524288]{0:T(1024)(128)(4,1)S(1)}, s32[]{:S(2)}) async-start(s8[4718592]{0:T(1024)(128)(4,1)} %bitcast.429), calls=%async_computation.35 | async-start | bytes 1048576 | tf_op jit(solution)/shard_map/cond
  355.0 9.0 copy-start.6
  364.1 6.9 copy-start.92
  393.7 11.0 %slice-start.6 = ((s8[12582912]{0:T(1024)(128)(4,1)}), s8[4194304]{0:T(1024)(128)(4,1)S(1)}, s32[]{:S(2)}) async-start(s8[12582912]{0:T(1024)(128)(4,1)} %bitcast.329), calls=%async_computation.16 | async-start | bytes 8388608 | tf_op jit(solution)/shard_map/cond
  393.7 11.0 %slice-start.7 = ((s8[12582912]{0:T(1024)(128)(4,1)}), s8[4194304]{0:T(1024)(128)(4,1)S(1)}, s32[]{:S(2)}) async-start(s8[12582912]{0:T(1024)(128)(4,1)} %bitcast.329), calls=%async_computation.17 | async-start | bytes 8388608 | tf_op jit(solution)/shard_map/cond
  393.7 12.8 %slice-start.8 = ((s8[12582912]{0:T(1024)(128)(4,1)}), s8[4194304]{0:T(1024)(128)(4,1)S(1)}, s32[]{:S(2)}) async-start(s8[12582912]{0:T(1024)(128)(4,1)} %bitcast.329), calls=%async_computation.18 | async-start | bytes 8388608 | tf_op jit(solution)/shard_map/cond
  421.5 7.2 copy-start.31
  421.6 7.2 copy-start.82
  421.6 7.1 copy-start.89
  432.7 5.3 copy-start.45
  442.1 9.0 slice-start.16
  442.2 9.0 slice-start.17
  462.7 61.8 %collective-permute-start.3 = (bf16[1,512,768]{2,1,0:T(8,128)(2,1)S(1)}, bf16[1,512,768]{2,1,0:T(8,128)(2,1)S(1)}, u32[]{:S(2)}, u32[]{:S(2)}) collective-permute-start(bf16[1,512,768]{2,1,0:T(8,128)(2,1)S(1)} %convert_element_type.393), channel_id=1, source_target_pairs={{16,0},{17,1},{18,2},{19,3},{20,4},{21,5},{22,6},{23,7},{24,8},{25... | collective-permute-start | bytes 2359304 | tf_op jit(solution)/shard_map/ppermute | solution.py:20
  524.6 38.2 %copy-start.23 = (bf16[1,512,768]{2,1,0:T(8,128)(2,1)}, bf16[1,512,768]{2,1,0:T(8,128)(2,1)S(1)}, u32[]{:S(2)}) copy-start(bf16[1,512,768]{2,1,0:T(8,128)(2,1)S(1)} %get-tuple-element.546) | copy-start | bytes 2359300 | tf_op jit(solution)/shard_map/cond
  526.5 16.0 %slice-start.26 = ((s8[4718592]{0:T(1024)(128)(4,1)}), s8[4194304]{0:T(1024)(128)(4,1)S(1)}, s32[]{:S(2)}) async-start(s8[4718592]{0:T(1024)(128)(4,1)} %bitcast.431), calls=%async_computation.36 | async-start | bytes 8388608 | tf_op jit(solution)/shard_map/cond
  528.4 14.2 %slice-start.27 = ((s8[4718592]{0:T(1024)(128)(4,1)}), s8[524288]{0:T(1024)(128)(4,1)S(1)}, s32[]{:S(2)}) async-start(s8[4718592]{0:T(1024)(128)(4,1)} %bitcast.431), calls=%async_computation.37 | async-start | bytes 1048576 | tf_op jit(solution)/shard_map/cond
  542.5 10.0 copy-start.4
  581.5 11.0 %slice-start.9 = ((s8[12582912]{0:T(1024)(128)(4,1)}), s8[4194304]{0:T(1024)(128)(4,1)S(1)}, s32[]{:S(2)}) async-start(s8[12582912]{0:T(1024)(128)(4,1)} %bitcast.331), calls=%async_computation.19 | async-start | bytes 8388608 | tf_op jit(solution)/shard_map/cond
  581.5 11.0 %slice-start.10 = ((s8[12582912]{0:T(1024)(128)(4,1)}), s8[4194304]{0:T(1024)(128)(4,1)S(1)}, s32[]{:S(2)}) async-start(s8[12582912]{0:T(1024)(128)(4,1)} %bitcast.331), calls=%async_computation.20 | async-start | bytes 8388608 | tf_op jit(solution)/shard_map/cond
  581.5 12.9 %slice-start.11 = ((s8[12582912]{0:T(1024)(128)(4,1)}), s8[4194304]{0:T(1024)(128)(4,1)S(1)}, s32[]{:S(2)}) async-start(s8[12582912]{0:T(1024)(128)(4,1)} %bitcast.331), calls=%async_computation.21 | async-start | bytes 8388608 | tf_op jit(solution)/shard_map/cond
  606.2 4.3 copy-start.25
  610.5 7.3 copy-start.29
  610.5 7.2 copy-start.83
  617.8 6.3 copy-start.24
  622.0 4.6 copy-start.41
  631.0 9.0 slice-start.12
  631.0 9.0 slice-start.13
  652.7 138.9 %reduce-scatter.8.cloned.1.call-start = ((), (), s32[]{:S(2)}) async-start(), calls=%async_computation.6 | async-start | bytes 2506752 | tf_op jit(solution)/shard_map/reduce_scatter | solution.py:403
  657.0 176.8 %reduce-scatter.6.cloned.1.call-start = ((), (), s32[]{:S(2)}) async-start(), calls=%async_computation.5 | async-start | bytes 7520256 | tf_op jit(solution)/shard_map/reduce_scatter | solution.py:400
  668.5 280.7 %reduce-scatter.12.cloned.1.call-start = ((), (), s32[]{:S(2)}) async-start(), calls=%async_computation.8 | async-start | bytes 10027008 | tf_op jit(solution)/shard_map/reduce_scatter | solution.py:409
  682.5 382.1 %reduce-scatter.10.cloned.1.call-start = ((), (), s32[]{:S(2)}) async-start(), calls=%async_computation.7 | async-start | bytes 10027008 | tf_op jit(solution)/shard_map/reduce_scatter | solution.py:407
  698.3 3.8 copy-start.8
  698.3 3.8 copy-start.61
  698.3 10.8 %copy-start.65 = (f32[768]{0:T(1024)S(1)}, f32[768]{0:T(1024)}, u32[]{:S(2)}) copy-start(f32[768]{0:T(1024)} %copy-done.64) | copy-start | bytes 9220
  698.3 10.7 %copy-start.75 = (f32[768]{0:T(1024)S(1)}, f32[768]{0:T(1024)}, u32[]{:S(2)}) copy-start(f32[768]{0:T(1024)} %copy-done.74) | copy-start | bytes 9220
  698.3 10.8 %copy-start.63 = (f32[768]{0:T(1024)S(1)}, f32[768]{0:T(1024)}, u32[]{:S(2)}) copy-start(f32[768]{0:T(1024)} %copy-done.62) | copy-start | bytes 9220
  698.3 10.8 %copy-start.73 = (f32[768]{0:T(1024)S(1)}, f32[768]{0:T(1024)}, u32[]{:S(2)}) copy-start(f32[768]{0:T(1024)} %copy-done.72) | copy-start | bytes 9220
  698.3 10.8 %copy-start.67 = (f32[768]{0:T(1024)S(1)}, f32[768]{0:T(1024)}, u32[]{:S(2)}) copy-start(f32[768]{0:T(1024)} %copy-done.66) | copy-start | bytes 9220
  698.4 10.8 %copy-start.69 = (f32[768]{0:T(1024)S(1)}, f32[768]{0:T(1024)}, u32[]{:S(2)}) copy-start(f32[768]{0:T(1024)} %copy-done.68) | copy-start | bytes 9220
  698.4 10.8 %copy-start.77 = (f32[768]{0:T(1024)S(1)}, f32[768]{0:T(1024)}, u32[]{:S(2)}) copy-start(f32[768]{0:T(1024)} %copy-done.76) | copy-start | bytes 9220
  698.4 10.8 %copy-start.79 = (f32[768]{0:T(1024)S(1)}, f32[768]{0:T(1024)}, u32[]{:S(2)}) copy-start(f32[768]{0:T(1024)} %copy-done.78) | copy-start | bytes 9220
  698.4 10.8 %copy-start.71 = (f32[3072]{0:T(1024)S(1)}, f32[3072]{0:T(1024)}, u32[]{:S(2)}) copy-start(f32[3072]{0:T(1024)} %copy-done.70) | copy-start | bytes 36868
  698.4 10.8 %copy-start.49 = (bf16[1,1,512,768]{3,2,1,0:T(8,128)(2,1)S(1)}, bf16[1,1,512,768]{3,2,1,0:T(8,128)(2,1)}, u32[]{:S(2)}) copy-start(bf16[1,1,512,768]{3,2,1,0:T(8,128)(2,1)} %copy-done.48) | copy-start | bytes 2359300
  698.4 10.8 %copy-start.59 = (f32[2,512]{1,0:T(2,128)S(1)}, f32[2,512]{1,0:T(2,128)}, u32[]{:S(2)}) copy-start(f32[2,512]{1,0:T(2,128)} %copy-done.58) | copy-start | bytes 12292
  (20 other events, 47.1 us)
Sparse Core Ops, SparseCore 0:
  652.8 17.9 reduce-scatter.13
  675.1 64.3 reduce-scatter.7
  744.1 89.6 reduce-scatter.5
  838.4 110.8 reduce-scatter.11
  953.8 110.8 reduce-scatter.9
where the time goes:
time: 1080 us; the launch traced here: 1070 us
  waiting for transfers between devices  452 us (42%)
  matrix products  253 us (23%)
  other arithmetic  149 us (14%)
  blocking collectives  77.6 us (7%)
  local copies, waits for them, and re-layouts  73.4 us (7%)
  loops' own time  38.5 us (4%)
  between operations  16.6 us (2%)
    ppermute x4, waiting for transfers between devices, passed_along(): return lax.ppermute(block, axis, route)  179 us
    reduce_scatter x1, waiting for transfers between devices, shards(): lax.psum_scatter(feed_down, 'batch', scatter_dimension=0, tiled=True)  115 us
    reduce_scatter x1, waiting for transfers between devices, shards(): lax.psum_scatter(feed_up, 'batch', scatter_dimension=0, tiled=True)  115 us
    unnamed x2, blocking collectives  77.6 us
    dot_general x8, matrix products, contract_rows(): lax.dot_general(left, right, (((0,), (0,)), ((), ())), preferred_element_...  55.2 us
    add x9, other arithmetic, add_tuples(): first_item + second_item  45.4 us
    dot_general x8, matrix products, contract_cols(): lax.dot_general(left, right, (((1,), (1,)), ((), ())), preferred_element_...  44.8 us
    reduce_scatter x1, waiting for transfers between devices, shards(): lax.psum_scatter(attn_joint, 'batch', scatter_dimension=0, tiled=True)  42.3 us
  transfers between devices with their start and end apart: 9, of which 6 were waited for; matrix products, arithmetic and copies ran while one was open for 7% of the time, Pallas kernels for 0%

commit v1 on v0

v1 whole, which is shorter than its diff:
```python
import functools
import jax
import jax.numpy as jnp
from jax import lax
from jax.experimental import pallas as pl
from jax.experimental.pallas import tpu as pltpu
from jax.sharding import PartitionSpec as P
D, HEADS, HD, FF, L = 768, 12, 64, 3072, 512
bf, f32 = jnp.bfloat16, jnp.float32
LOG2E = 1.4426950408889634
SCORE = HD ** (-0.5) * LOG2E
ERF_P = 0.3
ERF_C = (0.11962929578251927, 0.12075400757487373, 0.09991313981909876, 0.12856288726251214,
         -0.05368619840832163, 0.2063564440760747, -0.15720486481493717, 0.035675215624358596)
ANY = pl.BlockSpec(memory_space=pl.ANY)
VM = pl.BlockSpec(memory_space=pltpu.VMEM)
SM = pl.BlockSpec(memory_space=pltpu.SMEM)


def mm(left, right, lc, rc):
    return lax.dot_general(left, right, (((lc,), (rc,)), ((), ())), preferred_element_type=f32)


def gelu_parts(value):
    size = jnp.abs(value)
    t = 1.0 / (1.0 + ERF_P * size)
    total = ERF_C[-1] * t + ERF_C[-2]
    for coefficient in ERF_C[-3::-1]:
        total = total * t + coefficient
    bell = jnp.exp2(value * value * (-0.5 * LOG2E))
    tail = total * t * bell
    phi = jnp.where(value < 0.0, tail, 1.0 - tail)
    return value * phi, phi + value * (bell * 0.3989422804014327)


def norm_stats(rows):
    mean = jnp.mean(rows, axis=1, keepdims=True)
    centered = rows - mean
    rstd = lax.rsqrt(jnp.mean(centered * centered, axis=1, keepdims=True) + 1e-6)
    return centered * rstd, rstd


def norm_back(e, xhat, rstd, gain):
    eg = e * gain
    return (eg - jnp.mean(eg, axis=1, keepdims=True) - xhat * jnp.mean(eg * xhat, axis=1, keepdims=True)) * rstd


class Copies:
    def __init__(self, sems):
        self.sems, self.count, self.pending = sems, 0, []

    def start(self, src, dst):
        copy = pltpu.make_async_copy(src, dst, self.sems.at[self.count])
        self.count += 1
        copy.start()
        return copy

    def out(self, src, dst):
        self.pending.append(self.start(src, dst))

    def finish(self):
        for copy in self.pending:
            copy.wait()


def front(clip, extra, side, x_in, vec, ub, wj_in, wm_in, wu_in, wd_in, *rest):
    outs = rest[extra : extra + 9]
    x, wj, wm, wu, wd, n1, qkv, lt, mixed, after, n2, act, slope, out, sems = rest[extra + 9 :]
    o_n1, o_qkv, o_lt, o_mixed, o_after, o_n2, o_act, o_slope, o_out = outs

    @pl.when(side[0] != 0)
    def _():
        c = Copies(sems)
        cx = c.start(x_in.at[clip] if clip is not None else x_in, x)
        cj = c.start(wj_in, wj)
        cm = c.start(wm_in, wm)
        cu = c.start(wu_in, wu)
        cd = c.start(wd_in, wd)
        g1, s1, qb, vb, mb, g2, s2, db = [vec[i : i + 1, :] for i in range(8)]
        cx.wait()
        xhat, _ = norm_stats(x[...].astype(f32))
        n1[...] = (xhat * g1 + s1).astype(bf)
        c.out(n1, o_n1)
        cj.wait()
        for part, bias in enumerate((qb, None, vb)):
            s = slice(part * D, (part + 1) * D)
            block = mm(n1[...], wj[:, s], 1, 0)
            qkv[:, s] = (block if bias is None else block + bias).astype(bf)
        c.out(qkv, o_qkv)

        lane = lax.broadcasted_iota(jnp.int32, (L, 128), 1)

        def pair(p, logs):
            cols = [pl.ds(pl.multiple_of(p * 128 + part * D, 128), 128) for part in range(3)]
            q, k, v = [qkv[:, s] for s in cols]
            res = []
            for h in range(2):
                qm = jnp.where((lane < 64) == (h == 0), q, jnp.zeros_like(q))
                s = mm(qm, k, 1, 1)
                top = jnp.max(s, axis=1, keepdims=True)
                e = jnp.exp2((s - top) * SCORE)
                total = jnp.sum(e, axis=1, keepdims=True)
                w = (e * (1.0 / total)).astype(bf)
                res.append(mm(w, v, 1, 0))
                logs = jnp.where(lane == 2 * p + h, top * SCORE + jnp.log2(total), logs)
            mixed[:, cols[0]] = jnp.where(lane < 64, res[0], res[1]).astype(bf)
            return logs

        logs = lax.fori_loop(0, HEADS // 2, pair, jnp.zeros((L, 128), f32))
        lt[...] = jnp.transpose(logs)[:16, :]
        c.out(lt, o_lt)
        c.out(mixed, o_mixed)
        cm.wait()
        rows = x[...].astype(f32) + (mm(mixed[...], wm[...], 1, 0) + mb)
        after[...] = rows
        c.out(after, o_after)
        xhat, _ = norm_stats(rows)
        n2[...] = (xhat * g2 + s2).astype(bf)
        c.out(n2, o_n2)
        cu.wait()
        for j in range(FF // D):
            s = slice(j * D, (j + 1) * D)
            for r in range(2):
                rs = slice(r * 256, (r + 1) * 256)
                lifted = mm(n2[rs, :], wu[:, s], 1, 0) + ub[:, s]
                a, b = gelu_parts(lifted)
                act[rs, s] = a.astype(bf)
                slope[rs, s] = b.astype(bf)
        c.out(act, o_act)
        c.out(slope, o_slope)
        cd.wait()
        out[...] = (after[...] + (mm(act[...], wd[...], 1, 0) + db)).astype(bf)
        c.out(out, o_out)
        c.finish()


SAVED = (((L, D), bf), ((L, 3 * D), bf), ((16, L), f32), ((L, D), bf), ((L, D), f32), ((L, D), bf),
         ((L, FF), bf), ((L, FF), bf), ((L, D), bf))


def shapes(spec):
    return [jax.ShapeDtypeStruct(*one) for one in spec]


def scratch(spec):
    return [pltpu.VMEM(*one) for one in spec]


PARAMS = pltpu.CompilerParams(vmem_limit_bytes=62 << 20)


def forward(side, x, clip, vec, ub, weights, old=None):
    extra = 0 if old is None else 9
    xt = ((L, D), x.dtype)
    ws = [(w.shape, w.dtype) for w in weights]
    return pl.pallas_call(
        functools.partial(front, clip, extra),
        out_shape=shapes(SAVED),
        in_specs=[SM, ANY, VM, VM] + [ANY] * (4 + extra),
        out_specs=[ANY] * 9,
        scratch_shapes=scratch([xt] + ws + list(SAVED)) + [pltpu.SemaphoreType.DMA((16,))],
        input_output_aliases={8 + i: i for i in range(extra)},
        compiler_params=PARAMS,
        cost_estimate=pl.CostEstimate(flops=8_050_000_000, bytes_accessed=30_000_000, transcendentals=5_000_000),
    )(side, x, vec, ub, *weights, *(old or ()))


def mlp_back(clip, extra, side, g_in, vec, slope_in, after_in, wu_in, wd_in, *rest):
    o_gl, o_ga, o_vec = rest[extra : extra + 3]
    g, slope, after, wu, wd, gl, ga, vout, sems = rest[extra + 3 :]

    @pl.when(side[0] != 0)
    def _():
        c = Copies(sems)
        cg = c.start(g_in.at[clip] if clip is not None else g_in, g)
        cd = c.start(wd_in, wd)
        cs = c.start(slope_in, slope)
        cu = c.start(wu_in, wu)
        ca = c.start(after_in, after)
        cg.wait()
        cd.wait()
        cs.wait()
        for j in range(FF // D):
            s = slice(j * D, (j + 1) * D)
            piece = (mm(g[...], wd[s, :], 1, 1) * slope[:, s].astype(f32)).astype(bf)
            gl[:, s] = piece
            vout[0:1, s] = jnp.sum(piece.astype(f32), axis=0, keepdims=True)
        c.out(gl, o_gl)
        cu.wait()
        ca.wait()
        e = mm(gl[...], wu[...], 1, 1)
        xhat, rstd = norm_stats(after[...])
        gv = g[...].astype(f32)
        vout[1:2, 0:D] = jnp.sum(e * xhat, axis=0, keepdims=True)
        vout[1:2, D : 2 * D] = jnp.sum(e, axis=0, keepdims=True)
        vout[1:2, 2 * D : 3 * D] = jnp.sum(gv, axis=0, keepdims=True)
        ga[...] = gv + norm_back(e, xhat, rstd, vec[5:6, :])
        c.out(ga, o_ga)
        c.out(vout, o_vec)
        c.finish()


MB_OUT = (((L, FF), bf), ((L, D), f32), ((8, FF), f32))


def backward_mlp(side, g, clip, vec, slope, after, wu, wd, old=None):
    extra = 0 if old is None else 3
    sc = [((L, D), bf), ((L, FF), bf), ((L, D), f32), (wu.shape, bf), (wd.shape, bf)]
    return pl.pallas_call(
        functools.partial(mlp_back, clip, extra),
        out_shape=shapes(MB_OUT),
        in_specs=[SM, ANY, VM] + [ANY] * (4 + extra),
        out_specs=[ANY] * 3,
        scratch_shapes=scratch(sc + list(MB_OUT)) + [pltpu.SemaphoreType.DMA((16,))],
        input_output_aliases={7 + i: i for i in range(extra)},
        compiler_params=PARAMS,
        cost_estimate=pl.CostEstimate(flops=4_830_000_000, bytes_accessed=20_000_000, transcendentals=1000),
    )(side, g, vec, slope, after, wu, wd, *(old or ()))


def attn_back(clip, extra, side, ga_in, x_in, vec, qkv_in, lt_in, wm_in, wj_in, *rest):
    o_gb, o_gj, o_gh, o_vec = rest[extra : extra + 4]
    ga, x, qkv, lt, wm, wj, gm, gb, gj, gh, vout, sems = rest[extra + 4 :]

    @pl.when(side[0] != 0)
    def _():
        c = Copies(sems)
        cg = c.start(ga_in, ga)
        cm = c.start(wm_in, wm)
        cq = c.start(qkv_in, qkv)
        cl = c.start(lt_in, lt)
        cj = c.start(wj_in, wj)
        cx = c.start(x_in.at[clip] if clip is not None else x_in, x)
        cg.wait()
        cm.wait()
        gb[...] = ga[...].astype(bf)
        c.out(gb, o_gb)
        gm[...] = mm(gb[...], wm[...], 1, 1).astype(bf)
        cq.wait()
        cl.wait()
        lane = lax.broadcasted_iota(jnp.int32, (L, 128), 1)

        def pair(p, carry):
            cols = [pl.ds(pl.multiple_of(p * 128 + part * D, 128), 128) for part in range(3)]
            q, k, v = [qkv[:, s] for s in cols]
            go = gm[:, cols[0]]
            res = []
            for h in range(2):
                own = (lane < 64) == (h == 0)
                km = jnp.where(own, k, jnp.zeros_like(k))
                vm = jnp.where(own, v, jnp.zeros_like(v))
                w = jnp.exp2(mm(km, q, 1, 1) * SCORE - lt[pl.ds(2 * p + h, 1), :])
                gw = mm(vm, go, 1, 1)
                inner = jnp.sum(w * gw, axis=0, keepdims=True)
                gs = (w * (gw - inner)).astype(bf)
                res.append((mm(gs, k, 0, 0), mm(gs, q, 1, 0), mm(w.astype(bf), go, 1, 0)))
            for part, scale in enumerate((HD ** (-0.5), HD ** (-0.5), 1.0)):
                both = jnp.where(lane < 64, res[0][part], res[1][part])
                gj[:, cols[part]] = (both * scale).astype(bf)
            return carry

        lax.fori_loop(0, HEADS // 2, pair, 0)
        c.out(gj, o_gj)
        cj.wait()
        cx.wait()
        e = mm(gj[...], wj[...], 1, 1)
        xhat, rstd = norm_stats(x[...].astype(f32))
        vout[0:1, :] = jnp.sum(e * xhat, axis=0, keepdims=True)
        vout[1:2, :] = jnp.sum(e, axis=0, keepdims=True)
        vout[2:3, :] = jnp.sum(gj[:, 0:D].astype(f32), axis=0, keepdims=True)
        vout[3:4, :] = jnp.sum(gj[:, 2 * D :].astype(f32), axis=0, keepdims=True)
        vout[4:5, :] = jnp.sum(gb[...].astype(f32), axis=0, keepdims=True)
        gh[...] = (ga[...] + norm_back(e, xhat, rstd, vec[0:1, :])).astype(gh.dtype)
        c.out(gh, o_gh)
        c.out(vout, o_vec)
        c.finish()


def backward_attn(side, ga, x, clip, vec, qkv, lt, wm, wj, gh_type, old=None):
    extra = 0 if old is None else 3
    outs = (((L, D), bf), ((L, 3 * D), bf), ((L, D), gh_type), ((8, D), f32))
    sc = [((L, D), f32), ((L, D), x.dtype), ((L, 3 * D), bf), ((16, L), f32), (wm.shape, bf), (wj.shape, bf), ((L, D), bf)]
    return pl.pallas_call(
        functools.partial(attn_back, clip, extra),
        out_shape=shapes(outs),
        in_specs=[SM, ANY, ANY, VM] + [ANY] * (4 + extra),
        out_specs=[ANY] * 4,
        scratch_shapes=scratch(sc + list(outs)) + [pltpu.SemaphoreType.DMA((16,))],
        input_output_aliases=dict(zip(range(8, 8 + extra), (0, 1, 3))),
        compiler_params=PARAMS,
        cost_estimate=pl.CostEstimate(flops=4_400_000_000, bytes_accessed=20_000_000, transcendentals=3_000_000),
    )(side, ga, x, vec, qkv, lt, wm, wj, *(old or ()))


def weight_grad(pieces, a0, b0, a1, b1, o_ref, a, b, o, sems):
    c = Copies(sems)
    waits = [c.start(src, dst) for src, dst in ((a0, a.at[0:L]), (a1, a.at[L:]), (b0, b.at[0:L]), (b1, b.at[L:]))]
    for w in waits:
        w.wait()
    rows, cols = o.shape
    if rows > D:
        for j in range(rows // D):
            s = slice(j * D, (j + 1) * D)
            o[s, :] = mm(a[:, s], b[...], 0, 0).astype(bf)
            c.out(o.at[s], o_ref.at[s])
    else:
        for j in range(cols // D):
            s = slice(j * D, (j + 1) * D)
            o[:, s] = mm(a[...], b[:, s], 0, 0).astype(bf)
            c.out(o.at[:, s], o_ref.at[:, s])
    c.finish()


def weight_gradient(a0, b0, a1, b1):
    m, n = a0.shape[1], b0.shape[1]
    return pl.pallas_call(
        functools.partial(weight_grad, None),
        out_shape=jax.ShapeDtypeStruct((m, n), bf),
        in_specs=[ANY] * 4,
        out_specs=ANY,
        scratch_shapes=scratch([((2 * L, m), bf), ((2 * L, n), bf), ((m, n), bf)]) + [pltpu.SemaphoreType.DMA((16,))],
        compiler_params=PARAMS,
        cost_estimate=pl.CostEstimate(flops=4 * L * m * n, bytes_accessed=2 * (2 * L * (m + n) + m * n), transcendentals=0),
    )(a0, b0, a1, b1)


def passed_along(block, distance):
    devices = range(lax.axis_size("section"))
    route = [(i - distance, i) for i in devices if i - distance in devices]
    return lax.ppermute(block, "section", route)


def scatter(values):
    return lax.psum_scatter(values, "batch", scatter_dimension=0, tiled=True)


def shards(clips, mask_flags, mask_embed, pos_embed, first_gain, first_shift, joint_weight, query_bias, value_bias,
           mixer_weight, mixer_bias, second_gain, second_shift, up_weight, up_bias, down_weight, down_bias, out_grad):
    first = lax.axis_index("section") == 0
    lead = first.astype(jnp.int32).reshape(1)
    tail = 1 - lead
    count = lax.axis_size("batch")
    keep = mask_flags.astype(f32)[..., None]
    blended = clips.astype(f32) * (1.0 - keep) + keep * mask_embed + pos_embed
    vec = jnp.concatenate([first_gain, first_shift, query_bias, value_bias, mixer_bias, second_gain, second_shift, down_bias])
    wj, wm, wu, wd = joint_weight[0], mixer_weight[0], up_weight[0], down_weight[0]
    weights = (wj, wm, wu, wd)

    lead0 = forward(lead, blended, 0, vec, up_bias, weights)
    arriving0 = passed_along(lead0[8], 1)
    lead1 = forward(lead, blended, 1, vec, up_bias, weights)
    arriving1 = passed_along(lead1[8], 1)

    def back(side, saved, g, g_clip, x, x_clip, gh_type, old):
        n1, qkv, lt, mixed, after, n2, act, slope, out = saved
        gl, ga, vm = backward_mlp(side, g, g_clip, vec, slope, after, wu, wd, old and old[:3])
        gb, gj, gh, va = backward_attn(side, ga, x, x_clip, vec, qkv, lt, wm, wj, gh_type, old and old[3:])
        return (gl, ga, vm, gb, gj, va), gh

    saved0 = forward(tail, arriving0, None, vec, up_bias, weights, lead0)
    grads0, back0 = back(tail, saved0, out_grad, 0, arriving0, None, bf, None)
    leaving0 = passed_along(back0, -1)
    saved1 = forward(tail, arriving1, None, vec, up_bias, weights, lead1)
    grads1, back1 = back(tail, saved1, out_grad, 1, arriving1, None, bf, None)
    leaving1 = passed_along(back1, -1)
    grads0, blend0 = back(lead, saved0, leaving0, None, blended, 0, f32, grads0)
    g0 = jnp.where(first, leaving0, out_grad[0])
    g1 = jnp.where(first, leaving1, out_grad[1])
    grads1, blend1 = back(lead, saved1, leaving1, None, blended, 1, f32, grads1)

    def pair(i, j):
        return [(a, b) for a, b in ((saved0[i], grads0[j]), (saved1[i], grads1[j]))]

    down = weight_gradient(saved0[6], g0, saved1[6], g1)
    up = weight_gradient(saved0[5], grads0[0], saved1[5], grads1[0])
    joint = weight_gradient(saved0[0], grads0[4], saved1[0], grads1[4])
    mixer = weight_gradient(saved0[3], grads0[3], saved1[3], grads1[3])
    down, up, joint, mixer = [scatter(one).astype(f32)[None] for one in (down, up, joint, mixer)]

    vm = grads0[2] + grads1[2]
    va = grads0[5] + grads1[5]
    columns = [vm[0], vm[1, :D], vm[1, D : 2 * D], vm[1, 2 * D : 3 * D]] + [va[i] for i in range(5)]
    packed = scatter(jnp.concatenate([one.reshape(count, -1) for one in columns], axis=1))
    pieces, at = [], 0
    for one in columns:
        width = one.shape[0] // count
        pieces.append(packed[:, at : at + width])
        at += width
    g_ub, g_gain2, g_shift2, g_db, g_gain1, g_shift1, g_qb, g_vb, g_mb = pieces

    layer_outputs = jnp.stack([saved0[8], saved1[8]])[None]
    blend = jnp.stack([blend0, blend1])
    input_grads = jnp.where(first, blend * (1.0 - keep), jnp.stack([back0, back1]).astype(f32)).astype(bf)[None]
    position = jnp.where(first, blend0 + blend1, 0.0)
    masked = jnp.sum(jnp.where(first, blend * keep, 0.0), axis=(0, 1))
    half = L // 2
    sent_position = passed_along(position[half:].astype(bf), 1).astype(f32)
    sent_masked = passed_along(masked[D // 2 :], 1)
    position = jnp.where(first, position[:half], sent_position)
    masked = jnp.where(first, masked[: D // 2], sent_masked)
    grad_mask, grad_position = lax.psum((masked, position), "batch")
    return (layer_outputs, input_grads, g_gain1, g_shift1, joint, g_qb, g_vb, mixer, g_mb, g_gain2, g_shift2, up, g_ub,
            down, g_db, grad_mask, grad_position)


def solution(mesh):
    whole, section, both = P(), P("section"), P("section", "batch")
    in_specs = (P("batch"), P("batch"), whole, whole) + (section,) * 13 + (P("batch"),)
    out_specs = (both,) * 15 + (section, section)
    return jax.shard_map(shards, mesh=mesh, in_specs=in_specs, out_specs=out_specs, check_vma=False)
```

time: 1080 us -> 643 us (0.60)
  matrix products: 253 us -> 0 us
  Pallas kernels: 0 us -> 185 us
  other arithmetic: 149 us -> 21.5 us
  waiting for transfers between devices: 452 us -> 328 us
  local copies, waits for them, and re-layouts: 73.4 us -> 18.6 us
  loops' own time: 38.5 us -> 0 us
  blocking collectives: 77.6 us -> 61.1 us
    dot_general x38 -> x0, matrix products: 253 us -> none  [the longest x8 55.2 us: contract_rows(): lax.dot_general(left, right, (((0,), (0,)), ((), ())), preferred_element_...]
    pallas_call x0 -> x16, Pallas kernels: none -> 185 us  [the longest x4 82.3 us: forward(): pl.pallas_call(functools.partial(front, clip, extra), out_shape=shapes(SA...]
    ppermute x4 -> x6, waiting for transfers between devices: 179 us -> 66.5 us  [passed_along(): return lax.ppermute(block, 'section', route)]
    reduce_scatter x5 -> x4, waiting for transfers between devices: 273 us -> 167 us  [scatter(): return lax.psum_scatter(values, 'batch', scatter_dimension=0, tiled=True)]
    psum x0 -> x1, waiting for transfers between devices: none -> 93.9 us  [shards(): grad_mask, grad_position = lax.psum((masked, position), 'batch')]
    add x12 -> x3, other arithmetic: 48.5 us -> 4.22 us  [the longest x1 4.2 us: shards(): blended = clips.astype(f32) * (1.0 - keep) + keep * mask_embed + pos_embed]
    reduce_sum x26 -> x1, other arithmetic: 38.6 us -> 0.38 us  [shards(): masked = jnp.sum(jnp.where(first, blend * keep, 0.0), axis=(0, 1))]
    another operation x5 -> x0, loops' own time: 29.4 us -> none  [the longest x3 20.1 us: shards(): lax.cond(first_section, lead_backward, tail_backward)]
  transfers between devices with their start and end apart: 9 -> 11, of which waited for: 6 -> 7; matrix products, arithmetic and copies ran while one was open for 7% -> 4% of each run, Pallas kernels for 0% -> 19%
where the time goes in v1:
time: 643 us; the launch traced here: 638 us
  waiting for transfers between devices  328 us (51%)
  Pallas kernels  185 us (29%)
  blocking collectives  61.1 us (10%)
  other arithmetic  21.5 us (3%)
  local copies, waits for them, and re-layouts  18.6 us (3%)
  between operations  14.5 us (2%)
  starting transfers between devices  9.7 us (2%)
    reduce_scatter x4, waiting for transfers between devices, scatter(): return lax.psum_scatter(values, 'batch', scatter_dimension=0, tiled=True)  167 us
    psum x1, waiting for transfers between devices, shards(): grad_mask, grad_position = lax.psum((masked, position), 'batch')  93.9 us
    pallas_call x4, Pallas kernels, forward(): pl.pallas_call(functools.partial(front, clip, extra), out_shape=shapes(SA...  82.3 us
    ppermute x6, waiting for transfers between devices, passed_along(): return lax.ppermute(block, 'section', route)  66.5 us
    unnamed x1, blocking collectives  61.1 us
    pallas_call x4, Pallas kernels, backward_attn(): pl.pallas_call(functools.partial(attn_back, clip, extra), out_shape=shape...  42.4 us
    pallas_call x4, Pallas kernels, weight_gradient(): pl.pallas_call(functools.partial(weight_grad, None), out_shape=jax.ShapeD...  31.9 us
    pallas_call x4, Pallas kernels, backward_mlp(): pl.pallas_call(functools.partial(mlp_back, clip, extra), out_shape=shapes...  28.5 us
  transfers between devices with their start and end apart: 11, of which 7 were waited for; matrix products, arithmetic and copies ran while one was open for 4% of the time, Pallas kernels for 19%

profile of v1, /device:TPU:0, one launch (start us, length us, event | category | flops | bytes accessed | tf_op | source)
XLA Modules:
  0.0 638.0 jit_solution(9412150251983690050)
XLA Ops:
  7.2 0.7 broadcast_subtract_fusion
  7.9 0.7 convert_element_type.36
  8.7 4.2 add_add_fusion.x_in
  13.0 0.6 concatenate.20.vec
  13.6 28.0 %shard_map.305 = (bf16[512,768]{1,0:T(8,128)(2,1)}, bf16[512,2304]{1,0:T(8,128)(2,1)}, f32[16,512]{1,0:T(8,128)}, bf16[512,768]{1,0:T(8,128)(2,1)}, f32[512,768]...) custom-call(s32[1]{0:T(128)} %bitcast.side, ...), custom_call_target="tpu_custom_call" | custom-call | flops 8049999872 | bytes 30000000 | tf_op jit(solution)/shard_map/pallas_call | solution.py:156
  41.6 1.3 collective-permute-start
  43.0 27.6 %shard_map.307 = (bf16[512,768]{1,0:T(8,128)(2,1)}, bf16[512,2304]{1,0:T(8,128)(2,1)}, f32[16,512]{1,0:T(8,128)}, bf16[512,768]{1,0:T(8,128)(2,1)}, f32[512,768]...) custom-call(s32[1]{0:T(128)} %bitcast.side, ...), custom_call_target="tpu_custom_call" | custom-call | flops 8049999872 | bytes 30000000 | tf_op jit(solution)/shard_map/pallas_call | solution.py:156
  70.6 1.3 collective-permute-start.1
  72.0 0.9 copy-done.24
  72.9 13.4 %shard_map.306 = (bf16[512,768]{1,0:T(8,128)(2,1)}, bf16[512,2304]{1,0:T(8,128)(2,1)}, f32[16,512]{1,0:T(8,128)}, bf16[512,768]{1,0:T(8,128)(2,1)}, f32[512,768]...) custom-call(s32[1]{0:T(128)S(6)} %sub.8.side, ...), custom_call_target="tpu_custom_call", output_to_operand_aliasing={{0}: (8, {}), {1}: (9, {}), {2}: (10, {}), {3}: (11, {}), {... | custom-call | flops 8049999872 | bytes 30000000 | tf_op jit(solution)/shard_map/pallas_call | solution.py:156
  86.3 0.9 shard_map.309
  87.2 0.9 shard_map.310
  88.1 1.3 collective-permute-start.2
  89.4 0.5 collective-permute-done.1.x_in
  89.9 0.9 copy-done.23
  90.8 13.2 %shard_map.308 = (bf16[512,768]{1,0:T(8,128)(2,1)}, bf16[512,2304]{1,0:T(8,128)(2,1)}, f32[16,512]{1,0:T(8,128)}, bf16[512,768]{1,0:T(8,128)(2,1)}, f32[512,768]...) custom-call(s32[1]{0:T(128)S(6)} %sub.8.side, ...), custom_call_target="tpu_custom_call", output_to_operand_aliasing={{0}: (8, {}), {1}: (9, {}), {2}: (10, {}), {3}: (11, {}), {... | custom-call | flops 8049999872 | bytes 30000000 | tf_op jit(solution)/shard_map/pallas_call | solution.py:156
  104.0 0.9 shard_map.313
  104.9 0.9 shard_map.314
  105.8 1.3 collective-permute-start.3
  107.1 37.2 %collective-permute-done.2.g_in = bf16[512,768]{1,0:T(8,128)(2,1)S(1)} collective-permute-done((bf16[512,768]{1,0:T(8,128)(2,1)}, bf16[512,768]{1,0:T(8,128)(2,1)S(1)}, u32[]{:S(2)}, u32[]{:S(2)}) %collective-permute-start.2) | collective-permute-done | bytes 786464 | tf_op jit(solution)/shard_map/ppermute | solution.py:330
  144.3 0.9 copy-done.3
  145.2 13.2 %shard_map.311 = (bf16[512,3072]{1,0:T(8,128)(2,1)}, f32[512,768]{1,0:T(8,128)}, f32[8,3072]{1,0:T(8,128)}) custom-call(s32[1]{0:T(128)} %bitcast.side, bf16[512,768]{1,0:T(8,128)(2,1)} %copy-done.3, f32[8,768]{1,0:T(8,128)} %concatenate.20.vec, ...), custom_call_target="tpu_custom_call", output_to_operand_aliasing={{0}: (7, {}), {1}: (8, {}), {2}: (9, {})} | custom-call | flops 4830000128 | bytes 20000000 | tf_op jit(solution)/shard_map/pallas_call | solution.py:209
  158.4 20.3 %shard_map.312 = (bf16[512,768]{1,0:T(8,128)(2,1)}, bf16[512,2304]{1,0:T(8,128)(2,1)}, f32[512,768]{1,0:T(8,128)}, f32[8,768]{1,0:T(8,128)}) custom-call(s32[1]{0:T(128)} %bitcast.side, f32[512,768]{1,0:T(8,128)} %get-tuple-element.109.ga_in, f32[2,512,768]{2,1,0:T(8,128)} %add_add_fusion.x_in, ...), custom_call_target="tpu_custom_call", output_to_operand_aliasing={{0}: (8, {}), {1}: (9, {}), {3}: (10, {})} | custom-call | flops 4400000000 | bytes 20000000 | tf_op jit(solution)/shard_map/pallas_call | solution.py:283
  178.7 28.8 %collective-permute-done.3.g_in = bf16[512,768]{1,0:T(8,128)(2,1)S(1)} collective-permute-done((bf16[512,768]{1,0:T(8,128)(2,1)}, bf16[512,768]{1,0:T(8,128)(2,1)S(1)}, u32[]{:S(2)}, u32[]{:S(2)}) %collective-permute-start.3) | collective-permute-done | bytes 786464 | tf_op jit(solution)/shard_map/ppermute | solution.py:330
  207.5 0.9 copy-done.5
  208.4 13.5 %shard_map.315 = (bf16[512,3072]{1,0:T(8,128)(2,1)}, f32[512,768]{1,0:T(8,128)}, f32[8,3072]{1,0:T(8,128)}) custom-call(s32[1]{0:T(128)} %bitcast.side, bf16[512,768]{1,0:T(8,128)(2,1)} %copy-done.5, f32[8,768]{1,0:T(8,128)} %concatenate.20.vec, ...), custom_call_target="tpu_custom_call", output_to_operand_aliasing={{0}: (7, {}), {1}: (8, {}), {2}: (9, {})} | custom-call | flops 4830000128 | bytes 20000000 | tf_op jit(solution)/shard_map/pallas_call | solution.py:209
  221.9 20.3 %shard_map.316 = (bf16[512,768]{1,0:T(8,128)(2,1)}, bf16[512,2304]{1,0:T(8,128)(2,1)}, f32[512,768]{1,0:T(8,128)}, f32[8,768]{1,0:T(8,128)}) custom-call(s32[1]{0:T(128)} %bitcast.side, f32[512,768]{1,0:T(8,128)} %get-tuple-element.122.ga_in, f32[2,512,768]{2,1,0:T(8,128)} %add_add_fusion.x_in, ...), custom_call_target="tpu_custom_call", output_to_operand_aliasing={{0}: (8, {}), {1}: (9, {}), {3}: (10, {})} | custom-call | flops 4400000000 | bytes 20000000 | tf_op jit(solution)/shard_map/pallas_call | solution.py:283
  242.2 4.4 shard_map.318
  246.9 8.1 %shard_map.317 = bf16[768,2304]{1,0:T(8,128)(2,1)} custom-call(bf16[512,768]{1,0:T(8,128)(2,1)} %get-tuple-element.131.a0, bf16[512,2304]{1,0:T(8,128)(2,1)} %get-tuple-element.132.b0, bf16[512,768]{1,0:T(8,128)(2,1)} %get-tuple-element.133.a1, bf16[512,2304]{1,0:T(8,128)(2,1)} %get-tuple-element.134.b1), custom_call_target="tpu_custom_call" | custom-call | flops 3623878656 | bytes 9830400 | tf_op jit(solution)/shard_map/pallas_call | solution.py:316
  255.0 9.9 %shard_map.319 = bf16[768,3072]{1,0:T(8,128)(2,1)} custom-call(bf16[512,768]{1,0:T(8,128)(2,1)} %get-tuple-element.139.a0, bf16[512,3072]{1,0:T(8,128)(2,1)} %get-tuple-element.140.b0, bf16[512,768]{1,0:T(8,128)(2,1)} %get-tuple-element.141.a1, bf16[512,3072]{1,0:T(8,128)(2,1)} %get-tuple-element.142.b1), custom_call_target="tpu_custom_call" | custom-call | flops 4831838208 | bytes 12582912 | tf_op jit(solution)/shard_map/pallas_call | solution.py:316
  265.0 1.0 copy-done.4
  266.0 0.2 copy-done.6
  266.3 0.5 copy-done.7
  266.8 1.3 bitcast_select_fusion
  268.1 9.5 %shard_map.320 = bf16[3072,768]{1,0:T(8,128)(2,1)} custom-call(bf16[512,3072]{1,0:T(8,128)(2,1)} %get-tuple-element.143.a0, bf16[512,768]{1,0:T(8,128)(2,1)} %get-tuple-element.156.b0, bf16[512,3072]{1,0:T(8,128)(2,1)} %get-tuple-element.144.a1, bf16[512,768]{1,0:T(8,128)(2,1)} %get-tuple-element.155.b1), custom_call_target="tpu_custom_call" | custom-call | flops 4831838208 | bytes 12582912 | tf_op jit(solution)/shard_map/pallas_call | solution.py:316
  277.8 0.5 copy-done.25
  278.3 0.6 dynamic-slice
  278.9 2.7 maximum_bitcast_fusion
  281.8 1.1 copy-done.2
  283.0 2.2 collective-permute-start.5
  285.2 0.4 fusion.3
  285.6 0.6 slice.94
  286.2 1.9 collective-permute-start.4
  288.1 0.6 slice_reduce_fusion.1
  288.8 1.6 fusion.1
  290.4 0.8 reshape_squeeze.31
  291.2 0.8 reshape_squeeze.32
  292.0 0.8 reshape_squeeze.33
  292.7 0.8 reshape_squeeze.34
  293.5 0.8 reshape_squeeze.35
  294.7 0.7 slice_select_fusion.1
  295.4 61.1 %all-reduce.1 = (f32[16,576]{1,0:T(8,128)S(1)}, f32[384]{0:T(512)}) all-reduce(f32[16,576]{1,0:T(8,128)S(1)} %concatenate.21, f32[384]{0:T(512)S(1)} %slice_select_fusion.1), channel_id=2, replica_groups=mesh['section'=2,'batch'=16] {'batch'}, use_global_device_ids=true, to_apply=%region_0.1.clone | all-reduce | flops 9600 | bytes 76800
  356.5 1.2 constant_dynamic-slice_fusion
  357.7 1.3 fusion.4
  359.0 2.2 slice_select_fusion
  361.2 1.6 bitcast_convert_fusion.3
  362.8 14.0 %reduce-scatter.5.cloned.1.call-done = bf16[48,2304]{1,0:T(8,128)(2,1)} async-done(((bf16[768,2304]{1,0:T(8,128)(2,1)}), bf16[48,2304]{1,0:T(8,128)(2,1)}) %reduce-scatter.5.cloned.1.call-update) | async-done | bytes 221200 | tf_op jit(solution)/shard_map/reduce_scatter | solution.py:334
  376.8 1.7 bitcast_convert_fusion.2
  378.5 76.5 %reduce-scatter.9.cloned.1.call-done = bf16[48,3072]{1,0:T(8,128)(2,1)} async-done(((bf16[768,3072]{1,0:T(8,128)(2,1)}), bf16[48,3072]{1,0:T(8,128)(2,1)}) %reduce-scatter.9.cloned.1.call-update) | async-done | bytes 294928 | tf_op jit(solution)/shard_map/reduce_scatter | solution.py:334
  455.1 1.8 bitcast_convert_fusion.1
  456.9 76.6 %reduce-scatter.11.cloned.1.call-done = bf16[192,768]{1,0:T(8,128)(2,1)} async-done(((bf16[3072,768]{1,0:T(8,128)(2,1)}), bf16[192,768]{1,0:T(8,128)(2,1)}) %reduce-scatter.11.cloned.1.call-update) | async-done | bytes 294928 | tf_op jit(solution)/shard_map/reduce_scatter | solution.py:334
  533.5 1.8 bitcast_convert_fusion
  535.3 93.9 %all-reduce.4.cloned.1.call-done = f32[256,768]{1,0:T(8,128)} async-done(((f32[256,768]{1,0:T(8,128)}), f32[256,768]{1,0:T(8,128)}) %all-reduce.4.cloned.1.call-update) | async-done | bytes 786448 | tf_op jit(solution)/shard_map/psum | solution.py:401
  629.2 2.1 copy.96
  (68 shorter events, 1.3 us)
Async XLA Ops:
  7.2 354.0 %reduce-scatter.7.cloned.1.call-start = ((), (), s32[]{:S(2)}) async-start(), calls=%async_computation.5 | async-start | bytes 1253376 | tf_op jit(solution)/shard_map/reduce_scatter | solution.py:334
  8.6 4.3 copy-start.15
  8.6 4.3 copy-start.16
  8.6 4.3 copy-start.17
  8.6 4.3 copy-start.18
  8.6 4.3 copy-start.19
  8.7 4.3 copy-start.20
  8.7 4.3 copy-start.21
  8.7 4.3 copy-start.22
  41.6 30.3 %collective-permute-start = (bf16[512,768]{1,0:T(8,128)(2,1)}, bf16[512,768]{1,0:T(8,128)(2,1)S(1)}, u32[]{:S(2)}, u32[]{:S(2)}) collective-permute-start(bf16[512,768]{1,0:T(8,128)(2,1)} %get-tuple-element.81.rest_8_), channel_id=1, source_target_pairs={{0,16},{1,17},{2,18},{3,19},{4,20},{5,21},{6,22},{7,23},{8,24},{9,... | collective-permute-start | bytes 2359304 | tf_op jit(solution)/shard_map/ppermute | solution.py:330
  70.6 19.3 %collective-permute-start.1 = (bf16[512,768]{1,0:T(8,128)(2,1)}, bf16[512,768]{1,0:T(8,128)(2,1)S(1)}, u32[]{:S(2)}, u32[]{:S(2)}) collective-permute-start(bf16[512,768]{1,0:T(8,128)(2,1)} %get-tuple-element.91.rest_8_), channel_id=1, source_target_pairs={{0,16},{1,17},{2,18},{3,19},{4,20},{5,21},{6,22},{7,23},{8,24},{9,... | collective-permute-start | bytes 2359304 | tf_op jit(solution)/shard_map/ppermute | solution.py:330
  72.0 0.9 copy-start.24
  88.1 56.2 %collective-permute-start.2 = (bf16[512,768]{1,0:T(8,128)(2,1)}, bf16[512,768]{1,0:T(8,128)(2,1)S(1)}, u32[]{:S(2)}, u32[]{:S(2)}) collective-permute-start(bf16[512,768]{1,0:T(8,128)(2,1)} %get-tuple-element.106), channel_id=1, source_target_pairs={{16,0},{17,1},{18,2},{19,3},{20,4},{21,5},{22,6},{23,7},{24,8},{25... | collective-permute-start | bytes 2359304 | tf_op jit(solution)/shard_map/ppermute | solution.py:330
  89.9 0.9 copy-start.23
  105.8 101.7 %collective-permute-start.3 = (bf16[512,768]{1,0:T(8,128)(2,1)}, bf16[512,768]{1,0:T(8,128)(2,1)S(1)}, u32[]{:S(2)}, u32[]{:S(2)}) collective-permute-start(bf16[512,768]{1,0:T(8,128)(2,1)} %get-tuple-element.119), channel_id=1, source_target_pairs={{16,0},{17,1},{18,2},{19,3},{20,4},{21,5},{22,6},{23,7},{24,8},{25... | collective-permute-start | bytes 2359304 | tf_op jit(solution)/shard_map/ppermute | solution.py:330
  144.3 0.9 copy-start.3
  207.5 0.9 copy-start.5
  246.7 130.1 %reduce-scatter.5.cloned.1.call-start = ((), (), s32[]{:S(2)}) async-start(), calls=%async_computation.4 | async-start | bytes 3760128 | tf_op jit(solution)/shard_map/reduce_scatter | solution.py:334
  255.0 200.1 %reduce-scatter.9.cloned.1.call-start = ((), (), s32[]{:S(2)}) async-start(), calls=%async_computation.6 | async-start | bytes 5013504 | tf_op jit(solution)/shard_map/reduce_scatter | solution.py:334
  264.9 1.1 copy-start.4
  264.9 1.4 copy-start.6
  264.9 1.9 copy-start.7
  265.0 268.6 %reduce-scatter.11.cloned.1.call-start = ((), (), s32[]{:S(2)}) async-start(), calls=%async_computation.7 | async-start | bytes 5013504 | tf_op jit(solution)/shard_map/reduce_scatter | solution.py:334
  277.6 0.7 copy-start.25
  277.7 3.9 copy-start
  277.7 3.9 copy-start.1
  277.7 351.5 %all-reduce.4.cloned.1.call-start = ((), (), s32[]{:S(2)}) async-start(), calls=%async_computation.8 | async-start | bytes 1572864 | tf_op jit(solution)/shard_map/psum | solution.py:401
  281.8 1.1 copy-start.2
  283.0 5.1 copy-start.12
  283.0 5.1 copy-start.13
  283.0 5.1 copy-start.10
  283.0 5.1 copy-start.11
  283.0 5.8 copy-start.8
  283.0 5.8 copy-start.9
  283.0 76.0 %collective-permute-start.5 = (bf16[256,768]{1,0:T(8,128)(2,1)S(1)}, bf16[256,768]{1,0:T(8,128)(2,1)}, u32[]{:S(2)}, u32[]{:S(2)}) collective-permute-start(bf16[256,768]{1,0:T(8,128)(2,1)S(1)} %slice.122), channel_id=1, source_target_pairs={{0,16},{1,17},{2,18},{3,19},{4,20},{5,21},{6,22},{7,23},{8,24},{9,... | collective-permute-start | bytes 1179656 | tf_op jit(solution)/shard_map/ppermute | solution.py:330
  285.6 2.5 copy-start.14
  286.2 8.4 %collective-permute-start.4 = (f32[384]{0:T(512)}, f32[384]{0:T(512)}, u32[]{:S(2)}, u32[]{:S(2)}) collective-permute-start(f32[384]{0:T(512)} %slice.94), channel_id=1, source_target_pairs={{0,16},{1,17},{2,18},{3,19},{4,20},{5,21},{6,22},{7,23},{8,24},{9,... | collective-permute-start | bytes 4616 | tf_op jit(solution)/shard_map/ppermute | solution.py:330
Sparse Core Ops, SparseCore 0:
  246.8 58.6 reduce-scatter.6
  309.3 67.4 reduce-scatter.4
  380.7 74.3 reduce-scatter.8
  458.8 74.7 reduce-scatter.10
  537.3 91.8 all-reduce.3

commit v2 on v1

--- a/solution.py
+++ b/solution.py
@@ -5,6 +5,7 @@
 from jax.experimental import pallas as pl
 from jax.experimental.pallas import tpu as pltpu
 from jax.sharding import PartitionSpec as P
+
 D, HEADS, HD, FF, L = 768, 12, 64, 3072, 512
 bf, f32 = jnp.bfloat16, jnp.float32
 LOG2E = 1.4426950408889634
@@ -218,9 +219,12 @@
     )(side, g, vec, slope, after, wu, wd, *(old or ()))
 
 
-def attn_back(clip, extra, side, ga_in, x_in, vec, qkv_in, lt_in, wm_in, wj_in, *rest):
+def attn_back(clip, lead, extra, side, ga_in, x_in, vec, flags, qkv_in, lt_in, wm_in, wj_in, *rest):
     o_gb, o_gj, o_gh, o_vec = rest[extra : extra + 4]
-    ga, x, qkv, lt, wm, wj, gm, gb, gj, gh, vout, sems = rest[extra + 4 :]
+    rest = rest[extra + 4 :]
+    if lead:
+        o_full, full, rest = rest[0], rest[-2], rest[1:-2] + rest[-1:]
+    ga, x, qkv, lt, wm, wj, gm, gb, gj, gh, vout, sems = rest
 
     @pl.when(side[0] != 0)
     def _():
@@ -270,29 +274,38 @@
         vout[2:3, :] = jnp.sum(gj[:, 0:D].astype(f32), axis=0, keepdims=True)
         vout[3:4, :] = jnp.sum(gj[:, 2 * D :].astype(f32), axis=0, keepdims=True)
         vout[4:5, :] = jnp.sum(gb[...].astype(f32), axis=0, keepdims=True)
-        gh[...] = (ga[...] + norm_back(e, xhat, rstd, vec[0:1, :])).astype(gh.dtype)
+        whole = ga[...] + norm_back(e, xhat, rstd, vec[0:1, :])
+        if lead:
+            free = whole * (1.0 - flags[clip].astype(f32))
+            full[...] = whole
+            c.out(full, o_full)
+            vout[5:6, :] = jnp.sum(whole - free, axis=0, keepdims=True)
+            whole = free
+        gh[...] = whole.astype(bf)
         c.out(gh, o_gh)
         c.out(vout, o_vec)
         c.finish()
 
 
-def backward_attn(side, ga, x, clip, vec, qkv, lt, wm, wj, gh_type, old=None):
-    extra = 0 if old is None else 3
-    outs = (((L, D), bf), ((L, 3 * D), bf), ((L, D), gh_type), ((8, D), f32))
+def backward_attn(side, ga, x, clip, vec, flags, qkv, lt, wm, wj, old=None):
+    lead = old is not None
+    extra = 4 if lead else 0
+    outs = (((L, D), bf), ((L, 3 * D), bf), ((L, D), bf), ((8, D), f32))
+    full = (((L, D), f32),) if lead else ()
     sc = [((L, D), f32), ((L, D), x.dtype), ((L, 3 * D), bf), ((16, L), f32), (wm.shape, bf), (wj.shape, bf), ((L, D), bf)]
     return pl.pallas_call(
-        functools.partial(attn_back, clip, extra),
-        out_shape=shapes(outs),
-        in_specs=[SM, ANY, ANY, VM] + [ANY] * (4 + extra),
-        out_specs=[ANY] * 4,
-        scratch_shapes=scratch(sc + list(outs)) + [pltpu.SemaphoreType.DMA((16,))],
-        input_output_aliases=dict(zip(range(8, 8 + extra), (0, 1, 3))),
+        functools.partial(attn_back, clip, lead, extra),
+        out_shape=shapes(outs + full),
+        in_specs=[SM, ANY, ANY, VM, VM] + [ANY] * (4 + extra),
+        out_specs=[ANY] * (4 + lead),
+        scratch_shapes=scratch(sc + list(outs + full)) + [pltpu.SemaphoreType.DMA((16,))],
+        input_output_aliases={9 + i: i for i in range(extra)},
         compiler_params=PARAMS,
         cost_estimate=pl.CostEstimate(flops=4_400_000_000, bytes_accessed=20_000_000, transcendentals=3_000_000),
-    )(side, ga, x, vec, qkv, lt, wm, wj, *(old or ()))
-
-
-def weight_grad(pieces, a0, b0, a1, b1, o_ref, a, b, o, sems):
+    )(side, ga, x, vec, flags, qkv, lt, wm, wj, *(old or ()))
+
+
+def weight_grad(a0, b0, a1, b1, o_ref, a, b, o, sems):
     c = Copies(sems)
     waits = [c.start(src, dst) for src, dst in ((a0, a.at[0:L]), (a1, a.at[L:]), (b0, b.at[0:L]), (b1, b.at[L:]))]
     for w in waits:
@@ -314,7 +327,7 @@
 def weight_gradient(a0, b0, a1, b1):
     m, n = a0.shape[1], b0.shape[1]
     return pl.pallas_call(
-        functools.partial(weight_grad, None),
+        weight_grad,
         out_shape=jax.ShapeDtypeStruct((m, n), bf),
         in_specs=[ANY] * 4,
         out_specs=ANY,
@@ -332,6 +345,255 @@
 
 def scatter(values):
     return lax.psum_scatter(values, "batch", scatter_dimension=0, tiled=True)
+
+
+def split_grad(kind, count, part, *refs):
+    ins, (keep, send), (a, b, o, sems) = refs[:-6], refs[-6:-4], refs[-4:]
+    c = Copies(sems)
+    mine = part[0]
+
+    def load(pairs):
+        return [c.start(src, dst) for src, dst in pairs]
+
+    if kind == "down":
+        a0, b0, a1, b1, other = ins
+        waits = load(((a0, a.at[0:L]), (a1, a.at[L:])))
+        rows = (b.at[0:L], b.at[L:])
+
+        @pl.when(part[1] != 0)
+        def _():
+            for src, dst, sem in zip((b0, b1), rows, (18, 19)):
+                pltpu.make_async_copy(src, dst, sems.at[sem]).start()
+
+        @pl.when(part[1] == 0)
+        def _():
+            for at, dst, sem in zip((0, 1), rows, (18, 19)):
+                pltpu.make_async_copy(other.at[at], dst, sems.at[sem]).start()
+
+        for src, dst, sem in zip((b0, b1), rows, (18, 19)):
+            pltpu.make_async_copy(src, dst, sems.at[sem]).wait()
+        for w in waits:
+            w.wait()
+        height = FF // count
+        per = D // height // 2
+        for j in range(FF // D):
+            tile = mm(a[:, j * D : (j + 1) * D], b[...], 0, 0).astype(bf)
+            for i in range(2 * per):
+                o[i % 2, j * per + i // 2] = tile[i * height : (i + 1) * height]
+            s = slice(j * per, (j + 1) * per)
+            c.out(o.at[mine, s], keep.at[s])
+            c.out(o.at[1 - mine, s], send.at[s])
+    else:
+        height = D // count
+        groups = [ins[i : i + 4] for i in range(0, len(ins), 4)]
+        loads = []
+        column = 0
+        for g, (a0, b0, a1, b1) in enumerate(groups):
+            width = b0.shape[1]
+            r = slice(column, column + width)
+            l = slice(g * D, (g + 1) * D)
+            loads.append(load(((a0, a.at[0:L, l]), (a1, a.at[L:, l]), (b0, b.at[0:L, r]), (b1, b.at[L:, r]))))
+            column += width
+        t = 0
+        for g, (a0, b0, a1, b1) in enumerate(groups):
+            for w in loads[g]:
+                w.wait()
+            for _ in range(b0.shape[1] // D):
+                tile = mm(a[:, g * D : (g + 1) * D], b[:, t * D : (t + 1) * D], 0, 0).astype(bf)
+                for i in range(count):
+                    o[i % 2, i // 2, t * height : (t + 1) * height] = tile[i * height : (i + 1) * height]
+                t += 1
+        c.out(o.at[mine], keep)
+        c.out(o.at[1 - mine], send)
+    c.finish()
+
+
+def split_gradient(kind, count, part, groups):
+    flat = [one for group in groups for one in group]
+    pairs = groups if kind == "both" else groups[:1]
+    m = sum(group[0].shape[1] for group in pairs)
+    n = sum(group[1].shape[1] for group in pairs)
+    half = jax.ShapeDtypeStruct((count // 2, 4 * D // count, D), bf)
+    return pl.pallas_call(
+        functools.partial(split_grad, kind, count),
+        out_shape=(half, half),
+        in_specs=[SM] + [ANY] * len(flat),
+        out_specs=(ANY, ANY),
+        scratch_shapes=scratch([((2 * L, m), bf), ((2 * L, n), bf), ((2,) + half.shape, bf)]) + [pltpu.SemaphoreType.DMA((20,))],
+        compiler_params=PARAMS,
+        cost_estimate=pl.CostEstimate(flops=16 * L * D * D, bytes_accessed=2 * (2 * L * (m + n) + 4 * D * D), transcendentals=0),
+    )(part, *flat)
+
+
+def swapped(values, bit):
+    return lax.ppermute(values, "batch", [(i, i ^ bit) for i in range(lax.axis_size("batch"))])
+
+
+def added(left, right):
+    return left.astype(f32) + right.astype(f32)
+
+
+def after(value, *others):
+    return lax.optimization_barrier((value,) + others)
+
+
+def halve(keep, send, place, level):
+    came = swapped(send, 1 << level)
+    if keep.shape[0] == 1:
+        return added(keep[0], came[0])
+    own = (place >> (level + 1)) & 1
+    shape = (keep.shape[0] // 2, 2) + keep.shape[1:]
+    kept, got = keep.reshape(shape), came.reshape(shape)
+
+    def pick(side):
+        return added(lax.dynamic_index_in_dim(kept, side, 1, False), lax.dynamic_index_in_dim(got, side, 1, False)).astype(bf)
+
+    return pick(own), pick(1 - own)
+
+
+def summed(values, place):
+    levels = lax.axis_size("batch").bit_length() - 1
+    cut = [level for level in (2, 3) if level < levels]
+
+    def exchange(block, level):
+        return swapped(block, 1 << level)
+
+    values = added(values, exchange(values, 0)).astype(bf)
+    for level in cut:
+        own = (place >> level) & 1
+        parts = values.reshape(2, -1, D)
+        came = exchange(lax.dynamic_index_in_dim(parts, 1 - own, 0, False), level)
+        values = added(lax.dynamic_index_in_dim(parts, own, 0, False), came).astype(bf)
+    for level in range(1, levels):
+        if level not in cut:
+            values = added(values, exchange(values, level)).astype(bf)
+    for level in reversed(cut):
+        own = (place >> level) & 1
+        came = exchange(values, level)
+        low, high = jnp.where(own == 0, values, came), jnp.where(own == 0, came, values)
+        values = jnp.concatenate([low, high])
+    return values
+
+
+def collect_small(flag, b0, b1, v0, v1, a0, a1, here, moved):
+    half = L // 2
+    for out, s in ((here, slice(0, half)), (moved, slice(half, L))):
+        out[0:half, :] = (b0[s, :] + b1[s, :]).astype(bf)
+        out[half:, :] = jnp.zeros((64, D), bf)
+    vm = v0[...] + v1[...]
+    va = a0[...] + a1[...]
+    for out in (here, moved):
+        out[half : half + 1, :] = va[5:6].astype(bf)
+    block = jnp.concatenate([vm[0:1, i * D : (i + 1) * D] for i in range(4)] + [vm[1:2, i * D : (i + 1) * D] for i in range(3)]
+                            + [va[i : i + 1] for i in range(5)] + [jnp.zeros((4, D), f32)])
+    here[half + 16 : half + 32, :] = block.astype(bf)
+
+
+def collect(*values):
+    half = jax.ShapeDtypeStruct((L // 2 + 64, D), bf)
+    return pl.pallas_call(
+        collect_small,
+        out_shape=(half, half),
+        in_specs=[SM] + [VM] * 6,
+        out_specs=(VM, VM),
+        cost_estimate=pl.CostEstimate(flops=1_000_000, bytes_accessed=5_000_000, transcendentals=0),
+    )(*values)
+
+
+def passed_along(block, distance):
+    devices = range(lax.axis_size("section"))
+    route = [(i - distance, i) for i in devices if i - distance in devices]
+    return lax.ppermute(block, "section", route)
+
+
+def scatter(values):
+    return lax.psum_scatter(values, "batch", scatter_dimension=0, tiled=True)
+
+
+def split_grad(kind, count, part, *refs):
+    ins, (keep, send), (a, b, o, sems) = refs[:-6], refs[-6:-4], refs[-4:]
+    c = Copies(sems)
+    mine = part[0]
+
+    def load(pairs):
+        return [c.start(src, dst) for src, dst in pairs]
+
+    if kind == "down":
+        a0, b0, a1, b1, other = ins
+        waits = load(((a0, a.at[0:L]), (a1, a.at[L:])))
+        rows = (b.at[0:L], b.at[L:])
+
+        @pl.when(part[1] != 0)
+        def _():
+            for src, dst, sem in zip((b0, b1), rows, (18, 19)):
+                pltpu.make_async_copy(src, dst, sems.at[sem]).start()
+
+        @pl.when(part[1] == 0)
+        def _():
+            for at, dst, sem in zip((0, 1), rows, (18, 19)):
+                pltpu.make_async_copy(other.at[at], dst, sems.at[sem]).start()
+
+        for src, dst, sem in zip((b0, b1), rows, (18, 19)):
+            pltpu.make_async_copy(src, dst, sems.at[sem]).wait()
+        for w in waits:
+            w.wait()
+        height = FF // count
+        per = D // height // 2
+        for j in range(FF // D):
+            tile = mm(a[:, j * D : (j + 1) * D], b[...], 0, 0).astype(bf)
+            for i in range(2 * per):
+                o[i % 2, j * per + i // 2] = tile[i * height : (i + 1) * height]
+            s = slice(j * per, (j + 1) * per)
+            c.out(o.at[mine, s], keep.at[s])
+            c.out(o.at[1 - mine, s], send.at[s])
+    else:
+        height = D // count
+        groups = [ins[i : i + 4] for i in range(0, len(ins), 4)]
+        loads = []
+        column = 0
+        for g, (a0, b0, a1, b1) in enumerate(groups):
+            width = b0.shape[1]
+            r = slice(column, column + width)
+            l = slice(g * D, (g + 1) * D)
+            loads.append(load(((a0, a.at[0:L, l]), (a1, a.at[L:, l]), (b0, b.at[0:L, r]), (b1, b.at[L:, r]))))
+            column += width
+        t = 0
+        for g, (a0, b0, a1, b1) in enumerate(groups):
+            for w in loads[g]:
+                w.wait()
+            for _ in range(b0.shape[1] // D):
+                tile = mm(a[:, g * D : (g + 1) * D], b[:, t * D : (t + 1) * D], 0, 0).astype(bf)
+                for i in range(count):
+                    o[i % 2, i // 2, t * height : (t + 1) * height] = tile[i * height : (i + 1) * height]
+                t += 1
+        c.out(o.at[mine], keep)
+        c.out(o.at[1 - mine], send)
+    c.finish()
+
+
+def split_gradient(kind, count, part, groups):
+    flat = [one for group in groups for one in group]
+    pairs = groups if kind == "both" else groups[:1]
+    m = sum(group[0].shape[1] for group in pairs)
+    n = sum(group[1].shape[1] for group in pairs)
+    half = jax.ShapeDtypeStruct((count // 2, 4 * D // count, D), bf)
+    return pl.pallas_call(
+        functools.partial(split_grad, kind, count),
+        out_shape=(half, half),
+        in_specs=[SM] + [ANY] * len(flat),
+        out_specs=(ANY, ANY),
+        scratch_shapes=scratch([((2 * L, m), bf), ((2 * L, n), bf), ((2,) + half.shape, bf)]) + [pltpu.SemaphoreType.DMA((20,))],
+        compiler_params=PARAMS,
+        cost_estimate=pl.CostEstimate(flops=16 * L * D * D, bytes_accessed=2 * (2 * L * (m + n) + 4 * D * D), transcendentals=0),
+    )(part, *flat)
+
+
+def swapped(values, bit):
+    return lax.ppermute(values, "batch", [(i, i ^ bit) for i in range(lax.axis_size("batch"))])
+
+
+def added(left, right):
+    return left.astype(f32) + right.astype(f32)
 
 
 def shards(clips, mask_flags, mask_embed, pos_embed, first_gain, first_shift, joint_weight, query_bias, value_bias,
@@ -346,59 +608,88 @@
     wj, wm, wu, wd = joint_weight[0], mixer_weight[0], up_weight[0], down_weight[0]
     weights = (wj, wm, wu, wd)
 
+    flags = mask_flags[..., None]
+    place = lax.axis_index("batch")
+    part = jnp.stack([place % 2, lead[0]]).astype(jnp.int32)
+    fast = (D // count) % 16 == 0
+
+    def handed(block, distance):
+        return passed_along(block, distance)
+
     lead0 = forward(lead, blended, 0, vec, up_bias, weights)
-    arriving0 = passed_along(lead0[8], 1)
+    arriving0 = handed(lead0[8], 1)
     lead1 = forward(lead, blended, 1, vec, up_bias, weights)
-    arriving1 = passed_along(lead1[8], 1)
-
-    def back(side, saved, g, g_clip, x, x_clip, gh_type, old):
-        n1, qkv, lt, mixed, after, n2, act, slope, out = saved
-        gl, ga, vm = backward_mlp(side, g, g_clip, vec, slope, after, wu, wd, old and old[:3])
-        gb, gj, gh, va = backward_attn(side, ga, x, x_clip, vec, qkv, lt, wm, wj, gh_type, old and old[3:])
-        return (gl, ga, vm, gb, gj, va), gh
+    arriving1 = handed(lead1[8], 1)
+
+    def back(side, saved, g, x, clip, old):
+        _, qkv, lt, _, after_rows, _, _, slope, _ = saved
+        own = clip if old is None else None
+        gl, ga, vm = backward_mlp(side, g, own, vec, slope, after_rows, wu, wd, old and old[:3])
+        at = None if old is None else clip
+        gb, gj, gh, va, *full = backward_attn(side, ga, x, at, vec, flags, qkv, lt, wm, wj, old and old[3:])
+        return (gl, ga, vm, gb, gj, gh, va), full
 
     saved0 = forward(tail, arriving0, None, vec, up_bias, weights, lead0)
-    grads0, back0 = back(tail, saved0, out_grad, 0, arriving0, None, bf, None)
-    leaving0 = passed_along(back0, -1)
+    grads0, _ = back(tail, saved0, out_grad, arriving0, 0, None)
+    leaving0 = handed(grads0[5], -1)
     saved1 = forward(tail, arriving1, None, vec, up_bias, weights, lead1)
-    grads1, back1 = back(tail, saved1, out_grad, 1, arriving1, None, bf, None)
-    leaving1 = passed_along(back1, -1)
-    grads0, blend0 = back(lead, saved0, leaving0, None, blended, 0, f32, grads0)
-    g0 = jnp.where(first, leaving0, out_grad[0])
-    g1 = jnp.where(first, leaving1, out_grad[1])
-    grads1, blend1 = back(lead, saved1, leaving1, None, blended, 1, f32, grads1)
-
-    def pair(i, j):
-        return [(a, b) for a, b in ((saved0[i], grads0[j]), (saved1[i], grads1[j]))]
-
-    down = weight_gradient(saved0[6], g0, saved1[6], g1)
-    up = weight_gradient(saved0[5], grads0[0], saved1[5], grads1[0])
-    joint = weight_gradient(saved0[0], grads0[4], saved1[0], grads1[4])
-    mixer = weight_gradient(saved0[3], grads0[3], saved1[3], grads1[3])
-    down, up, joint, mixer = [scatter(one).astype(f32)[None] for one in (down, up, joint, mixer)]
-
-    vm = grads0[2] + grads1[2]
-    va = grads0[5] + grads1[5]
-    columns = [vm[0], vm[1, :D], vm[1, D : 2 * D], vm[1, 2 * D : 3 * D]] + [va[i] for i in range(5)]
-    packed = scatter(jnp.concatenate([one.reshape(count, -1) for one in columns], axis=1))
-    pieces, at = [], 0
-    for one in columns:
-        width = one.shape[0] // count
-        pieces.append(packed[:, at : at + width])
-        at += width
-    g_ub, g_gain2, g_shift2, g_db, g_gain1, g_shift1, g_qb, g_vb, g_mb = pieces
+    grads1, _ = back(tail, saved1, out_grad, arriving1, 1, None)
+    leaving1 = handed(grads1[5], -1)
+    grads0, (blend0,) = back(lead, saved0, leaving0, blended, 0, grads0)
+    va0 = grads0[6]
+
+    n1_1, qkv_1, lt_1, mixed_1, after_1, n2_1, act_1, slope_1, _ = saved1
+    if fast:
+        part_d, va0 = after(part, va0)
+        down = split_gradient("down", count, part_d, [(saved0[6], leaving0, act_1, leaving1, out_grad)])
+        lead_m, *down = after(lead, *down)
+        gl1, ga1, vm1 = backward_mlp(lead_m, leaving1, None, vec, slope_1, after_1, wu, wd, grads1[:3])
+        down = halve(*down, place, 0)
+        part_u, *down = after(part, *down)
+        up = split_gradient("up", count, part_u, [(saved0[5], grads0[0], n2_1, gl1)])
+        lead_a, *up = after(lead, *up)
+    else:
+        gl1, ga1, vm1 = backward_mlp(lead, leaving1, None, vec, slope_1, after_1, wu, wd, grads1[:3])
+        lead_a = lead
+    gb1, gj1, gh1, va1, blend1 = backward_attn(lead_a, ga1, blended, 1, vec, flags, qkv_1, lt_1, wm, wj, grads1[3:])
+    here, moved = collect(lead, blend0, blend1, grads0[2], vm1, va0, va1)
+    joint_group, mixer_group = (saved0[0], grads0[4], n1_1, gj1), (saved0[3], grads0[3], mixed_1, gb1)
+    if fast:
+        up = halve(*up, place, 0)
+        down = halve(*down, place, 1)
+        part_b, *rest = after(part, *up, *down)
+        up, down = rest[:2], rest[2:]
+        both = split_gradient("both", count, part_b, [joint_group, mixer_group])
+        levels = count.bit_length() - 1
+        down, up, both = [functools.reduce(lambda pair, level: halve(*pair, place, level), range(at, levels), value)
+                          for at, value in ((2, down), (1, up), (0, both))]
+        height = D // count
+
+        def wide(block):
+            return jnp.swapaxes(block.reshape(-1, height, D), 0, 1).reshape(height, -1)
+
+        up, joint, mixer = wide(up), wide(both[: 3 * height]), both[3 * height :]
+    else:
+        g0 = jnp.where(first, leaving0, out_grad[0])
+        g1 = jnp.where(first, leaving1, out_grad[1])
+        down_group, up_group = (saved0[6], g0, act_1, g1), (saved0[5], grads0[0], n2_1, gl1)
+        down, up, joint, mixer = [
+            scatter(weight_gradient(*group)).astype(f32) for group in (down_group, up_group, joint_group, mixer_group)
+        ]
+    down, up, joint, mixer = [one[None] for one in (down, up, joint, mixer)]
 
     layer_outputs = jnp.stack([saved0[8], saved1[8]])[None]
-    blend = jnp.stack([blend0, blend1])
-    input_grads = jnp.where(first, blend * (1.0 - keep), jnp.stack([back0, back1]).astype(f32)).astype(bf)[None]
-    position = jnp.where(first, blend0 + blend1, 0.0)
-    masked = jnp.sum(jnp.where(first, blend * keep, 0.0), axis=(0, 1))
+    input_grads = jnp.stack([grads0[5], gh1])[None]
     half = L // 2
-    sent_position = passed_along(position[half:].astype(bf), 1).astype(f32)
-    sent_masked = passed_along(masked[D // 2 :], 1)
-    position = jnp.where(first, position[:half], sent_position)
-    masked = jnp.where(first, masked[: D // 2], sent_masked)
-    grad_mask, grad_position = lax.psum((masked, position), "batch")
+    arrived = handed(moved, 1)[: half + 16]
+    top = jnp.where(first, here[: half + 16], arrived)
+    total = summed(jnp.concatenate([top, here[half + 16 :]]), place).astype(f32)
+    grad_position = total[:half]
+    grad_mask = lax.dynamic_slice(total[half], (jnp.where(first, 0, D // 2),), (D // 2,))
+    sums = total[half + 16 :]
+    g_ub = lax.dynamic_slice(sums[:4].reshape(1, FF), (0, place * (FF // count)), (1, FF // count))
+    rest = lax.dynamic_slice(sums[4:12], (0, place * (D // count)), (8, D // count))
+    g_gain2, g_shift2, g_db, g_gain1, g_shift1, g_qb, g_vb, g_mb = [rest[i : i + 1] for i in range(8)]
     return (layer_outputs, input_grads, g_gain1, g_shift1, joint, g_qb, g_vb, mixer, g_mb, g_gain2, g_shift2, up, g_ub,
             down, g_db, grad_mask, grad_position)
 
@@ -407,4 +698,9 @@
     whole, section, both = P(), P("section"), P("section", "batch")
     in_specs = (P("batch"), P("batch"), whole, whole) + (section,) * 13 + (P("batch"),)
     out_specs = (both,) * 15 + (section, section)
-    return jax.shard_map(shards, mesh=mesh, in_specs=in_specs, out_specs=out_specs, check_vma=False)
+
+    def step(*arrays):
+        return shards(*arrays)
+
+    step = jax.shard_map(step, mesh=mesh, in_specs=in_specs, out_specs=out_specs, check_vma=False)
+    return step

time: 643 us -> 430 us (0.67)
  waiting for transfers between devices: 328 us -> 141 us
  blocking collectives: 61.1 us -> 0 us
  starting transfers between devices: 9.7 us -> 38.2 us
  other arithmetic: 21.5 us -> 38.8 us
  between operations: 14.5 us -> 1.32 us
    reduce_scatter x4 -> x0, waiting for transfers between devices: 167 us -> none  [scatter(): return lax.psum_scatter(values, 'batch', scatter_dimension=0, tiled=True)]
    psum x1 -> x0, waiting for transfers between devices: 93.9 us -> none  [shards(): grad_mask, grad_position = lax.psum((masked, position), 'batch')]
    ppermute x0 -> x18, waiting for transfers between devices: none -> 75.1 us  [swapped(): lax.ppermute(values, 'batch', [(i, i ^ bit) for i in range(lax.axis_size(...]
    unnamed x1 -> x0, blocking collectives: 61.1 us -> none
    ppermute x0 -> x18, starting transfers between devices: none -> 30.7 us  [swapped(): lax.ppermute(values, 'batch', [(i, i ^ bit) for i in range(lax.axis_size(...]
    convert_element_type x1 -> x15, other arithmetic: 1.57 us -> 23.5 us  [the longest x10 18.7 us: pick(): added(lax.dynamic_index_in_dim(kept, side, 1, False), lax.dynamic_index_i...]
    pallas_call x8, Pallas kernels: 74.3 us -> 81.4 us  [the longest x4 44.8 us: backward_attn(): pl.pallas_call(functools.partial(attn_back, clip, lead, extra), out_shape...]
    broadcast_in_dim x4 -> x0, other arithmetic: 6.91 us -> none  [shards(): scatter(one).astype(f32)[None]]
  transfers between devices with their start and end apart: 11 -> 23, of which waited for: 7 -> 13; matrix products, arithmetic and copies ran while one was open for 4% -> 8% of each run, Pallas kernels for 19% -> 33%
where the time goes in v2:
time: 430 us; the launch traced here: 425 us
  Pallas kernels  191 us (44%)
  waiting for transfers between devices  141 us (33%)
  other arithmetic  38.8 us (9%)
  starting transfers between devices  38.2 us (9%)
  local copies, waits for them, and re-layouts  15.9 us (4%)
    pallas_call x4, Pallas kernels, forward(): pl.pallas_call(functools.partial(front, clip, extra), out_shape=shapes(SA...  80.7 us
    ppermute x18, waiting for transfers between devices, swapped(): lax.ppermute(values, 'batch', [(i, i ^ bit) for i in range(lax.axis_size(...  75.1 us
    ppermute x5, waiting for transfers between devices, passed_along(): return lax.ppermute(block, 'section', route)  65.5 us
    pallas_call x4, Pallas kernels, backward_attn(): pl.pallas_call(functools.partial(attn_back, clip, lead, extra), out_shape...  44.8 us
    pallas_call x3, Pallas kernels, split_gradient(): pl.pallas_call(functools.partial(split_grad, kind, count), out_shape=(hal...  33.6 us
    ppermute x18, starting transfers between devices, swapped(): lax.ppermute(values, 'batch', [(i, i ^ bit) for i in range(lax.axis_size(...  30.7 us
    pallas_call x4, Pallas kernels, backward_mlp(): pl.pallas_call(functools.partial(mlp_back, clip, extra), out_shape=shapes...  28.4 us
    convert_element_type x10, other arithmetic, pick(): added(lax.dynamic_index_in_dim(kept, side, 1, False), lax.dynamic_index_i...  18.7 us
  transfers between devices with their start and end apart: 23, of which 13 were waited for; matrix products, arithmetic and copies ran while one was open for 8% of the time, Pallas kernels for 33%

profile of v2, /device:TPU:0, one launch (start us, length us, event | category | flops | bytes accessed | tf_op | source)
XLA Modules:
  0.0 425.3 jit_solution(6120665788496490718)
XLA Ops:
  2.1 4.1 add_add_fusion.x_in
  7.0 27.9 %shard_map.305 = (bf16[512,768]{1,0:T(8,128)(2,1)}, bf16[512,2304]{1,0:T(8,128)(2,1)}, f32[16,512]{1,0:T(8,128)}, bf16[512,768]{1,0:T(8,128)(2,1)}, f32[512,768]...) custom-call(s32[1]{0:T(128)} %bitcast.side.flag, ...), custom_call_target="tpu_custom_call" | custom-call | flops 8049999872 | bytes 30000000 | tf_op jit(solution)/shard_map/pallas_call | solution.py:157
  34.9 1.3 collective-permute-start
  36.3 27.7 %shard_map.307 = (bf16[512,768]{1,0:T(8,128)(2,1)}, bf16[512,2304]{1,0:T(8,128)(2,1)}, f32[16,512]{1,0:T(8,128)}, bf16[512,768]{1,0:T(8,128)(2,1)}, f32[512,768]...) custom-call(s32[1]{0:T(128)} %bitcast.side.flag, ...), custom_call_target="tpu_custom_call" | custom-call | flops 8049999872 | bytes 30000000 | tf_op jit(solution)/shard_map/pallas_call | solution.py:157
  63.9 1.3 collective-permute-start.1
  65.3 1.0 copy.79.flags
  67.8 11.9 %shard_map.306 = (bf16[512,768]{1,0:T(8,128)(2,1)}, bf16[512,2304]{1,0:T(8,128)(2,1)}, f32[16,512]{1,0:T(8,128)}, bf16[512,768]{1,0:T(8,128)(2,1)}, f32[512,768]...) custom-call(s32[1]{0:T(128)S(6)} %sub.13.side, ...), custom_call_target="tpu_custom_call", output_to_operand_aliasing={{0}: (8, {}), {1}: (9, {}), {2}: (10, {}), {3}: (11, {}), {... | custom-call | flops 8049999872 | bytes 30000000 | tf_op jit(solution)/shard_map/pallas_call | solution.py:157
  80.6 1.2 shard_map.310
  81.8 1.3 collective-permute-start.2
  84.2 13.2 %shard_map.308 = (bf16[512,768]{1,0:T(8,128)(2,1)}, bf16[512,2304]{1,0:T(8,128)(2,1)}, f32[16,512]{1,0:T(8,128)}, bf16[512,768]{1,0:T(8,128)(2,1)}, f32[512,768]...) custom-call(s32[1]{0:T(128)S(6)} %sub.13.side, ...), custom_call_target="tpu_custom_call", output_to_operand_aliasing={{0}: (8, {}), {1}: (9, {}), {2}: (10, {}), {3}: (11, {}), {... | custom-call | flops 8049999872 | bytes 30000000 | tf_op jit(solution)/shard_map/pallas_call | solution.py:157
  98.3 1.2 shard_map.314
  99.5 1.3 collective-permute-start.3
  100.8 37.2 %collective-permute-done.2.g_in.refs_1_ = bf16[512,768]{1,0:T(8,128)(2,1)S(1)} collective-permute-done((bf16[512,768]{1,0:T(8,128)(2,1)}, bf16[512,768]{1,0:T(8,128)(2,1)S(1)}, u32[]{:S(2)}, u32[]{:S(2)}) %collective-permute-start.2) | collective-permute-done | bytes 786464 | tf_op jit(solution)/shard_map/ppermute | solution.py:506
  138.9 13.2 %shard_map.311 = (bf16[512,3072]{1,0:T(8,128)(2,1)}, f32[512,768]{1,0:T(8,128)}, f32[8,3072]{1,0:T(8,128)}) custom-call(s32[1]{0:T(128)} %bitcast.side.flag, bf16[512,768]{1,0:T(8,128)(2,1)} %copy-done.6, f32[8,768]{1,0:T(8,128)} %concatenate.12.vec, ...), custom_call_target="tpu_custom_call", output_to_operand_aliasing={{0}: (7, {}), {1}: (8, {}), {2}: (9, {})} | custom-call | flops 4830000128 | bytes 20000000 | tf_op jit(solution)/shard_map/pallas_call | solution.py:210
  152.1 21.3 %shard_map.312 = (bf16[512,768]{1,0:T(8,128)(2,1)}, bf16[512,2304]{1,0:T(8,128)(2,1)}, bf16[512,768]{1,0:T(8,128)(2,1)}, f32[8,768]{1,0:T(8,128)}, f32[512,768]{1,0:T(8,128)}) custom-call(s32[1]{0:T(128)} %bitcast.side.flag, f32[512,768]{1,0:T(8,128)} %get-tuple-element.135.ga_in, ...), custom_call_target="tpu_custom_call", output_to_operand_aliasing={{0}: (9, {}), {1}: (10, {}), {2}: (11, {}), {3}: (12, {})} | custom-call | flops 4400000000 | bytes 20000000 | tf_op jit(solution)/shard_map/pallas_call | solution.py:296
  173.4 28.1 %collective-permute-done.3.refs_3_.g_in = bf16[512,768]{1,0:T(8,128)(2,1)S(1)} collective-permute-done((bf16[512,768]{1,0:T(8,128)(2,1)}, bf16[512,768]{1,0:T(8,128)(2,1)S(1)}, u32[]{:S(2)}, u32[]{:S(2)}) %collective-permute-start.3) | collective-permute-done | bytes 786464 | tf_op jit(solution)/shard_map/ppermute | solution.py:506
  201.5 0.9 copy-done.7
  202.4 10.2 %shard_map.315 = (bf16[8,192,768]{2,1,0:T(8,128)(2,1)}, bf16[8,192,768]{2,1,0:T(8,128)(2,1)}) custom-call(s32[2]{0:T(128)} %pad_add_fusion.part, bf16[512,3072]{1,0:T(8,128)(2,1)} %get-tuple-element.142.refs_0_, bf16[512,768]{1,0:T(8,128)(2,1)} %copy-done.6, bf16[512,3072]{1,0:T(8,128)(2,1)} %get-tuple-element.143.refs_2_, bf16[512,768]{1,0:T(8,128)(2,1)} %copy-done.7, ...), custom_call_target="tpu_custom_call" | custom-call | flops 4831838208 | bytes 12582912 | tf_op jit(solution)/shard_map/pallas_call | solution.py:580
  212.8 13.4 %shard_map.316 = (bf16[512,3072]{1,0:T(8,128)(2,1)}, f32[512,768]{1,0:T(8,128)}, f32[8,3072]{1,0:T(8,128)}) custom-call(s32[1]{0:T(128)} %bitcast.side.flag, bf16[512,768]{1,0:T(8,128)(2,1)} %copy-done.7, f32[8,768]{1,0:T(8,128)} %concatenate.12.vec, ...), custom_call_target="tpu_custom_call", output_to_operand_aliasing={{0}: (7, {}), {1}: (8, {}), {2}: (9, {})} | custom-call | flops 4830000128 | bytes 20000000 | tf_op jit(solution)/shard_map/pallas_call | solution.py:210
  226.2 3.9 fusion.1
  230.2 11.4 %shard_map.317 = (bf16[8,192,768]{2,1,0:T(8,128)(2,1)}, bf16[8,192,768]{2,1,0:T(8,128)(2,1)}) custom-call(s32[2]{0:T(128)} %pad_add_fusion.part, bf16[512,768]{1,0:T(8,128)(2,1)} %get-tuple-element.155.refs_0_, bf16[512,3072]{1,0:T(8,128)(2,1)} %get-tuple-element.156.refs_1_, bf16[512,768]{1,0:T(8,128)(2,1)} %get-tuple-element.157.refs_2_, ...), custom_call_target="tpu_custom_call" | custom-call | flops 4831838208 | bytes 12582912 | tf_op jit(solution)/shard_map/pallas_call | solution.py:580
  242.1 1.7 collective-permute-start.13
  243.8 21.1 %shard_map.318 = (bf16[512,768]{1,0:T(8,128)(2,1)}, bf16[512,2304]{1,0:T(8,128)(2,1)}, bf16[512,768]{1,0:T(8,128)(2,1)}, f32[8,768]{1,0:T(8,128)}, f32[512,768]{1,0:T(8,128)}) custom-call(s32[1]{0:T(128)} %bitcast.side.flag, f32[512,768]{1,0:T(8,128)} %get-tuple-element.165.ga_in, ...), custom_call_target="tpu_custom_call", output_to_operand_aliasing={{0}: (9, {}), {1}: (10, {}), {2}: (11, {}), {3}: (12, {})} | custom-call | flops 4400000000 | bytes 20000000 | tf_op jit(solution)/shard_map/pallas_call | solution.py:296
  264.9 3.1 shard_map.319
  267.9 1.5 slice.58
  269.4 2.2 collective-permute-start.5
  271.7 2.2 fusion.5
  273.9 2.0 fusion.6
  275.9 3.2 fusion.3
  279.1 12.0 %shard_map.320 = (bf16[8,192,768]{2,1,0:T(8,128)(2,1)}, bf16[8,192,768]{2,1,0:T(8,128)(2,1)}) custom-call(s32[2]{0:T(128)} %pad_add_fusion.part, bf16[512,768]{1,0:T(8,128)(2,1)} %get-tuple-element.183.refs_0_, bf16[512,2304]{1,0:T(8,128)(2,1)} %get-tuple-element.184.refs_1_, bf16[512,768]{1,0:T(8,128)(2,1)} %get-tuple-element.185.refs_2_, ...), custom_call_target="tpu_custom_call" | custom-call | flops 4831838208 | bytes 14155776 | tf_op jit(solution)/shard_map/pallas_call | solution.py:580
  291.2 1.2 slice_select_fusion
  292.4 0.9 pad_maximum_fusion
  293.8 2.8 collective-permute-done.6
  298.2 1.6 collective-permute-start.7
  299.8 6.7 %collective-permute-done.7 = bf16[160,768]{1,0:T(8,128)(2,1)} collective-permute-done((bf16[160,768]{1,0:T(8,128)(2,1)}, bf16[160,768]{1,0:T(8,128)(2,1)}, u32[]{:S(2)}, u32[]{:S(2)}) %collective-permute-start.7) | collective-permute-done | bytes 245792 | tf_op jit(solution)/shard_map/ppermute | solution.py:592
  306.5 1.1 fusion.13
  309.0 2.6 collective-permute-start.8
  311.6 5.7 %collective-permute-done.8 = bf16[80,768]{1,0:T(8,128)(2,1)} collective-permute-done((bf16[80,768]{1,0:T(8,128)(2,1)}, bf16[80,768]{1,0:T(8,128)(2,1)}, u32[]{:S(2)}, u32[]{:S(2)}) %collective-permute-start.8) | collective-permute-done | bytes 122912 | tf_op jit(solution)/shard_map/ppermute | solution.py:592
  317.4 1.6 fusion.15
  319.4 4.8 %collective-permute-done.9 = bf16[80,768]{1,0:T(8,128)(2,1)} collective-permute-done((bf16[80,768]{1,0:T(8,128)(2,1)}, bf16[80,768]{1,0:T(8,128)(2,1)}, u32[]{:S(2)}, u32[]{:S(2)}) %collective-permute-start.9) | collective-permute-done | bytes 122912 | tf_op jit(solution)/shard_map/ppermute | solution.py:592
  324.2 1.0 add_convert_fusion.15
  326.1 1.4 copy-done.2
  327.5 4.0 add_convert_fusion.1
  331.5 1.6 collective-permute-start.15
  333.8 3.8 collective-permute-start.11
  337.6 3.6 maximum_bitcast_fusion
  341.2 0.9 collective-permute-done.11
  342.1 1.0 broadcast_select_fusion
  343.2 0.9 fusion.14
  344.1 2.0 collective-permute-start.21
  346.1 8.6 %collective-permute-done.18 = bf16[4,192,768]{2,1,0:T(8,128)(2,1)} collective-permute-done((bf16[4,192,768]{2,1,0:T(8,128)(2,1)}, bf16[4,192,768]{2,1,0:T(8,128)(2,1)}, u32[]{:S(2)}, u32[]{:S(2)}) %collective-permute-start.18) | collective-permute-done | bytes 1179680 | tf_op jit(solution)/shard_map/ppermute | solution.py:592
  354.8 1.5 add_convert_fusion.7
  356.3 3.9 collective-permute-start.19
  360.2 16.5 %collective-permute-done.15 = bf16[4,192,768]{2,1,0:T(8,128)(2,1)} collective-permute-done((bf16[4,192,768]{2,1,0:T(8,128)(2,1)}, bf16[4,192,768]{2,1,0:T(8,128)(2,1)}, u32[]{:S(2)}, u32[]{:S(2)}) %collective-permute-start.15) | collective-permute-done | bytes 1179680 | tf_op jit(solution)/shard_map/ppermute | solution.py:592
  376.7 1.6 add_convert_fusion.9
  378.2 4.9 %collective-permute-start.16 = (bf16[2,192,768]{2,1,0:T(8,128)(2,1)S(1)}, bf16[2,192,768]{2,1,0:T(8,128)(2,1)S(1)}, u32[]{:S(2)}, u32[]{:S(2)}) collective-permute-start(bf16[2,192,768]{2,1,0:T(8,128)(2,1)S(1)} %get-tuple-element.206), channel_id=1, source_target_pairs={{0,4},{1,5},{2,6},{3,7},{4,0},{5,1},{6,2},{7,3},{8,12},{9,13},{10,... | collective-permute-start | bytes 1769480 | tf_op jit(solution)/shard_map/ppermute | solution.py:592
  385.6 2.6 collective-permute-start.20
  388.3 15.7 %collective-permute-done.16 = bf16[2,192,768]{2,1,0:T(8,128)(2,1)S(1)} collective-permute-done((bf16[2,192,768]{2,1,0:T(8,128)(2,1)S(1)}, bf16[2,192,768]{2,1,0:T(8,128)(2,1)S(1)}, u32[]{:S(2)}, u32[]{:S(2)}) %collective-permute-start.16) | collective-permute-done | bytes 589856 | tf_op jit(solution)/shard_map/ppermute | solution.py:592
  404.1 3.0 collective-permute-start.17
  407.1 0.9 convert_add_fusion.4
  408.0 11.6 %collective-permute-done.20 = bf16[1,192,768]{2,1,0:T(8,128)(2,1)S(1)} collective-permute-done((bf16[1,192,768]{2,1,0:T(8,128)(2,1)S(1)}, bf16[1,192,768]{2,1,0:T(8,128)(2,1)S(1)}, u32[]{:S(2)}, u32[]{:S(2)}) %collective-permute-start.20) | collective-permute-done | bytes 294944 | tf_op jit(solution)/shard_map/ppermute | solution.py:592
  420.1 1.1 broadcast_in_dim_reshape.7
  421.3 1.7 collective-permute-done.17
  424.0 1.1 broadcast_in_dim_reshape.6
  (85 shorter events, 17.8 us)
Async XLA Ops:
  2.0 4.2 copy-start.11
  2.0 4.2 copy-start.12
  2.0 4.2 copy-start.13
  2.1 4.2 copy-start.14
  2.1 4.2 copy-start.15
  2.1 4.2 copy-start.16
  2.1 4.2 copy-start.17
  2.1 4.2 copy-start.18
  34.9 30.4 %copy-start.10 = (s32[2,512]{1,0:T(2,128)S(1)}, s32[2,512]{1,0:T(2,128)}, u32[]{:S(2)}) copy-start(s32[2,512]{1,0:T(2,128)} %param.19) | copy-start | bytes 12292
  34.9 32.0 %collective-permute-start = (bf16[512,768]{1,0:T(8,128)(2,1)}, bf16[512,768]{1,0:T(8,128)(2,1)S(1)}, u32[]{:S(2)}, u32[]{:S(2)}) collective-permute-start(bf16[512,768]{1,0:T(8,128)(2,1)} %get-tuple-element.107.rest_8_), channel_id=1, source_target_pairs={{0,16},{1,17},{2,18},{3,19},{4,20},{5,21},{6,22},{7,23},{8,24},{9,... | collective-permute-start | bytes 2359304 | tf_op jit(solution)/shard_map/ppermute | solution.py:506
  63.9 19.3 %collective-permute-start.1 = (bf16[512,768]{1,0:T(8,128)(2,1)}, bf16[512,768]{1,0:T(8,128)(2,1)S(1)}, u32[]{:S(2)}, u32[]{:S(2)}) collective-permute-start(bf16[512,768]{1,0:T(8,128)(2,1)} %get-tuple-element.117.rest_8_), channel_id=1, source_target_pairs={{0,16},{1,17},{2,18},{3,19},{4,20},{5,21},{6,22},{7,23},{8,24},{9,... | collective-permute-start | bytes 2359304 | tf_op jit(solution)/shard_map/ppermute | solution.py:506
  66.9 0.9 copy-start.20
  81.8 56.2 %collective-permute-start.2 = (bf16[512,768]{1,0:T(8,128)(2,1)}, bf16[512,768]{1,0:T(8,128)(2,1)S(1)}, u32[]{:S(2)}, u32[]{:S(2)}) collective-permute-start(bf16[512,768]{1,0:T(8,128)(2,1)} %get-tuple-element.132.rest_2_), channel_id=1, source_target_pairs={{16,0},{17,1},{18,2},{19,3},{20,4},{21,5},{22,6},{23,7},{24,8},{25... | collective-permute-start | bytes 2359304 | tf_op jit(solution)/shard_map/ppermute | solution.py:506
  83.3 0.9 copy-start.19
  99.5 102.0 %collective-permute-start.3 = (bf16[512,768]{1,0:T(8,128)(2,1)}, bf16[512,768]{1,0:T(8,128)(2,1)S(1)}, u32[]{:S(2)}, u32[]{:S(2)}) collective-permute-start(bf16[512,768]{1,0:T(8,128)(2,1)} %get-tuple-element.149.rest_2_), channel_id=1, source_target_pairs={{16,0},{17,1},{18,2},{19,3},{20,4},{21,5},{22,6},{23,7},{24,8},{25... | collective-permute-start | bytes 2359304 | tf_op jit(solution)/shard_map/ppermute | solution.py:506
  138.0 0.9 copy-start.6
  201.5 0.9 copy-start.7
  212.7 13.5 %collective-permute-start.4 = (bf16[8,192,768]{2,1,0:T(8,128)(2,1)}, bf16[8,192,768]{2,1,0:T(8,128)(2,1)}, u32[]{:S(2)}, u32[]{:S(2)}) collective-permute-start(bf16[8,192,768]{2,1,0:T(8,128)(2,1)} %get-tuple-element.153), channel_id=1, source_target_pairs={{0,1},{1,0},{2,3},{3,2},{4,5},{5,4},{6,7},{7,6},{8,9},{9,8},{10,11... | collective-permute-start | bytes 7077896 | tf_op jit(solution)/shard_map/ppermute | solution.py:592
  241.6 34.3 %collective-permute-start.12 = (bf16[8,192,768]{2,1,0:T(8,128)(2,1)}, bf16[8,192,768]{2,1,0:T(8,128)(2,1)}, u32[]{:S(2)}, u32[]{:S(2)}) collective-permute-start(bf16[8,192,768]{2,1,0:T(8,128)(2,1)} %get-tuple-element.179), channel_id=1, source_target_pairs={{0,1},{1,0},{2,3},{3,2},{4,5},{5,4},{6,7},{7,6},{8,9},{9,8},{10,11... | collective-permute-start | bytes 7077896 | tf_op jit(solution)/shard_map/ppermute | solution.py:592
  242.1 29.5 %collective-permute-start.13 = (bf16[4,192,768]{2,1,0:T(8,128)(2,1)}, bf16[4,192,768]{2,1,0:T(8,128)(2,1)}, u32[]{:S(2)}, u32[]{:S(2)}) collective-permute-start(bf16[4,192,768]{2,1,0:T(8,128)(2,1)} %get-tuple-element.181), channel_id=1, source_target_pairs={{0,2},{1,3},{2,0},{3,1},{4,6},{5,7},{6,4},{7,5},{8,10},{9,11},{10,... | collective-permute-start | bytes 3538952 | tf_op jit(solution)/shard_map/ppermute | solution.py:592
  269.4 21.7 %collective-permute-start.5 = (bf16[320,768]{1,0:T(8,128)(2,1)}, bf16[320,768]{1,0:T(8,128)(2,1)}, u32[]{:S(2)}, u32[]{:S(2)}) collective-permute-start(bf16[320,768]{1,0:T(8,128)(2,1)} %get-tuple-element.177), channel_id=1, source_target_pairs={{0,16},{1,17},{2,18},{3,19},{4,20},{5,21},{6,22},{7,23},{8,24},{9,... | collective-permute-start | bytes 1474568 | tf_op jit(solution)/shard_map/ppermute | solution.py:506
  271.7 4.2 copy-start.3
  291.1 5.5 %copy-start.8 = (bf16[48,768]{1,0:T(8,128)(2,1)S(1)}, bf16[48,768]{1,0:T(8,128)(2,1)}, u32[]{:S(2)}) copy-start(bf16[48,768]{1,0:T(8,128)(2,1)} %slice.58) | copy-start | bytes 221188
  291.1 35.0 %collective-permute-start.14 = (bf16[8,192,768]{2,1,0:T(8,128)(2,1)}, bf16[8,192,768]{2,1,0:T(8,128)(2,1)S(1)}, u32[]{:S(2)}, u32[]{:S(2)}) collective-permute-start(bf16[8,192,768]{2,1,0:T(8,128)(2,1)} %get-tuple-element.192), channel_id=1, source_target_pairs={{0,1},{1,0},{2,3},{3,2},{4,5},{5,4},{6,7},{7,6},{8,9},{9,8},{10,11... | collective-permute-start | bytes 7077896 | tf_op jit(solution)/shard_map/ppermute | solution.py:592
  293.3 3.3 collective-permute-start.6
  296.7 0.8 copy-start.4
  298.2 8.3 %collective-permute-start.7 = (bf16[160,768]{1,0:T(8,128)(2,1)}, bf16[160,768]{1,0:T(8,128)(2,1)}, u32[]{:S(2)}, u32[]{:S(2)}) collective-permute-start(bf16[160,768]{1,0:T(8,128)(2,1)} %dynamic-slice_bitcast_fusion), channel_id=1, source_target_pairs={{0,4},{1,5},{2,6},{3,7},{4,0},{5,1},{6,2},{7,3},{8,12},{9,13},{10,... | collective-permute-start | bytes 737288 | tf_op jit(solution)/shard_map/ppermute | solution.py:592
  307.7 0.7 copy-start.5
  309.0 8.4 %collective-permute-start.8 = (bf16[80,768]{1,0:T(8,128)(2,1)}, bf16[80,768]{1,0:T(8,128)(2,1)}, u32[]{:S(2)}, u32[]{:S(2)}) collective-permute-start(bf16[80,768]{1,0:T(8,128)(2,1)} %dynamic-slice_bitcast_fusion.1), channel_id=1, source_target_pairs={{0,8},{1,9},{2,10},{3,11},{4,12},{5,13},{6,14},{7,15},{8,0},{9,1},... | collective-permute-start | bytes 368648 | tf_op jit(solution)/shard_map/ppermute | solution.py:592
  319.0 5.2 %collective-permute-start.9 = (bf16[80,768]{1,0:T(8,128)(2,1)}, bf16[80,768]{1,0:T(8,128)(2,1)}, u32[]{:S(2)}, u32[]{:S(2)}) collective-permute-start(bf16[80,768]{1,0:T(8,128)(2,1)} %fusion.15), channel_id=1, source_target_pairs={{0,2},{1,3},{2,0},{3,1},{4,6},{5,7},{6,4},{7,5},{8,10},{9,11},{10,... | collective-permute-start | bytes 368648 | tf_op jit(solution)/shard_map/ppermute | solution.py:592
  325.2 7.9 %collective-permute-start.10 = (bf16[80,768]{1,0:T(8,128)(2,1)S(1)}, bf16[80,768]{1,0:T(8,128)(2,1)S(1)}, u32[]{:S(2)}, u32[]{:S(2)}) collective-permute-start(bf16[80,768]{1,0:T(8,128)(2,1)S(1)} %add_convert_fusion.15), channel_id=1, source_target_pairs={{0,8},{1,9},{2,10},{3,11},{4,12},{5,13},{6,14},{7,15},{8,0},{9,1},... | collective-permute-start | bytes 368648 | tf_op jit(solution)/shard_map/ppermute | solution.py:592
  325.6 29.2 %collective-permute-start.18 = (bf16[4,192,768]{2,1,0:T(8,128)(2,1)}, bf16[4,192,768]{2,1,0:T(8,128)(2,1)}, u32[]{:S(2)}, u32[]{:S(2)}) collective-permute-start(bf16[4,192,768]{2,1,0:T(8,128)(2,1)} %get-tuple-element.194), channel_id=1, source_target_pairs={{0,2},{1,3},{2,0},{3,1},{4,6},{5,7},{6,4},{7,5},{8,10},{9,11},{10,... | collective-permute-start | bytes 3538952 | tf_op jit(solution)/shard_map/ppermute | solution.py:592
  326.1 1.4 copy-start.2
  327.5 10.1 %copy-start = (bf16[512,768]{1,0:T(8,128)(2,1)S(1)}, bf16[512,768]{1,0:T(8,128)(2,1)}, u32[]{:S(2)}) copy-start(bf16[512,768]{1,0:T(8,128)(2,1)} %get-tuple-element.169) | copy-start | bytes 2359300
  331.5 45.1 %collective-permute-start.15 = (bf16[4,192,768]{2,1,0:T(8,128)(2,1)}, bf16[4,192,768]{2,1,0:T(8,128)(2,1)}, u32[]{:S(2)}, u32[]{:S(2)}) collective-permute-start(bf16[4,192,768]{2,1,0:T(8,128)(2,1)} %get-tuple-element.198), channel_id=1, source_target_pairs={{0,2},{1,3},{2,0},{3,1},{4,6},{5,7},{6,4},{7,5},{8,10},{9,11},{10,... | collective-permute-start | bytes 3538952 | tf_op jit(solution)/shard_map/ppermute | solution.py:592
  333.8 8.3 %collective-permute-start.11 = (bf16[160,768]{1,0:T(8,128)(2,1)}, bf16[160,768]{1,0:T(8,128)(2,1)}, u32[]{:S(2)}, u32[]{:S(2)}) collective-permute-start(bf16[160,768]{1,0:T(8,128)(2,1)} %pad_maximum_fusion.2), channel_id=1, source_target_pairs={{0,4},{1,5},{2,6},{3,7},{4,0},{5,1},{6,2},{7,3},{8,12},{9,13},{10,... | collective-permute-start | bytes 737288 | tf_op jit(solution)/shard_map/ppermute | solution.py:592
  341.2 2.9 copy-start.9
  344.1 39.7 %collective-permute-start.21 = (bf16[2,192,768]{2,1,0:T(8,128)(2,1)S(1)}, bf16[2,192,768]{2,1,0:T(8,128)(2,1)S(1)}, u32[]{:S(2)}, u32[]{:S(2)}) collective-permute-start(bf16[2,192,768]{2,1,0:T(8,128)(2,1)S(1)} %copy-done.9), channel_id=1, source_target_pairs={{0,4},{1,5},{2,6},{3,7},{4,0},{5,1},{6,2},{7,3},{8,12},{9,13},{10,... | collective-permute-start | bytes 1769480 | tf_op jit(solution)/shard_map/ppermute | solution.py:592
  356.3 29.3 %collective-permute-start.19 = (bf16[2,192,768]{2,1,0:T(8,128)(2,1)S(1)}, bf16[2,192,768]{2,1,0:T(8,128)(2,1)S(1)}, u32[]{:S(2)}, u32[]{:S(2)}) collective-permute-start(bf16[2,192,768]{2,1,0:T(8,128)(2,1)S(1)} %get-tuple-element.204), channel_id=1, source_target_pairs={{0,4},{1,5},{2,6},{3,7},{4,0},{5,1},{6,2},{7,3},{8,12},{9,13},{10,... | collective-permute-start | bytes 1769480 | tf_op jit(solution)/shard_map/ppermute | solution.py:592
  376.7 7.2 %copy-start.1 = (bf16[2,192,768]{2,1,0:T(8,128)(2,1)S(1)}, bf16[2,192,768]{2,1,0:T(8,128)(2,1)}, u32[]{:S(2)}) copy-start(bf16[2,192,768]{2,1,0:T(8,128)(2,1)} %fusion.5) | copy-start | bytes 1769476
  378.2 25.7 %collective-permute-start.16 = (bf16[2,192,768]{2,1,0:T(8,128)(2,1)S(1)}, bf16[2,192,768]{2,1,0:T(8,128)(2,1)S(1)}, u32[]{:S(2)}, u32[]{:S(2)}) collective-permute-start(bf16[2,192,768]{2,1,0:T(8,128)(2,1)S(1)} %get-tuple-element.206), channel_id=1, source_target_pairs={{0,4},{1,5},{2,6},{3,7},{4,0},{5,1},{6,2},{7,3},{8,12},{9,13},{10,... | collective-permute-start | bytes 1769480 | tf_op jit(solution)/shard_map/ppermute | solution.py:592
  383.9 23.2 %collective-permute-start.22 = (bf16[1,192,768]{2,1,0:T(8,128)(2,1)S(1)}, bf16[1,192,768]{2,1,0:T(8,128)(2,1)S(1)}, u32[]{:S(2)}, u32[]{:S(2)}) collective-permute-start(bf16[1,192,768]{2,1,0:T(8,128)(2,1)S(1)} %add_convert_fusion.13), channel_id=1, source_target_pairs={{0,8},{1,9},{2,10},{3,11},{4,12},{5,13},{6,14},{7,15},{8,0},{9,1},... | collective-permute-start | bytes 884744 | tf_op jit(solution)/shard_map/ppermute | solution.py:592
  385.6 34.0 %collective-permute-start.20 = (bf16[1,192,768]{2,1,0:T(8,128)(2,1)S(1)}, bf16[1,192,768]{2,1,0:T(8,128)(2,1)S(1)}, u32[]{:S(2)}, u32[]{:S(2)}) collective-permute-start(bf16[1,192,768]{2,1,0:T(8,128)(2,1)S(1)} %fusion.9), channel_id=1, source_target_pairs={{0,8},{1,9},{2,10},{3,11},{4,12},{5,13},{6,14},{7,15},{8,0},{9,1},... | collective-permute-start | bytes 884744 | tf_op jit(solution)/shard_map/ppermute | solution.py:592
  404.1 18.8 %collective-permute-start.17 = (bf16[1,192,768]{2,1,0:T(8,128)(2,1)S(1)}, bf16[1,192,768]{2,1,0:T(8,128)(2,1)S(1)}, u32[]{:S(2)}, u32[]{:S(2)}) collective-permute-start(bf16[1,192,768]{2,1,0:T(8,128)(2,1)S(1)} %fusion.11), channel_id=1, source_target_pairs={{0,8},{1,9},{2,10},{3,11},{4,12},{5,13},{6,14},{7,15},{8,0},{9,1},... | collective-permute-start | bytes 884744 | tf_op jit(solution)/shard_map/ppermute | solution.py:592

commit v3 on v2

--- a/solution.py
+++ b/solution.py
@@ -24,7 +24,7 @@
 
 def gelu_parts(value):
     size = jnp.abs(value)
-    t = 1.0 / (1.0 + ERF_P * size)
+    t = pl.reciprocal(1.0 + ERF_P * size)
     total = ERF_C[-1] * t + ERF_C[-2]
     for coefficient in ERF_C[-3::-1]:
         total = total * t + coefficient
@@ -73,21 +73,21 @@
     def _():
         c = Copies(sems)
         cx = c.start(x_in.at[clip] if clip is not None else x_in, x)
-        cj = c.start(wj_in, wj)
-        cm = c.start(wm_in, wm)
-        cu = c.start(wu_in, wu)
-        cd = c.start(wd_in, wd)
+        parts = [slice(i * D, (i + 1) * D) for i in range(3)]
+        cj = [c.start(wj_in.at[:, s], wj.at[:, s]) for s in parts]
         g1, s1, qb, vb, mb, g2, s2, db = [vec[i : i + 1, :] for i in range(8)]
         cx.wait()
         xhat, _ = norm_stats(x[...].astype(f32))
         n1[...] = (xhat * g1 + s1).astype(bf)
         c.out(n1, o_n1)
-        cj.wait()
-        for part, bias in enumerate((qb, None, vb)):
-            s = slice(part * D, (part + 1) * D)
+        for s, copy, bias in zip(parts, cj, (qb, None, vb)):
+            copy.wait()
             block = mm(n1[...], wj[:, s], 1, 0)
             qkv[:, s] = (block if bias is None else block + bias).astype(bf)
         c.out(qkv, o_qkv)
+        cm = c.start(wm_in, wm)
+        cu = c.start(wu_in, wu)
+        cd = c.start(wd_in, wd)
 
         lane = lax.broadcasted_iota(jnp.int32, (L, 128), 1)
 
@@ -119,14 +119,15 @@
         n2[...] = (xhat * g2 + s2).astype(bf)
         c.out(n2, o_n2)
         cu.wait()
-        for j in range(FF // D):
-            s = slice(j * D, (j + 1) * D)
-            for r in range(2):
-                rs = slice(r * 256, (r + 1) * 256)
-                lifted = mm(n2[rs, :], wu[:, s], 1, 0) + ub[:, s]
-                a, b = gelu_parts(lifted)
-                act[rs, s] = a.astype(bf)
-                slope[rs, s] = b.astype(bf)
+
+        def block(j, carry):
+            s = pl.ds(pl.multiple_of(j * 256, 256), 256)
+            a, b = gelu_parts(mm(n2[...], wu[:, s], 1, 0) + ub[:, s])
+            act[:, s] = a.astype(bf)
+            slope[:, s] = b.astype(bf)
+            return carry
+
+        lax.fori_loop(0, FF // 256, block, 0)
         c.out(act, o_act)
         c.out(slope, o_slope)
         cd.wait()
@@ -159,7 +160,7 @@
         out_shape=shapes(SAVED),
         in_specs=[SM, ANY, VM, VM] + [ANY] * (4 + extra),
         out_specs=[ANY] * 9,
-        scratch_shapes=scratch([xt] + ws + list(SAVED)) + [pltpu.SemaphoreType.DMA((16,))],
+        scratch_shapes=scratch([xt] + ws + list(SAVED)) + [pltpu.SemaphoreType.DMA((20,))],
         input_output_aliases={8 + i: i for i in range(extra)},
         compiler_params=PARAMS,
         cost_estimate=pl.CostEstimate(flops=8_050_000_000, bytes_accessed=30_000_000, transcendentals=5_000_000),
@@ -167,22 +168,25 @@
 
 
 def mlp_back(clip, extra, side, g_in, vec, slope_in, after_in, wu_in, wd_in, *rest):
-    o_gl, o_ga, o_vec = rest[extra : extra + 3]
-    g, slope, after, wu, wd, gl, ga, vout, sems = rest[extra + 3 :]
+    o_gl, o_ga, o_gb, o_vec = rest[extra : extra + 4]
+    g, slope, after, wu, wd, gl, ga, gb, vout, sems = rest[extra + 4 :]
 
     @pl.when(side[0] != 0)
     def _():
         c = Copies(sems)
         cg = c.start(g_in.at[clip] if clip is not None else g_in, g)
-        cd = c.start(wd_in, wd)
-        cs = c.start(slope_in, slope)
+        tiles = [slice(j * D, (j + 1) * D) for j in range(FF // D)]
+
+        def load(s):
+            return c.start(wd_in.at[s], wd.at[s]), c.start(slope_in.at[:, s], slope.at[:, s])
+
+        pairs = [load(s) for s in tiles]
         cu = c.start(wu_in, wu)
         ca = c.start(after_in, after)
         cg.wait()
-        cd.wait()
-        cs.wait()
-        for j in range(FF // D):
-            s = slice(j * D, (j + 1) * D)
+        for j, s in enumerate(tiles):
+            for copy in pairs[j]:
+                copy.wait()
             piece = (mm(g[...], wd[s, :], 1, 1) * slope[:, s].astype(f32)).astype(bf)
             gl[:, s] = piece
             vout[0:1, s] = jnp.sum(piece.astype(f32), axis=0, keepdims=True)
@@ -195,24 +199,27 @@
         vout[1:2, 0:D] = jnp.sum(e * xhat, axis=0, keepdims=True)
         vout[1:2, D : 2 * D] = jnp.sum(e, axis=0, keepdims=True)
         vout[1:2, 2 * D : 3 * D] = jnp.sum(gv, axis=0, keepdims=True)
-        ga[...] = gv + norm_back(e, xhat, rstd, vec[5:6, :])
+        whole = gv + norm_back(e, xhat, rstd, vec[5:6, :])
+        ga[...] = whole
+        gb[...] = whole.astype(bf)
         c.out(ga, o_ga)
+        c.out(gb, o_gb)
         c.out(vout, o_vec)
         c.finish()
 
 
-MB_OUT = (((L, FF), bf), ((L, D), f32), ((8, FF), f32))
+MB_OUT = (((L, FF), bf), ((L, D), f32), ((L, D), bf), ((8, FF), f32))
 
 
 def backward_mlp(side, g, clip, vec, slope, after, wu, wd, old=None):
-    extra = 0 if old is None else 3
+    extra = 0 if old is None else 4
     sc = [((L, D), bf), ((L, FF), bf), ((L, D), f32), (wu.shape, bf), (wd.shape, bf)]
     return pl.pallas_call(
         functools.partial(mlp_back, clip, extra),
         out_shape=shapes(MB_OUT),
         in_specs=[SM, ANY, VM] + [ANY] * (4 + extra),
-        out_specs=[ANY] * 3,
-        scratch_shapes=scratch(sc + list(MB_OUT)) + [pltpu.SemaphoreType.DMA((16,))],
+        out_specs=[ANY] * 4,
+        scratch_shapes=scratch(sc + list(MB_OUT)) + [pltpu.SemaphoreType.DMA((24,))],
         input_output_aliases={7 + i: i for i in range(extra)},
         compiler_params=PARAMS,
         cost_estimate=pl.CostEstimate(flops=4_830_000_000, bytes_accessed=20_000_000, transcendentals=1000),
@@ -220,8 +227,8 @@
 
 
 def attn_back(clip, lead, extra, side, ga_in, x_in, vec, flags, qkv_in, lt_in, wm_in, wj_in, *rest):
-    o_gb, o_gj, o_gh, o_vec = rest[extra : extra + 4]
-    rest = rest[extra + 4 :]
+    o_gj, o_gh, o_vec = rest[extra : extra + 3]
+    rest = rest[extra + 3 :]
     if lead:
         o_full, full, rest = rest[0], rest[-2], rest[1:-2] + rest[-1:]
     ga, x, qkv, lt, wm, wj, gm, gb, gj, gh, vout, sems = rest
@@ -233,15 +240,14 @@
         cm = c.start(wm_in, wm)
         cq = c.start(qkv_in, qkv)
         cl = c.start(lt_in, lt)
-        cj = c.start(wj_in, wj)
-        cx = c.start(x_in.at[clip] if clip is not None else x_in, x)
         cg.wait()
         cm.wait()
         gb[...] = ga[...].astype(bf)
-        c.out(gb, o_gb)
         gm[...] = mm(gb[...], wm[...], 1, 1).astype(bf)
         cq.wait()
         cl.wait()
+        cj = c.start(wj_in, wj)
+        cx = c.start(x_in.at[clip] if clip is not None else x_in, x)
         lane = lax.broadcasted_iota(jnp.int32, (L, 128), 1)
 
         def pair(p, carry):
@@ -289,15 +295,15 @@
 
 def backward_attn(side, ga, x, clip, vec, flags, qkv, lt, wm, wj, old=None):
     lead = old is not None
-    extra = 4 if lead else 0
-    outs = (((L, D), bf), ((L, 3 * D), bf), ((L, D), bf), ((8, D), f32))
+    extra = 3 if lead else 0
+    outs = (((L, 3 * D), bf), ((L, D), bf), ((8, D), f32))
     full = (((L, D), f32),) if lead else ()
-    sc = [((L, D), f32), ((L, D), x.dtype), ((L, 3 * D), bf), ((16, L), f32), (wm.shape, bf), (wj.shape, bf), ((L, D), bf)]
+    sc = [((L, D), f32), ((L, D), x.dtype), ((L, 3 * D), bf), ((16, L), f32), (wm.shape, bf), (wj.shape, bf), ((L, D), bf), ((L, D), bf)]
     return pl.pallas_call(
         functools.partial(attn_back, clip, lead, extra),
         out_shape=shapes(outs + full),
         in_specs=[SM, ANY, ANY, VM, VM] + [ANY] * (4 + extra),
-        out_specs=[ANY] * (4 + lead),
+        out_specs=[ANY] * (3 + lead),
         scratch_shapes=scratch(sc + list(outs + full)) + [pltpu.SemaphoreType.DMA((16,))],
         input_output_aliases={9 + i: i for i in range(extra)},
         compiler_params=PARAMS,
@@ -351,33 +357,36 @@
     ins, (keep, send), (a, b, o, sems) = refs[:-6], refs[-6:-4], refs[-4:]
     c = Copies(sems)
     mine = part[0]
-
-    def load(pairs):
-        return [c.start(src, dst) for src, dst in pairs]
-
+    tiles = [slice(j * D, (j + 1) * D) for j in range(FF // D)]
     if kind == "down":
         a0, b0, a1, b1, other = ins
-        waits = load(((a0, a.at[0:L]), (a1, a.at[L:])))
         rows = (b.at[0:L], b.at[L:])
+        own = [pltpu.make_async_copy(src, dst, sems.at[30 + i]) for i, (src, dst) in enumerate(zip((b0, b1), rows))]
 
         @pl.when(part[1] != 0)
         def _():
-            for src, dst, sem in zip((b0, b1), rows, (18, 19)):
-                pltpu.make_async_copy(src, dst, sems.at[sem]).start()
+            for copy in own:
+                copy.start()
 
         @pl.when(part[1] == 0)
         def _():
-            for at, dst, sem in zip((0, 1), rows, (18, 19)):
-                pltpu.make_async_copy(other.at[at], dst, sems.at[sem]).start()
-
-        for src, dst, sem in zip((b0, b1), rows, (18, 19)):
-            pltpu.make_async_copy(src, dst, sems.at[sem]).wait()
-        for w in waits:
-            w.wait()
+            for at in range(2):
+                pltpu.make_async_copy(other.at[at], rows[at], sems.at[30 + at]).start()
+
+        def load(s):
+            return c.start(a0.at[:, s], a.at[0:L, s]), c.start(a1.at[:, s], a.at[L:, s])
+
+        loads = [load(s) for s in tiles[:2]]
+        for copy in own:
+            copy.wait()
         height = FF // count
         per = D // height // 2
-        for j in range(FF // D):
-            tile = mm(a[:, j * D : (j + 1) * D], b[...], 0, 0).astype(bf)
+        for j, s in enumerate(tiles):
+            for copy in loads[j]:
+                copy.wait()
+            if j + 2 < len(tiles):
+                loads.append(load(tiles[j + 2]))
+            tile = mm(a[:, s], b[...], 0, 0).astype(bf)
             for i in range(2 * per):
                 o[i % 2, j * per + i // 2] = tile[i * height : (i + 1) * height]
             s = slice(j * per, (j + 1) * per)
@@ -385,43 +394,45 @@
             c.out(o.at[1 - mine, s], send.at[s])
     else:
         height = D // count
-        groups = [ins[i : i + 4] for i in range(0, len(ins), 4)]
-        loads = []
-        column = 0
-        for g, (a0, b0, a1, b1) in enumerate(groups):
-            width = b0.shape[1]
-            r = slice(column, column + width)
+        units = []
+        for g, first in enumerate(range(0, len(ins), 4)):
+            a0, b0, a1, b1 = ins[first : first + 4]
             l = slice(g * D, (g + 1) * D)
-            loads.append(load(((a0, a.at[0:L, l]), (a1, a.at[L:, l]), (b0, b.at[0:L, r]), (b1, b.at[L:, r]))))
-            column += width
-        t = 0
-        for g, (a0, b0, a1, b1) in enumerate(groups):
-            for w in loads[g]:
-                w.wait()
-            for _ in range(b0.shape[1] // D):
-                tile = mm(a[:, g * D : (g + 1) * D], b[:, t * D : (t + 1) * D], 0, 0).astype(bf)
-                for i in range(count):
-                    o[i % 2, i // 2, t * height : (t + 1) * height] = tile[i * height : (i + 1) * height]
-                t += 1
-        c.out(o.at[mine], keep)
-        c.out(o.at[1 - mine], send)
+            moves = [(a0, a.at[0:L, l]), (a1, a.at[L:, l])]
+            for s in tiles[: b0.shape[1] // D]:
+                r = slice(len(units) * D, (len(units) + 1) * D)
+                moves += [(b0.at[:, s], b.at[0:L, r]), (b1.at[:, s], b.at[L:, r])]
+                units.append((l, r, moves))
+                moves = []
+        loads = [[c.start(*move) for move in unit[2]] for unit in units[:2]]
+        for t, (l, r, _) in enumerate(units):
+            for copy in loads[t]:
+                copy.wait()
+            if t + 2 < len(units):
+                loads.append([c.start(*move) for move in units[t + 2][2]])
+            tile = mm(a[:, l], b[:, r], 0, 0).astype(bf)
+            s = slice(t * height, (t + 1) * height)
+            for i in range(count):
+                o[i % 2, i // 2, s] = tile[i * height : (i + 1) * height]
+            c.out(o.at[mine, :, s], keep.at[:, s])
+            c.out(o.at[1 - mine, :, s], send.at[:, s])
     c.finish()
 
 
 def split_gradient(kind, count, part, groups):
     flat = [one for group in groups for one in group]
-    pairs = groups if kind == "both" else groups[:1]
-    m = sum(group[0].shape[1] for group in pairs)
-    n = sum(group[1].shape[1] for group in pairs)
-    half = jax.ShapeDtypeStruct((count // 2, 4 * D // count, D), bf)
+    m = sum(group[0].shape[1] for group in groups)
+    n = sum(group[1].shape[1] for group in groups)
+    area = sum(group[0].shape[1] * group[1].shape[1] for group in groups)
+    half = jax.ShapeDtypeStruct((count // 2, area // D // count, D), bf)
     return pl.pallas_call(
         functools.partial(split_grad, kind, count),
         out_shape=(half, half),
         in_specs=[SM] + [ANY] * len(flat),
         out_specs=(ANY, ANY),
-        scratch_shapes=scratch([((2 * L, m), bf), ((2 * L, n), bf), ((2,) + half.shape, bf)]) + [pltpu.SemaphoreType.DMA((20,))],
+        scratch_shapes=scratch([((2 * L, m), bf), ((2 * L, n), bf), ((2,) + half.shape, bf)]) + [pltpu.SemaphoreType.DMA((32,))],
         compiler_params=PARAMS,
-        cost_estimate=pl.CostEstimate(flops=16 * L * D * D, bytes_accessed=2 * (2 * L * (m + n) + 4 * D * D), transcendentals=0),
+        cost_estimate=pl.CostEstimate(flops=4 * L * area, bytes_accessed=2 * (2 * L * (m + n) + area), transcendentals=0),
     )(part, *flat)
 
 
@@ -453,21 +464,19 @@
 
 def summed(values, place):
     levels = lax.axis_size("batch").bit_length() - 1
-    cut = [level for level in (2, 3) if level < levels]
+    split = min(levels, 3)
 
     def exchange(block, level):
         return swapped(block, 1 << level)
 
-    values = added(values, exchange(values, 0)).astype(bf)
-    for level in cut:
+    for level in range(split):
         own = (place >> level) & 1
         parts = values.reshape(2, -1, D)
         came = exchange(lax.dynamic_index_in_dim(parts, 1 - own, 0, False), level)
         values = added(lax.dynamic_index_in_dim(parts, own, 0, False), came).astype(bf)
-    for level in range(1, levels):
-        if level not in cut:
-            values = added(values, exchange(values, level)).astype(bf)
-    for level in reversed(cut):
+    for level in range(split, levels):
+        values = added(values, exchange(values, level)).astype(bf)
+    for level in reversed(range(split)):
         own = (place >> level) & 1
         came = exchange(values, level)
         low, high = jnp.where(own == 0, values, came), jnp.where(own == 0, came, values)
@@ -479,7 +488,7 @@
     half = L // 2
     for out, s in ((here, slice(0, half)), (moved, slice(half, L))):
         out[0:half, :] = (b0[s, :] + b1[s, :]).astype(bf)
-        out[half:, :] = jnp.zeros((64, D), bf)
+        out[half:, :] = jnp.zeros((out.shape[0] - half, D), bf)
     vm = v0[...] + v1[...]
     va = a0[...] + a1[...]
     for out in (here, moved):
@@ -490,110 +499,13 @@
 
 
 def collect(*values):
-    half = jax.ShapeDtypeStruct((L // 2 + 64, D), bf)
     return pl.pallas_call(
         collect_small,
-        out_shape=(half, half),
+        out_shape=[jax.ShapeDtypeStruct((L // 2 + more, D), bf) for more in (128, 16)],
         in_specs=[SM] + [VM] * 6,
-        out_specs=(VM, VM),
+        out_specs=[VM, VM],
         cost_estimate=pl.CostEstimate(flops=1_000_000, bytes_accessed=5_000_000, transcendentals=0),
     )(*values)
-
-
-def passed_along(block, distance):
-    devices = range(lax.axis_size("section"))
-    route = [(i - distance, i) for i in devices if i - distance in devices]
-    return lax.ppermute(block, "section", route)
-
-
-def scatter(values):
-    return lax.psum_scatter(values, "batch", scatter_dimension=0, tiled=True)
-
-
-def split_grad(kind, count, part, *refs):
-    ins, (keep, send), (a, b, o, sems) = refs[:-6], refs[-6:-4], refs[-4:]
-    c = Copies(sems)
-    mine = part[0]
-
-    def load(pairs):
-        return [c.start(src, dst) for src, dst in pairs]
-
-    if kind == "down":
-        a0, b0, a1, b1, other = ins
-        waits = load(((a0, a.at[0:L]), (a1, a.at[L:])))
-        rows = (b.at[0:L], b.at[L:])
-
-        @pl.when(part[1] != 0)
-        def _():
-            for src, dst, sem in zip((b0, b1), rows, (18, 19)):
-                pltpu.make_async_copy(src, dst, sems.at[sem]).start()
-
-        @pl.when(part[1] == 0)
-        def _():
-            for at, dst, sem in zip((0, 1), rows, (18, 19)):
-                pltpu.make_async_copy(other.at[at], dst, sems.at[sem]).start()
-
-        for src, dst, sem in zip((b0, b1), rows, (18, 19)):
-            pltpu.make_async_copy(src, dst, sems.at[sem]).wait()
-        for w in waits:
-            w.wait()
-        height = FF // count
-        per = D // height // 2
-        for j in range(FF // D):
-            tile = mm(a[:, j * D : (j + 1) * D], b[...], 0, 0).astype(bf)
-            for i in range(2 * per):
-                o[i % 2, j * per + i // 2] = tile[i * height : (i + 1) * height]
-            s = slice(j * per, (j + 1) * per)
-            c.out(o.at[mine, s], keep.at[s])
-            c.out(o.at[1 - mine, s], send.at[s])
-    else:
-        height = D // count
-        groups = [ins[i : i + 4] for i in range(0, len(ins), 4)]
-        loads = []
-        column = 0
-        for g, (a0, b0, a1, b1) in enumerate(groups):
-            width = b0.shape[1]
-            r = slice(column, column + width)
-            l = slice(g * D, (g + 1) * D)
-            loads.append(load(((a0, a.at[0:L, l]), (a1, a.at[L:, l]), (b0, b.at[0:L, r]), (b1, b.at[L:, r]))))
-            column += width
-        t = 0
-        for g, (a0, b0, a1, b1) in enumerate(groups):
-            for w in loads[g]:
-                w.wait()
-            for _ in range(b0.shape[1] // D):
-                tile = mm(a[:, g * D : (g + 1) * D], b[:, t * D : (t + 1) * D], 0, 0).astype(bf)
-                for i in range(count):
-                    o[i % 2, i // 2, t * height : (t + 1) * height] = tile[i * height : (i + 1) * height]
-                t += 1
-        c.out(o.at[mine], keep)
-        c.out(o.at[1 - mine], send)
-    c.finish()
-
-
-def split_gradient(kind, count, part, groups):
-    flat = [one for group in groups for one in group]
-    pairs = groups if kind == "both" else groups[:1]
-    m = sum(group[0].shape[1] for group in pairs)
-    n = sum(group[1].shape[1] for group in pairs)
-    half = jax.ShapeDtypeStruct((count // 2, 4 * D // count, D), bf)
-    return pl.pallas_call(
-        functools.partial(split_grad, kind, count),
-        out_shape=(half, half),
-        in_specs=[SM] + [ANY] * len(flat),
-        out_specs=(ANY, ANY),
-        scratch_shapes=scratch([((2 * L, m), bf), ((2 * L, n), bf), ((2,) + half.shape, bf)]) + [pltpu.SemaphoreType.DMA((20,))],
-        compiler_params=PARAMS,
-        cost_estimate=pl.CostEstimate(flops=16 * L * D * D, bytes_accessed=2 * (2 * L * (m + n) + 4 * D * D), transcendentals=0),
-    )(part, *flat)
-
-
-def swapped(values, bit):
-    return lax.ppermute(values, "batch", [(i, i ^ bit) for i in range(lax.axis_size("batch"))])
-
-
-def added(left, right):
-    return left.astype(f32) + right.astype(f32)
 
 
 def shards(clips, mask_flags, mask_embed, pos_embed, first_gain, first_shift, joint_weight, query_bias, value_bias,
@@ -613,28 +525,25 @@
     part = jnp.stack([place % 2, lead[0]]).astype(jnp.int32)
     fast = (D // count) % 16 == 0
 
-    def handed(block, distance):
-        return passed_along(block, distance)
-
     lead0 = forward(lead, blended, 0, vec, up_bias, weights)
-    arriving0 = handed(lead0[8], 1)
+    arriving0 = passed_along(lead0[8], 1)
     lead1 = forward(lead, blended, 1, vec, up_bias, weights)
-    arriving1 = handed(lead1[8], 1)
+    arriving1 = passed_along(lead1[8], 1)
 
     def back(side, saved, g, x, clip, old):
         _, qkv, lt, _, after_rows, _, _, slope, _ = saved
         own = clip if old is None else None
-        gl, ga, vm = backward_mlp(side, g, own, vec, slope, after_rows, wu, wd, old and old[:3])
+        gl, ga, gb, vm = backward_mlp(side, g, own, vec, slope, after_rows, wu, wd, old and old[:4])
         at = None if old is None else clip
-        gb, gj, gh, va, *full = backward_attn(side, ga, x, at, vec, flags, qkv, lt, wm, wj, old and old[3:])
-        return (gl, ga, vm, gb, gj, gh, va), full
+        gj, gh, va, *full = backward_attn(side, ga, x, at, vec, flags, qkv, lt, wm, wj, old and old[4:])
+        return (gl, ga, gb, vm, gj, gh, va), full
 
     saved0 = forward(tail, arriving0, None, vec, up_bias, weights, lead0)
     grads0, _ = back(tail, saved0, out_grad, arriving0, 0, None)
-    leaving0 = handed(grads0[5], -1)
+    leaving0 = passed_along(grads0[5], -1)
     saved1 = forward(tail, arriving1, None, vec, up_bias, weights, lead1)
     grads1, _ = back(tail, saved1, out_grad, arriving1, 1, None)
-    leaving1 = handed(grads1[5], -1)
+    leaving1 = passed_along(grads1[5], -1)
     grads0, (blend0,) = back(lead, saved0, leaving0, blended, 0, grads0)
     va0 = grads0[6]
 
@@ -643,32 +552,31 @@
         part_d, va0 = after(part, va0)
         down = split_gradient("down", count, part_d, [(saved0[6], leaving0, act_1, leaving1, out_grad)])
         lead_m, *down = after(lead, *down)
-        gl1, ga1, vm1 = backward_mlp(lead_m, leaving1, None, vec, slope_1, after_1, wu, wd, grads1[:3])
+        gl1, ga1, gb1, vm1 = backward_mlp(lead_m, leaving1, None, vec, slope_1, after_1, wu, wd, grads1[:4])
         down = halve(*down, place, 0)
         part_u, *down = after(part, *down)
-        up = split_gradient("up", count, part_u, [(saved0[5], grads0[0], n2_1, gl1)])
+        up = split_gradient("up", count, part_u, [(saved0[5], grads0[0], n2_1, gl1), (saved0[3], grads0[2], mixed_1, gb1)])
+        up = halve(*up, place, 0)
         lead_a, *up = after(lead, *up)
     else:
-        gl1, ga1, vm1 = backward_mlp(lead, leaving1, None, vec, slope_1, after_1, wu, wd, grads1[:3])
+        gl1, ga1, gb1, vm1 = backward_mlp(lead, leaving1, None, vec, slope_1, after_1, wu, wd, grads1[:4])
         lead_a = lead
-    gb1, gj1, gh1, va1, blend1 = backward_attn(lead_a, ga1, blended, 1, vec, flags, qkv_1, lt_1, wm, wj, grads1[3:])
-    here, moved = collect(lead, blend0, blend1, grads0[2], vm1, va0, va1)
-    joint_group, mixer_group = (saved0[0], grads0[4], n1_1, gj1), (saved0[3], grads0[3], mixed_1, gb1)
+    gj1, gh1, va1, blend1 = backward_attn(lead_a, ga1, blended, 1, vec, flags, qkv_1, lt_1, wm, wj, grads1[4:])
+    here, moved = collect(lead, blend0, blend1, grads0[3], vm1, va0, va1)
+    joint_group, mixer_group = (saved0[0], grads0[4], n1_1, gj1), (saved0[3], grads0[2], mixed_1, gb1)
     if fast:
-        up = halve(*up, place, 0)
         down = halve(*down, place, 1)
-        part_b, *rest = after(part, *up, *down)
-        up, down = rest[:2], rest[2:]
-        both = split_gradient("both", count, part_b, [joint_group, mixer_group])
+        part_b, *down = after(part, *down)
+        joint = split_gradient("joint", count, part_b, [joint_group])
         levels = count.bit_length() - 1
-        down, up, both = [functools.reduce(lambda pair, level: halve(*pair, place, level), range(at, levels), value)
-                          for at, value in ((2, down), (1, up), (0, both))]
+        down, up, joint = [functools.reduce(lambda pair, level: halve(*pair, place, level), range(at, levels), value)
+                           for at, value in ((2, down), (1, up), (0, joint))]
         height = D // count
 
         def wide(block):
             return jnp.swapaxes(block.reshape(-1, height, D), 0, 1).reshape(height, -1)
 
-        up, joint, mixer = wide(up), wide(both[: 3 * height]), both[3 * height :]
+        up, joint, mixer = wide(up[: 4 * height]), wide(joint), up[4 * height :]
     else:
         g0 = jnp.where(first, leaving0, out_grad[0])
         g1 = jnp.where(first, leaving1, out_grad[1])
@@ -681,7 +589,7 @@
     layer_outputs = jnp.stack([saved0[8], saved1[8]])[None]
     input_grads = jnp.stack([grads0[5], gh1])[None]
     half = L // 2
-    arrived = handed(moved, 1)[: half + 16]
+    arrived = passed_along(moved, 1)
     top = jnp.where(first, here[: half + 16], arrived)
     total = summed(jnp.concatenate([top, here[half + 16 :]]), place).astype(f32)
     grad_position = total[:half]

time: 430 us -> 414 us (0.963)
  waiting for transfers between devices: 141 us -> 157 us
  starting transfers between devices: 38.2 us -> 26.2 us
  Pallas kernels: 191 us -> 181 us
  other arithmetic: 38.8 us -> 30.5 us
  local copies, waits for them, and re-layouts: 15.9 us -> 11 us
    pallas_call x4, Pallas kernels: 80.7 us -> 58.6 us  [forward(): pl.pallas_call(functools.partial(front, clip, extra), out_shape=shapes(SA...]
    ppermute x5, waiting for transfers between devices: 65.5 us -> 82.2 us  [passed_along(): return lax.ppermute(block, 'section', route)]
    pallas_call x4, Pallas kernels: 28.4 us -> 42.1 us  [backward_mlp(): pl.pallas_call(functools.partial(mlp_back, clip, extra), out_shape=shapes...]
    ppermute x18 -> x19, starting transfers between devices: 30.7 us -> 18.4 us  [swapped(): lax.ppermute(values, 'batch', [(i, i ^ bit) for i in range(lax.axis_size(...]
    ppermute x18 -> x19, waiting for transfers between devices: 75.1 us -> 74.5 us  [swapped(): lax.ppermute(values, 'batch', [(i, i ^ bit) for i in range(lax.axis_size(...]
  transfers between devices with their start and end apart: 23 -> 24, of which waited for: 13 -> 14; matrix products, arithmetic and copies ran while one was open for 8% -> 6% of each run, Pallas kernels for 33% -> 32%
where the time goes in v3:
time: 414 us; the launch traced here: 407 us
  Pallas kernels  181 us (44%)
  waiting for transfers between devices  157 us (38%)
  other arithmetic  30.5 us (7%)
  starting transfers between devices  26.2 us (6%)
  local copies, waits for them, and re-layouts  11 us (3%)
    ppermute x5, waiting for transfers between devices, passed_along(): return lax.ppermute(block, 'section', route)  82.2 us
    ppermute x19, waiting for transfers between devices, swapped(): lax.ppermute(values, 'batch', [(i, i ^ bit) for i in range(lax.axis_size(...  74.5 us
    pallas_call x4, Pallas kernels, forward(): pl.pallas_call(functools.partial(front, clip, extra), out_shape=shapes(SA...  58.6 us
    pallas_call x4, Pallas kernels, backward_attn(): pl.pallas_call(functools.partial(attn_back, clip, lead, extra), out_shape...  44.7 us
    pallas_call x4, Pallas kernels, backward_mlp(): pl.pallas_call(functools.partial(mlp_back, clip, extra), out_shape=shapes...  42.1 us
    pallas_call x3, Pallas kernels, split_gradient(): pl.pallas_call(functools.partial(split_grad, kind, count), out_shape=(hal...  32.6 us
    ppermute x19, starting transfers between devices, swapped(): lax.ppermute(values, 'batch', [(i, i ^ bit) for i in range(lax.axis_size(...  18.4 us
    convert_element_type x10, other arithmetic, pick(): added(lax.dynamic_index_in_dim(kept, side, 1, False), lax.dynamic_index_i...  17.3 us
  transfers between devices with their start and end apart: 24, of which 14 were waited for; matrix products, arithmetic and copies ran while one was open for 6% of the time, Pallas kernels for 32%

profile of v3, /device:TPU:0, one launch (start us, length us, event | category | flops | bytes accessed | tf_op | source)
XLA Modules:
  0.0 407.1 jit_solution(5875254281968889086)
XLA Ops:
  0.7 0.7 convert_element_type.351
  2.1 4.1 %add_add_fusion.x_in = f32[2,512,768]{2,1,0:T(8,128)} fusion(bf16[2,512,768]{2,1,0:T(8,128)(2,1)} %param.18, f32[512,768]{1,0:T(8,128)} %param.21, f32[768]{0:T(1024)} %param.20, f32[2,512]{1,0:T(2,128)S(1)} %convert_element_type.351, f32[2,512]{1,0:T(2,128)S(1)} %broadcast_subtract_fusion), kind=kLoop, calls=%fused_computation | loop fusion | flops 3932160 | bytes 6302720 | tf_op jit(solution)/shard_map/add | solution.py:518
  7.0 28.1 %shard_map.305 = (bf16[512,768]{1,0:T(8,128)(2,1)}, bf16[512,2304]{1,0:T(8,128)(2,1)}, f32[16,512]{1,0:T(8,128)}, bf16[512,768]{1,0:T(8,128)(2,1)}, f32[512,768]...) custom-call(s32[1]{0:T(128)} %bitcast.side.flag, ...), custom_call_target="tpu_custom_call" | custom-call | flops 8049999872 | bytes 30000000 | tf_op jit(solution)/shard_map/pallas_call | solution.py:158
  35.1 2.2 collective-permute-start
  37.3 28.2 %shard_map.307 = (bf16[512,768]{1,0:T(8,128)(2,1)}, bf16[512,2304]{1,0:T(8,128)(2,1)}, f32[16,512]{1,0:T(8,128)}, bf16[512,768]{1,0:T(8,128)(2,1)}, f32[512,768]...) custom-call(s32[1]{0:T(128)} %bitcast.side.flag, ...), custom_call_target="tpu_custom_call" | custom-call | flops 8049999872 | bytes 30000000 | tf_op jit(solution)/shard_map/pallas_call | solution.py:158
  65.5 1.3 collective-permute-start.1
  66.9 1.0 copy.68.flags
  68.5 1.2 shard_map.306
  69.7 8.3 %shard_map.309 = (bf16[512,3072]{1,0:T(8,128)(2,1)}, f32[512,768]{1,0:T(8,128)}, bf16[512,768]{1,0:T(8,128)(2,1)}, f32[8,3072]{1,0:T(8,128)}) custom-call(s32[1]{0:T(128)S(6)} %sub.30.side, bf16[2,512,768]{2,1,0:T(8,128)(2,1)} %refs_4_.1, f32[8,768]{1,0:T(8,128)} %concatenate.15.vec, bf16[512,3072]{1,0:T(8,128)(2,1)} %get-tuple-element.125.slope_in, ...), custom_call_target="tpu_custom_call" | custom-call | flops 4830000128 | bytes 20000000 | tf_op jit(solution)/shard_map/pallas_call | solution.py:217
  77.9 1.2 shard_map.310
  79.2 1.3 collective-permute-start.2
  80.5 4.4 %collective-permute-done.1.x_in = bf16[512,768]{1,0:T(8,128)(2,1)S(1)} collective-permute-done((bf16[512,768]{1,0:T(8,128)(2,1)}, bf16[512,768]{1,0:T(8,128)(2,1)S(1)}, u32[]{:S(2)}, u32[]{:S(2)}) %collective-permute-start.1) | collective-permute-done | bytes 786464 | tf_op jit(solution)/shard_map/ppermute | solution.py:349
  84.9 0.9 copy-done.20
  85.7 1.1 shard_map.308
  86.8 8.0 %shard_map.313 = (bf16[512,3072]{1,0:T(8,128)(2,1)}, f32[512,768]{1,0:T(8,128)}, bf16[512,768]{1,0:T(8,128)(2,1)}, f32[8,3072]{1,0:T(8,128)}) custom-call(s32[1]{0:T(128)S(6)} %sub.30.side, bf16[2,512,768]{2,1,0:T(8,128)(2,1)} %refs_4_.1, f32[8,768]{1,0:T(8,128)} %concatenate.15.vec, bf16[512,3072]{1,0:T(8,128)(2,1)} %get-tuple-element.142.slope_in, ...), custom_call_target="tpu_custom_call" | custom-call | flops 4830000128 | bytes 20000000 | tf_op jit(solution)/shard_map/pallas_call | solution.py:217
  94.8 1.2 shard_map.314
  96.1 1.3 collective-permute-start.3
  97.4 40.5 %collective-permute-done.2.g_in.refs_1_ = bf16[512,768]{1,0:T(8,128)(2,1)S(1)} collective-permute-done((bf16[512,768]{1,0:T(8,128)(2,1)}, bf16[512,768]{1,0:T(8,128)(2,1)S(1)}, u32[]{:S(2)}, u32[]{:S(2)}) %collective-permute-start.2) | collective-permute-done | bytes 786464 | tf_op jit(solution)/shard_map/ppermute | solution.py:349
  137.8 0.9 copy-done.5
  138.7 13.0 %shard_map.311 = (bf16[512,3072]{1,0:T(8,128)(2,1)}, f32[512,768]{1,0:T(8,128)}, bf16[512,768]{1,0:T(8,128)(2,1)}, f32[8,3072]{1,0:T(8,128)}) custom-call(s32[1]{0:T(128)} %bitcast.side.flag, bf16[512,768]{1,0:T(8,128)(2,1)} %copy-done.5, f32[8,768]{1,0:T(8,128)} %concatenate.15.vec, ...), custom_call_target="tpu_custom_call", output_to_operand_aliasing={{0}: (7, {}), {1}: (8, {}), {2}: (9, {}), {3}: (10, {})} | custom-call | flops 4830000128 | bytes 20000000 | tf_op jit(solution)/shard_map/pallas_call | solution.py:217
  151.8 21.2 %shard_map.312 = (bf16[512,2304]{1,0:T(8,128)(2,1)}, bf16[512,768]{1,0:T(8,128)(2,1)}, f32[8,768]{1,0:T(8,128)}, f32[512,768]{1,0:T(8,128)}) custom-call(s32[1]{0:T(128)} %bitcast.side.flag, f32[512,768]{1,0:T(8,128)} %get-tuple-element.134.ga_in, f32[2,512,768]{2,1,0:T(8,128)} %add_add_fusion.x_in, ...), custom_call_target="tpu_custom_call", output_to_operand_aliasing={{0}: (9, {}), {1}: (10, {}), {2}: (11, {})} | custom-call | flops 4400000000 | bytes 20000000 | tf_op jit(solution)/shard_map/pallas_call | solution.py:302
  173.0 28.5 %collective-permute-done.3.refs_3_.g_in = bf16[512,768]{1,0:T(8,128)(2,1)S(1)} collective-permute-done((bf16[512,768]{1,0:T(8,128)(2,1)}, bf16[512,768]{1,0:T(8,128)(2,1)S(1)}, u32[]{:S(2)}, u32[]{:S(2)}) %collective-permute-start.3) | collective-permute-done | bytes 786464 | tf_op jit(solution)/shard_map/ppermute | solution.py:349
  201.5 0.9 copy-done.6
  202.4 11.1 %shard_map.315 = (bf16[8,192,768]{2,1,0:T(8,128)(2,1)}, bf16[8,192,768]{2,1,0:T(8,128)(2,1)}) custom-call(s32[2]{0:T(128)} %pad_add_fusion.part, bf16[512,3072]{1,0:T(8,128)(2,1)} %get-tuple-element.140.refs_0_, bf16[512,768]{1,0:T(8,128)(2,1)} %copy-done.5, bf16[512,3072]{1,0:T(8,128)(2,1)} %get-tuple-element.141.refs_2_, bf16[512,768]{1,0:T(8,128)(2,1)} %copy-done.6, ...), custom_call_target="tpu_custom_call" | custom-call | flops 4831838208 | bytes 12582912 | tf_op jit(solution)/shard_map/pallas_call | solution.py:428
  213.6 12.8 %shard_map.316 = (bf16[512,3072]{1,0:T(8,128)(2,1)}, f32[512,768]{1,0:T(8,128)}, bf16[512,768]{1,0:T(8,128)(2,1)}, f32[8,3072]{1,0:T(8,128)}) custom-call(s32[1]{0:T(128)} %bitcast.side.flag, bf16[512,768]{1,0:T(8,128)(2,1)} %copy-done.6, f32[8,768]{1,0:T(8,128)} %concatenate.15.vec, ...), custom_call_target="tpu_custom_call", output_to_operand_aliasing={{0}: (7, {}), {1}: (8, {}), {2}: (9, {}), {3}: (10, {})} | custom-call | flops 4830000128 | bytes 20000000 | tf_op jit(solution)/shard_map/pallas_call | solution.py:217
  226.5 4.3 %fusion.3 = (bf16[4,192,768]{2,1,0:T(8,128)(2,1)}, bf16[4,192,768]{2,1,0:T(8,128)(2,1)}) fusion(bf16[4,2,192,768]{3,2,1,0:T(8,128)(2,1)} %bitcast.12, s32[]{:T(128)S(6)} %select_n.134, bf16[4,2,192,768]{3,2,1,0:T(8,128)(2,1)} %bitcast.124, s32[]{:T(128)S(6)} %select_n.133), kind=kLoop, calls=%fused_computation.14 | loop fusion | flops 4718592 | bytes 7077896 | tf_op jit(solution)/shard_map/convert_element_type | solution.py:460
  230.8 12.6 %shard_map.317 = (bf16[8,240,768]{2,1,0:T(8,128)(2,1)}, bf16[8,240,768]{2,1,0:T(8,128)(2,1)}) custom-call(s32[2]{0:T(128)} %pad_add_fusion.part, bf16[512,768]{1,0:T(8,128)(2,1)} %get-tuple-element.153.refs_0_, bf16[512,3072]{1,0:T(8,128)(2,1)} %get-tuple-element.154.refs_1_, bf16[512,768]{1,0:T(8,128)(2,1)} %get-tuple-element.155.refs_2_, ...), custom_call_target="tpu_custom_call" | custom-call | flops 6039797760 | bytes 16908288 | tf_op jit(solution)/shard_map/pallas_call | solution.py:428
  243.9 1.6 collective-permute-start.14
  245.6 3.6 collective-permute-done.5
  249.2 3.7 fusion.1
  252.9 21.1 %shard_map.318 = (bf16[512,2304]{1,0:T(8,128)(2,1)}, bf16[512,768]{1,0:T(8,128)(2,1)}, f32[8,768]{1,0:T(8,128)}, f32[512,768]{1,0:T(8,128)}) custom-call(s32[1]{0:T(128)} %bitcast.side.flag, f32[512,768]{1,0:T(8,128)} %get-tuple-element.168.ga_in, f32[2,512,768]{2,1,0:T(8,128)} %add_add_fusion.x_in, ...), custom_call_target="tpu_custom_call", output_to_operand_aliasing={{0}: (9, {}), {1}: (10, {}), {2}: (11, {})} | custom-call | flops 4400000000 | bytes 20000000 | tf_op jit(solution)/shard_map/pallas_call | solution.py:302
  274.0 3.1 shard_map.319
  277.0 1.7 collective-permute-start.6
  278.7 0.9 slice.54
  279.7 8.8 %collective-permute-done.6 = bf16[272,768]{1,0:T(8,128)(2,1)S(1)} collective-permute-done((bf16[272,768]{1,0:T(8,128)(2,1)}, bf16[272,768]{1,0:T(8,128)(2,1)S(1)}, u32[]{:S(2)}, u32[]{:S(2)}) %collective-permute-start.6) | collective-permute-done | bytes 417824 | tf_op jit(solution)/shard_map/ppermute | solution.py:349
  288.5 1.0 slice_select_fusion
  289.6 0.8 copy-done.1
  290.5 2.1 fusion.8
  292.6 2.0 fusion.9
  294.7 1.7 collective-permute-start.8
  296.4 8.9 %shard_map.320 = (bf16[8,144,768]{2,1,0:T(8,128)(2,1)}, bf16[8,144,768]{2,1,0:T(8,128)(2,1)}) custom-call(s32[2]{0:T(128)} %pad_add_fusion.part, bf16[512,768]{1,0:T(8,128)(2,1)} %get-tuple-element.183.refs_0_, bf16[512,2304]{1,0:T(8,128)(2,1)} %get-tuple-element.184.refs_1_, bf16[512,768]{1,0:T(8,128)(2,1)} %get-tuple-element.185.refs_2_, ...), custom_call_target="tpu_custom_call" | custom-call | flops 3623878656 | bytes 9830400 | tf_op jit(solution)/shard_map/pallas_call | solution.py:428
  305.6 0.9 fusion.15
  306.6 1.7 collective-permute-start.9
  308.6 2.5 collective-permute-done.9
  311.2 2.8 collective-permute-start.10
  314.4 10.1 %collective-permute-done.10 = bf16[48,768]{1,0:T(8,128)(2,1)S(1)} collective-permute-done((bf16[48,768]{1,0:T(8,128)(2,1)S(1)}, bf16[48,768]{1,0:T(8,128)(2,1)S(1)}, u32[]{:S(2)}, u32[]{:S(2)}) %collective-permute-start.10) | collective-permute-done | bytes 73760 | tf_op jit(solution)/shard_map/ppermute | solution.py:440
  324.5 3.6 collective-permute-start.11
  328.1 1.0 add_convert_fusion.12
  329.2 1.5 collective-permute-done.11
  331.3 12.6 %collective-permute-done.23 = bf16[1,192,768]{2,1,0:T(8,128)(2,1)S(1)} collective-permute-done((bf16[1,192,768]{2,1,0:T(8,128)(2,1)S(1)}, bf16[1,192,768]{2,1,0:T(8,128)(2,1)S(1)}, u32[]{:S(2)}, u32[]{:S(2)}) %collective-permute-start.23) | collective-permute-done | bytes 294944 | tf_op jit(solution)/shard_map/ppermute | solution.py:440
  343.9 0.9 convert_add_fusion.4
  344.8 5.8 %collective-permute-done.12 = bf16[96,768]{1,0:T(8,128)(2,1)S(1)} collective-permute-done((bf16[96,768]{1,0:T(8,128)(2,1)S(1)}, bf16[96,768]{1,0:T(8,128)(2,1)S(1)}, u32[]{:S(2)}, u32[]{:S(2)}) %collective-permute-start.12) | collective-permute-done | bytes 147488 | tf_op jit(solution)/shard_map/ppermute | solution.py:440
  350.8 1.9 add_convert_fusion.5
  353.2 1.9 add_convert_fusion.7
  355.1 1.6 collective-permute-start.20
  356.8 1.9 maximum_bitcast_fusion
  359.0 0.9 fusion.14
  359.9 14.9 %collective-permute-done.16 = bf16[4,144,768]{2,1,0:T(8,128)(2,1)S(1)} collective-permute-done((bf16[4,144,768]{2,1,0:T(8,128)(2,1)S(1)}, bf16[4,144,768]{2,1,0:T(8,128)(2,1)S(1)}, u32[]{:S(2)}, u32[]{:S(2)}) %collective-permute-start.16) | collective-permute-done | bytes 884768 | tf_op jit(solution)/shard_map/ppermute | solution.py:440
  375.0 1.6 collective-permute-start.17
  378.9 14.8 %collective-permute-done.17 = bf16[2,144,768]{2,1,0:T(8,128)(2,1)S(1)} collective-permute-done((bf16[2,144,768]{2,1,0:T(8,128)(2,1)S(1)}, bf16[2,144,768]{2,1,0:T(8,128)(2,1)S(1)}, u32[]{:S(2)}, u32[]{:S(2)}) %collective-permute-start.17) | collective-permute-done | bytes 442400 | tf_op jit(solution)/shard_map/ppermute | solution.py:440
  394.2 1.2 collective-permute-done.21
  396.7 1.1 broadcast_in_dim_reshape.7
  397.8 7.4 %collective-permute-done.18 = bf16[1,144,768]{2,1,0:T(8,128)(2,1)S(1)} collective-permute-done((bf16[1,144,768]{2,1,0:T(8,128)(2,1)S(1)}, bf16[1,144,768]{2,1,0:T(8,128)(2,1)S(1)}, u32[]{:S(2)}, u32[]{:S(2)}) %collective-permute-start.18) | collective-permute-done | bytes 221216 | tf_op jit(solution)/shard_map/ppermute | solution.py:440
  405.6 1.1 broadcast_in_dim_reshape.6
  (90 shorter events, 10.2 us)
Async XLA Ops:
  2.0 4.2 %copy-start.12 = (f32[1,768]{1,0:T(1,128)S(1)}, f32[1,768]{1,0:T(1,128)}, u32[]{:S(2)}) copy-start(f32[1,768]{1,0:T(1,128)} %param.22) | copy-start | bytes 9220
  2.0 4.2 %copy-start.13 = (f32[1,768]{1,0:T(1,128)S(1)}, f32[1,768]{1,0:T(1,128)}, u32[]{:S(2)}) copy-start(f32[1,768]{1,0:T(1,128)} %param.23) | copy-start | bytes 9220
  2.0 4.2 %copy-start.14 = (f32[1,768]{1,0:T(1,128)S(1)}, f32[1,768]{1,0:T(1,128)}, u32[]{:S(2)}) copy-start(f32[1,768]{1,0:T(1,128)} %param.25) | copy-start | bytes 9220
  2.1 4.2 %copy-start.15 = (f32[1,768]{1,0:T(1,128)S(1)}, f32[1,768]{1,0:T(1,128)}, u32[]{:S(2)}) copy-start(f32[1,768]{1,0:T(1,128)} %param.26) | copy-start | bytes 9220
  2.1 4.2 %copy-start.16 = (f32[1,768]{1,0:T(1,128)S(1)}, f32[1,768]{1,0:T(1,128)}, u32[]{:S(2)}) copy-start(f32[1,768]{1,0:T(1,128)} %param.28) | copy-start | bytes 9220
  2.1 4.2 %copy-start.17 = (f32[1,768]{1,0:T(1,128)S(1)}, f32[1,768]{1,0:T(1,128)}, u32[]{:S(2)}) copy-start(f32[1,768]{1,0:T(1,128)} %param.29) | copy-start | bytes 9220
  2.1 4.2 %copy-start.18 = (f32[1,768]{1,0:T(1,128)S(1)}, f32[1,768]{1,0:T(1,128)}, u32[]{:S(2)}) copy-start(f32[1,768]{1,0:T(1,128)} %param.30) | copy-start | bytes 9220
  2.1 4.2 %copy-start.19 = (f32[1,768]{1,0:T(1,128)S(1)}, f32[1,768]{1,0:T(1,128)}, u32[]{:S(2)}) copy-start(f32[1,768]{1,0:T(1,128)} %param.34) | copy-start | bytes 9220
  35.1 31.8 %copy-start.11 = (s32[2,512]{1,0:T(2,128)S(1)}, s32[2,512]{1,0:T(2,128)}, u32[]{:S(2)}) copy-start(s32[2,512]{1,0:T(2,128)} %param.19) | copy-start | bytes 12292
  35.1 33.4 %collective-permute-start = (bf16[512,768]{1,0:T(8,128)(2,1)}, bf16[512,768]{1,0:T(8,128)(2,1)}, u32[]{:S(2)}, u32[]{:S(2)}) collective-permute-start(bf16[512,768]{1,0:T(8,128)(2,1)} %get-tuple-element.105.rest_8_), channel_id=1, source_target_pairs={{0,16},{1,17},{2,18},{3,19},{4,20},{5,21},{6,22},{7,23},{8,24},{9,... | collective-permute-start | bytes 2359304 | tf_op jit(solution)/shard_map/ppermute | solution.py:349
  65.5 19.3 %collective-permute-start.1 = (bf16[512,768]{1,0:T(8,128)(2,1)}, bf16[512,768]{1,0:T(8,128)(2,1)S(1)}, u32[]{:S(2)}, u32[]{:S(2)}) collective-permute-start(bf16[512,768]{1,0:T(8,128)(2,1)} %get-tuple-element.115.rest_8_), channel_id=1, source_target_pairs={{0,16},{1,17},{2,18},{3,19},{4,20},{5,21},{6,22},{7,23},{8,24},{9,... | collective-permute-start | bytes 2359304 | tf_op jit(solution)/shard_map/ppermute | solution.py:349
  79.2 58.7 %collective-permute-start.2 = (bf16[512,768]{1,0:T(8,128)(2,1)}, bf16[512,768]{1,0:T(8,128)(2,1)S(1)}, u32[]{:S(2)}, u32[]{:S(2)}) collective-permute-start(bf16[512,768]{1,0:T(8,128)(2,1)} %get-tuple-element.130.rest_1_), channel_id=1, source_target_pairs={{16,0},{17,1},{18,2},{19,3},{20,4},{21,5},{22,6},{23,7},{24,8},{25... | collective-permute-start | bytes 2359304 | tf_op jit(solution)/shard_map/ppermute | solution.py:349
  84.9 0.9 copy-start.20
  96.1 105.4 %collective-permute-start.3 = (bf16[512,768]{1,0:T(8,128)(2,1)}, bf16[512,768]{1,0:T(8,128)(2,1)S(1)}, u32[]{:S(2)}, u32[]{:S(2)}) collective-permute-start(bf16[512,768]{1,0:T(8,128)(2,1)} %get-tuple-element.147.rest_1_), channel_id=1, source_target_pairs={{16,0},{17,1},{18,2},{19,3},{20,4},{21,5},{22,6},{23,7},{24,8},{25... | collective-permute-start | bytes 2359304 | tf_op jit(solution)/shard_map/ppermute | solution.py:349
  137.8 0.9 copy-start.5
  201.5 0.9 copy-start.6
  213.5 12.9 %collective-permute-start.4 = (bf16[8,192,768]{2,1,0:T(8,128)(2,1)}, bf16[8,192,768]{2,1,0:T(8,128)(2,1)}, u32[]{:S(2)}, u32[]{:S(2)}) collective-permute-start(bf16[8,192,768]{2,1,0:T(8,128)(2,1)} %get-tuple-element.151), channel_id=1, source_target_pairs={{0,1},{1,0},{2,3},{3,2},{4,5},{5,4},{6,7},{7,6},{8,9},{9,8},{10,11... | collective-permute-start | bytes 7077896 | tf_op jit(solution)/shard_map/ppermute | solution.py:440
  243.4 5.8 %collective-permute-start.5 = (bf16[8,240,768]{2,1,0:T(8,128)(2,1)}, bf16[8,240,768]{2,1,0:T(8,128)(2,1)S(1)}, u32[]{:S(2)}, u32[]{:S(2)}) collective-permute-start(bf16[8,240,768]{2,1,0:T(8,128)(2,1)} %get-tuple-element.166), channel_id=1, source_target_pairs={{0,1},{1,0},{2,3},{3,2},{4,5},{5,4},{6,7},{7,6},{8,9},{9,8},{10,11... | collective-permute-start | bytes 8847368 | tf_op jit(solution)/shard_map/ppermute | solution.py:440
  243.9 46.5 %collective-permute-start.14 = (bf16[4,192,768]{2,1,0:T(8,128)(2,1)}, bf16[4,192,768]{2,1,0:T(8,128)(2,1)}, u32[]{:S(2)}, u32[]{:S(2)}) collective-permute-start(bf16[4,192,768]{2,1,0:T(8,128)(2,1)} %get-tuple-element.181), channel_id=1, source_target_pairs={{0,2},{1,3},{2,0},{3,1},{4,6},{5,7},{6,4},{7,5},{8,10},{9,11},{10,... | collective-permute-start | bytes 3538952 | tf_op jit(solution)/shard_map/ppermute | solution.py:440
  277.0 13.5 %copy-start = (bf16[4,192,768]{2,1,0:T(8,128)(2,1)S(1)}, bf16[4,192,768]{2,1,0:T(8,128)(2,1)}, u32[]{:S(2)}) copy-start(bf16[4,192,768]{2,1,0:T(8,128)(2,1)} %get-tuple-element.180) | copy-start | bytes 3538948
  277.0 11.4 %collective-permute-start.6 = (bf16[272,768]{1,0:T(8,128)(2,1)}, bf16[272,768]{1,0:T(8,128)(2,1)S(1)}, u32[]{:S(2)}, u32[]{:S(2)}) collective-permute-start(bf16[272,768]{1,0:T(8,128)(2,1)} %get-tuple-element.179), channel_id=1, source_target_pairs={{0,16},{1,17},{2,18},{3,19},{4,20},{5,21},{6,22},{7,23},{8,24},{9,... | collective-permute-start | bytes 1253384 | tf_op jit(solution)/shard_map/ppermute | solution.py:349
  289.6 0.8 copy-start.1
  290.4 4.2 %collective-permute-start.7 = (bf16[192,768]{1,0:T(8,128)(2,1)S(1)}, bf16[192,768]{1,0:T(8,128)(2,1)S(1)}, u32[]{:S(2)}, u32[]{:S(2)}) collective-permute-start(bf16[192,768]{1,0:T(8,128)(2,1)S(1)} %dynamic-slice_bitcast_fusion), channel_id=1, source_target_pairs={{0,1},{1,0},{2,3},{3,2},{4,5},{5,4},{6,7},{7,6},{8,9},{9,8},{10,11... | collective-permute-start | bytes 884744 | tf_op jit(solution)/shard_map/ppermute | solution.py:440
  290.5 4.1 %copy-start.2 = (bf16[384,768]{1,0:T(8,128)(2,1)S(1)}, bf16[384,768]{1,0:T(8,128)(2,1)}, u32[]{:S(2)}) copy-start(bf16[384,768]{1,0:T(8,128)(2,1)} %copy-done.1) | copy-start | bytes 1769476
  294.7 10.9 %collective-permute-start.8 = (bf16[96,768]{1,0:T(8,128)(2,1)S(1)}, bf16[96,768]{1,0:T(8,128)(2,1)}, u32[]{:S(2)}, u32[]{:S(2)}) collective-permute-start(bf16[96,768]{1,0:T(8,128)(2,1)S(1)} %dynamic-slice_bitcast_fusion.1), channel_id=1, source_target_pairs={{0,2},{1,3},{2,0},{3,1},{4,6},{5,7},{6,4},{7,5},{8,10},{9,11},{10,... | collective-permute-start | bytes 442376 | tf_op jit(solution)/shard_map/ppermute | solution.py:440
  305.3 38.6 %copy-start.3 = (bf16[2,192,768]{2,1,0:T(8,128)(2,1)S(1)}, bf16[2,192,768]{2,1,0:T(8,128)(2,1)}, u32[]{:S(2)}) copy-start(bf16[2,192,768]{2,1,0:T(8,128)(2,1)} %fusion.8) | copy-start | bytes 1769476
  305.3 45.4 %collective-permute-start.15 = (bf16[8,144,768]{2,1,0:T(8,128)(2,1)}, bf16[8,144,768]{2,1,0:T(8,128)(2,1)}, u32[]{:S(2)}, u32[]{:S(2)}) collective-permute-start(bf16[8,144,768]{2,1,0:T(8,128)(2,1)} %get-tuple-element.188), channel_id=1, source_target_pairs={{0,1},{1,0},{2,3},{3,2},{4,5},{5,4},{6,7},{7,6},{8,9},{9,8},{10,11... | collective-permute-start | bytes 5308424 | tf_op jit(solution)/shard_map/ppermute | solution.py:440
  306.6 4.6 %collective-permute-start.9 = (bf16[48,768]{1,0:T(8,128)(2,1)S(1)}, bf16[48,768]{1,0:T(8,128)(2,1)S(1)}, u32[]{:S(2)}, u32[]{:S(2)}) collective-permute-start(bf16[48,768]{1,0:T(8,128)(2,1)S(1)} %dynamic-slice_bitcast_fusion.2), channel_id=1, source_target_pairs={{0,4},{1,5},{2,6},{3,7},{4,0},{5,1},{6,2},{7,3},{8,12},{9,13},{10,... | collective-permute-start | bytes 221192 | tf_op jit(solution)/shard_map/ppermute | solution.py:440
  308.2 19.8 %collective-permute-start.22 = (bf16[2,192,768]{2,1,0:T(8,128)(2,1)}, bf16[2,192,768]{2,1,0:T(8,128)(2,1)S(1)}, u32[]{:S(2)}, u32[]{:S(2)}) collective-permute-start(bf16[2,192,768]{2,1,0:T(8,128)(2,1)} %fusion.9), channel_id=1, source_target_pairs={{0,4},{1,5},{2,6},{3,7},{4,0},{5,1},{6,2},{7,3},{8,12},{9,13},{10,... | collective-permute-start | bytes 1769480 | tf_op jit(solution)/shard_map/ppermute | solution.py:440
  311.2 13.3 %collective-permute-start.10 = (bf16[48,768]{1,0:T(8,128)(2,1)S(1)}, bf16[48,768]{1,0:T(8,128)(2,1)S(1)}, u32[]{:S(2)}, u32[]{:S(2)}) collective-permute-start(bf16[48,768]{1,0:T(8,128)(2,1)S(1)} %fusion.16), channel_id=1, source_target_pairs={{0,8},{1,9},{2,10},{3,11},{4,12},{5,13},{6,14},{7,15},{8,0},{9,1},... | collective-permute-start | bytes 221192 | tf_op jit(solution)/shard_map/ppermute | solution.py:440
  313.9 39.3 %collective-permute-start.19 = (bf16[4,240,768]{2,1,0:T(8,128)(2,1)}, bf16[4,240,768]{2,1,0:T(8,128)(2,1)}, u32[]{:S(2)}, u32[]{:S(2)}) collective-permute-start(bf16[4,240,768]{2,1,0:T(8,128)(2,1)} %get-tuple-element.190), channel_id=1, source_target_pairs={{0,2},{1,3},{2,0},{3,1},{4,6},{5,7},{6,4},{7,5},{8,10},{9,11},{10,... | collective-permute-start | bytes 4423688 | tf_op jit(solution)/shard_map/ppermute | solution.py:440
  324.5 6.2 %collective-permute-start.11 = (bf16[48,768]{1,0:T(8,128)(2,1)S(1)}, bf16[48,768]{1,0:T(8,128)(2,1)S(1)}, u32[]{:S(2)}, u32[]{:S(2)}) collective-permute-start(bf16[48,768]{1,0:T(8,128)(2,1)S(1)} %add_convert_fusion.14), channel_id=1, source_target_pairs={{0,4},{1,5},{2,6},{3,7},{4,0},{5,1},{6,2},{7,3},{8,12},{9,13},{10,... | collective-permute-start | bytes 221192 | tf_op jit(solution)/shard_map/ppermute | solution.py:440
  329.1 21.7 %copy-start.4 = (bf16[8,144,768]{2,1,0:T(8,128)(2,1)S(1)}, bf16[8,144,768]{2,1,0:T(8,128)(2,1)}, u32[]{:S(2)}) copy-start(bf16[8,144,768]{2,1,0:T(8,128)(2,1)} %get-tuple-element.187) | copy-start | bytes 5308420
  329.1 14.8 %collective-permute-start.23 = (bf16[1,192,768]{2,1,0:T(8,128)(2,1)S(1)}, bf16[1,192,768]{2,1,0:T(8,128)(2,1)S(1)}, u32[]{:S(2)}, u32[]{:S(2)}) collective-permute-start(bf16[1,192,768]{2,1,0:T(8,128)(2,1)S(1)} %add_convert_fusion.12), channel_id=1, source_target_pairs={{0,8},{1,9},{2,10},{3,11},{4,12},{5,13},{6,14},{7,15},{8,0},{9,1},... | collective-permute-start | bytes 884744 | tf_op jit(solution)/shard_map/ppermute | solution.py:440
  330.8 19.8 %collective-permute-start.12 = (bf16[96,768]{1,0:T(8,128)(2,1)S(1)}, bf16[96,768]{1,0:T(8,128)(2,1)S(1)}, u32[]{:S(2)}, u32[]{:S(2)}) collective-permute-start(bf16[96,768]{1,0:T(8,128)(2,1)S(1)} %pad_maximum_fusion.3), channel_id=1, source_target_pairs={{0,2},{1,3},{2,0},{3,1},{4,6},{5,7},{6,4},{7,5},{8,10},{9,11},{10,... | collective-permute-start | bytes 442376 | tf_op jit(solution)/shard_map/ppermute | solution.py:440
  350.7 8.0 %collective-permute-start.13 = (bf16[192,768]{1,0:T(8,128)(2,1)S(1)}, bf16[192,768]{1,0:T(8,128)(2,1)S(1)}, u32[]{:S(2)}, u32[]{:S(2)}) collective-permute-start(bf16[192,768]{1,0:T(8,128)(2,1)S(1)} %pad_maximum_fusion.2), channel_id=1, source_target_pairs={{0,1},{1,0},{2,3},{3,2},{4,5},{5,4},{6,7},{7,6},{8,9},{9,8},{10,11... | collective-permute-start | bytes 884744 | tf_op jit(solution)/shard_map/ppermute | solution.py:440
  352.7 22.1 %collective-permute-start.16 = (bf16[4,144,768]{2,1,0:T(8,128)(2,1)S(1)}, bf16[4,144,768]{2,1,0:T(8,128)(2,1)S(1)}, u32[]{:S(2)}, u32[]{:S(2)}) collective-permute-start(bf16[4,144,768]{2,1,0:T(8,128)(2,1)S(1)} %get-tuple-element.198), channel_id=1, source_target_pairs={{0,2},{1,3},{2,0},{3,1},{4,6},{5,7},{6,4},{7,5},{8,10},{9,11},{10,... | collective-permute-start | bytes 2654216 | tf_op jit(solution)/shard_map/ppermute | solution.py:440
  353.2 3.5 copy-start.7
  353.2 3.5 copy-start.8
  353.2 3.5 copy-start.9
  353.2 3.5 copy-start.10
  355.1 21.5 %collective-permute-start.20 = (bf16[2,240,768]{2,1,0:T(8,128)(2,1)S(1)}, bf16[2,240,768]{2,1,0:T(8,128)(2,1)S(1)}, u32[]{:S(2)}, u32[]{:S(2)}) collective-permute-start(bf16[2,240,768]{2,1,0:T(8,128)(2,1)S(1)} %get-tuple-element.200), channel_id=1, source_target_pairs={{0,4},{1,5},{2,6},{3,7},{4,0},{5,1},{6,2},{7,3},{8,12},{9,13},{10,... | collective-permute-start | bytes 2211848 | tf_op jit(solution)/shard_map/ppermute | solution.py:440
  375.0 18.8 %collective-permute-start.17 = (bf16[2,144,768]{2,1,0:T(8,128)(2,1)S(1)}, bf16[2,144,768]{2,1,0:T(8,128)(2,1)S(1)}, u32[]{:S(2)}, u32[]{:S(2)}) collective-permute-start(bf16[2,144,768]{2,1,0:T(8,128)(2,1)S(1)} %get-tuple-element.202), channel_id=1, source_target_pairs={{0,4},{1,5},{2,6},{3,7},{4,0},{5,1},{6,2},{7,3},{8,12},{9,13},{10,... | collective-permute-start | bytes 1327112 | tf_op jit(solution)/shard_map/ppermute | solution.py:440
  376.7 18.7 %collective-permute-start.21 = (bf16[1,240,768]{2,1,0:T(8,128)(2,1)S(1)}, bf16[1,240,768]{2,1,0:T(8,128)(2,1)S(1)}, u32[]{:S(2)}, u32[]{:S(2)}) collective-permute-start(bf16[1,240,768]{2,1,0:T(8,128)(2,1)S(1)} %fusion.6), channel_id=1, source_target_pairs={{0,8},{1,9},{2,10},{3,11},{4,12},{5,13},{6,14},{7,15},{8,0},{9,1},... | collective-permute-start | bytes 1105928 | tf_op jit(solution)/shard_map/ppermute | solution.py:440
  393.8 11.4 %collective-permute-start.18 = (bf16[1,144,768]{2,1,0:T(8,128)(2,1)S(1)}, bf16[1,144,768]{2,1,0:T(8,128)(2,1)S(1)}, u32[]{:S(2)}, u32[]{:S(2)}) collective-permute-start(bf16[1,144,768]{2,1,0:T(8,128)(2,1)S(1)} %fusion.12), channel_id=1, source_target_pairs={{0,8},{1,9},{2,10},{3,11},{4,12},{5,13},{6,14},{7,15},{8,0},{9,1},... | collective-permute-start | bytes 663560 | tf_op jit(solution)/shard_map/ppermute | solution.py:440
